TPU v7x, 128 devices: a whole 4x4x4 slice. The times are simulated.
128 devices in a mesh: dp: 2 (over y_lo), expert: 64 (over x, z, y_hi, core).
Axes of the slice: x: 4, y: 4 (y_hi: 2, y_lo: 2; y = y_hi * 2 + y_lo), z: 4, core: 2. Of those that a mesh axis runs over, the one named last changes fastest.
Arguments:
- tokens: bfloat16 [2, 2048, 3584], P(None, ('dp', 'expert')), may hold values from -6 to 6
- out_grad: bfloat16 [2, 2048, 3584], P(None, ('dp', 'expert')), may hold values from -6 to 6
- expert_ids: int32 [2, 2048, 4], P(None, ('dp', 'expert')), may hold values from 0 to 31, all different within a row
- route_probs: float32 [2, 2048, 4], P(None, ('dp', 'expert')), may hold values from 0.1 to 0.6
- copy_marks: int32 [2, 32], replicated, may hold values from 0 to 1, as said below
- w_gate: bfloat16 [3584, 32768], P(None, 'expert'), may hold values from -0.09375 to 0.09375
- w_up: bfloat16 [3584, 32768], P(None, 'expert'), may hold values from -0.09375 to 0.09375
- w_down: bfloat16 [3584, 32768], P(None, 'expert'), may hold values from -0.1875 to 0.1875
Outputs:
- moe_out: bfloat16 [2, 2048, 3584], P(None, ('dp', 'expert'))
- input_grad: bfloat16 [2, 2048, 3584], P(None, ('dp', 'expert'))
- grad_gate: float32 [3584, 32768], P('dp', 'expert')
- grad_up: float32 [3584, 32768], P('dp', 'expert')
- grad_down: float32 [3584, 32768], P('dp', 'expert')
Inputs may be any that keep to these rules, and one draw needn't show every extreme that they name: `copy_marks`: each row has exactly 16 ones.
All inputs are finite; a program needn't handle non-finite values.
Results may differ from a plain program's by a relative error of at most 0.0064.
Values may be sent and summed in bfloat16 or wider, within the bound.
No kernel may reach another device: no remote copies, remote signals or barrier semaphores. Data moves between devices by JAX's collectives and lax.ppermute only.
A program may use at most 128 MiB of HBM per device.

v0:
```python
import jax
import jax.numpy as jnp
from jax import lax
from jax.sharding import PartitionSpec as P

SPLIT = 2


def slot_table(expert_ids, marks, half, experts, capacity):
    tok_rows, topk = expert_ids.shape
    flat = expert_ids.reshape(tok_rows * topk)
    labels = jnp.arange(experts, dtype=jnp.int32)
    onehot = (flat[:, None] == labels[None, :]).astype(jnp.int32)
    earlier = jnp.cumsum(onehot, axis=0) - onehot
    ranked = jnp.sum(earlier * onehot, axis=1)
    marked = jnp.sum(onehot * marks[None, :], axis=1)
    at_home = ranked < capacity
    spilled = (marked > 0) & (ranked >= capacity) & (ranked < 2 * capacity)
    target = jnp.where(at_home, half, 1 - half)
    within = jnp.where(at_home, ranked, ranked - capacity)
    placed = jnp.where(at_home | spilled, (target * experts + flat) * capacity + within, -1)
    places = 2 * experts * capacity
    table = jnp.arange(places, dtype=jnp.int32)[:, None] == placed[None, :]
    return table.reshape(places, tok_rows, topk)


def pack_rows(table, tokens_now, probs_now, cot_now, n_dp, n_ep, experts, capacity):
    places, tok_rows, topk = table.shape
    width = tokens_now.shape[1]
    picked = jnp.sum(table.astype(jnp.int32), axis=2).astype(jnp.bfloat16)
    moved = jnp.dot(picked, tokens_now, preferred_element_type=jnp.float32).astype(jnp.bfloat16)
    scaled = (probs_now[:, :, None] * cot_now[:, None, :].astype(jnp.float32)).astype(jnp.bfloat16)
    spread = jnp.dot(
        table.astype(jnp.bfloat16).reshape(places, tok_rows * topk),
        scaled.reshape(tok_rows * topk, width),
        preferred_element_type=jnp.float32,
    ).astype(jnp.bfloat16)

    def widen(block):
        shaped = block.reshape(n_dp, experts, 1, capacity, width)
        wide = jnp.broadcast_to(shaped, (n_dp, experts, n_ep // experts, capacity, width))
        return wide.reshape(n_dp * n_ep, capacity, width)

    return (widen(moved), widen(spread))


def unpack_rows(table, probs_now, back_out, back_dx, n_dp, experts, capacity):
    places = table.shape[0]
    width = back_out.shape[2]

    def fold(block):
        shaped = block.reshape(n_dp, experts, -1, capacity, width).astype(jnp.float32)
        return jnp.sum(shaped, axis=2).reshape(places, width)

    table_f = table.astype(jnp.float32)
    mixing = jnp.einsum("ptk,tk->pt", table_f, probs_now, precision=lax.Precision.HIGHEST)
    picked = jnp.sum(table_f, axis=2)
    rows_first = (((0,), (0,)), ((), ()))
    moe = lax.dot_general(
        mixing,
        fold(back_out),
        rows_first,
        precision=lax.Precision.HIGHEST,
        preferred_element_type=jnp.float32,
    )
    grad_in = lax.dot_general(
        picked,
        fold(back_dx),
        rows_first,
        precision=lax.Precision.HIGHEST,
        preferred_element_type=jnp.float32,
    )
    return (moe.astype(jnp.bfloat16), grad_in.astype(jnp.bfloat16))


def expert_pass(rows_in, scaled, w_gate, w_up, w_down):
    contract = (((1,), (1,)), ((), ()))
    rows_first = (((0,), (0,)), ((), ()))
    gate_pre = jnp.dot(rows_in, w_gate, preferred_element_type=jnp.float32)
    up_pre = jnp.dot(rows_in, w_up, preferred_element_type=jnp.float32)
    squash = jax.nn.sigmoid(gate_pre)
    active = gate_pre * squash
    hidden = (active * up_pre).astype(jnp.bfloat16)
    part_out = lax.dot_general(hidden, w_down, contract, preferred_element_type=jnp.float32).astype(
        jnp.bfloat16
    )
    down_term = lax.dot_general(scaled, hidden, rows_first, preferred_element_type=jnp.float32)
    hidden_grad = jnp.dot(scaled, w_down, preferred_element_type=jnp.float32)
    gate_grad = (hidden_grad * up_pre * squash * (1.0 + gate_pre * (1.0 - squash))).astype(
        jnp.bfloat16
    )
    up_grad = (hidden_grad * active).astype(jnp.bfloat16)
    gate_term = lax.dot_general(rows_in, gate_grad, rows_first, preferred_element_type=jnp.float32)
    up_term = lax.dot_general(rows_in, up_grad, rows_first, preferred_element_type=jnp.float32)
    part_dx = lax.dot_general(gate_grad, w_gate, contract, preferred_element_type=jnp.float32)
    part_dx = (
        part_dx + lax.dot_general(up_grad, w_up, contract, preferred_element_type=jnp.float32)
    ).astype(jnp.bfloat16)
    return (part_out, part_dx, gate_term, up_term, down_term)


def send_out(moved, spread):
    return (
        lax.all_to_all(moved, ("dp", "expert"), split_axis=0, concat_axis=0, tiled=True),
        lax.all_to_all(spread, ("dp", "expert"), split_axis=0, concat_axis=0, tiled=True),
    )


def send_back(part_out, part_dx):
    return (
        lax.all_to_all(part_out, ("dp", "expert"), split_axis=0, concat_axis=0, tiled=True),
        lax.all_to_all(part_dx, ("dp", "expert"), split_axis=0, concat_axis=0, tiled=True),
    )


def local(tokens, out_grad, expert_ids, route_probs, copy_marks, w_gate, w_up, w_down):
    n_dp = lax.axis_size("dp")
    n_ep = lax.axis_size("expert")
    experts = n_ep // SPLIT
    tok_rows, topk = (expert_ids.shape[1], expert_ids.shape[2])
    width = tokens.shape[2]
    capacity = max(1, tok_rows * topk // experts)
    devices = n_dp * n_ep
    half = lax.axis_index("dp")
    tables = [
        slot_table(expert_ids[micro], copy_marks[micro], half, experts, capacity)
        for micro in range(2)
    ]
    packed = [
        pack_rows(
            tables[micro],
            tokens[micro],
            route_probs[micro],
            out_grad[micro],
            n_dp,
            n_ep,
            experts,
            capacity,
        )
        for micro in range(2)
    ]
    returned = []
    gate_sum = None
    for micro in range(2):
        got_in, got_cot = send_out(packed[micro][0], packed[micro][1])
        part_out, part_dx, gate_term, up_term, down_term = expert_pass(
            got_in.reshape(-1, width), got_cot.reshape(-1, width), w_gate, w_up, w_down
        )
        if gate_sum is None:
            gate_sum, up_sum, down_sum = (gate_term, up_term, down_term)
        else:
            gate_sum = gate_sum + gate_term
            up_sum = up_sum + up_term
            down_sum = down_sum + down_term
        returned.append(
            send_back(
                part_out.reshape(devices, capacity, width),
                part_dx.reshape(devices, capacity, width),
            )
        )
    outputs = []
    grads_in = []
    for micro in range(2):
        moe, grad_in = unpack_rows(
            tables[micro],
            route_probs[micro],
            returned[micro][0],
            returned[micro][1],
            n_dp,
            experts,
            capacity,
        )
        outputs.append(moe)
        grads_in.append(grad_in)
    gate_shard, up_shard, down_shard = (
        lax.psum_scatter(gate_sum, "dp", scatter_dimension=0, tiled=True),
        lax.psum_scatter(up_sum, "dp", scatter_dimension=0, tiled=True),
        lax.psum_scatter(down_sum, "dp", scatter_dimension=0, tiled=True),
    )
    return (jnp.stack(outputs), jnp.stack(grads_in), gate_shard, up_shard, down_shard)


def solution(mesh):
    return jax.shard_map(
        local,
        mesh=mesh,
        in_specs=(
            P(None, ("dp", "expert"), None),
            P(None, ("dp", "expert"), None),
            P(None, ("dp", "expert"), None),
            P(None, ("dp", "expert"), None),
            P(),
            P(None, "expert"),
            P(None, "expert"),
            P(None, "expert"),
        ),
        out_specs=(
            P(None, ("dp", "expert"), None),
            P(None, ("dp", "expert"), None),
            P("dp", "expert"),
            P("dp", "expert"),
            P("dp", "expert"),
        ),
        check_vma=False,
    )
```

profile of v0, /device:TPU:1, one launch (start us, length us, event | category | flops | bytes accessed | tf_op | source)
XLA Modules:
  0.0 523.9 jit_solution(5706552002119291410)
XLA Ops:
  13.9 11.5 %all-to-all-start.2 = ((bf16[128,2,3584]{2,1,0:T(2,128)(2,1)}), bf16[128,2,3584]{2,1,0:T(2,128)(2,1)S(1)}, u32[]{:S(2)}, u32[]{:S(2)}) async-start(bf16[128,2,3584]{2,1,0:T(2,128)(2,1)} %bitcast.113), calls=%async_computation.2 | async-start | bytes 3670016 | tf_op jit(solution)/shard_map/all_to_all | solution.py:104
  27.5 25.2 %all-to-all-done.2 = bf16[128,2,3584]{2,1,0:T(2,128)(2,1)S(1)} async-done(((bf16[128,2,3584]{2,1,0:T(2,128)(2,1)}), bf16[128,2,3584]{2,1,0:T(2,128)(2,1)S(1)}, u32[]{:S(2)}, u32[]{:S(2)}) %all-to-all-start.2) | async-done | bytes 1835040 | tf_op jit(solution)/shard_map/all_to_all | solution.py:104
  56.8 5.3 %all-to-all-start = ((bf16[128,2,3584]{2,1,0:T(2,128)(2,1)}), bf16[128,2,3584]{2,1,0:T(2,128)(2,1)}, u32[]{:S(2)}, u32[]{:S(2)}) async-start(bf16[128,2,3584]{2,1,0:T(2,128)(2,1)} %bitcast.112), calls=%async_computation | async-start | bytes 3670016 | tf_op jit(solution)/shard_map/all_to_all | solution.py:104
  63.7 25.5 %all-to-all-done = bf16[128,2,3584]{2,1,0:T(2,128)(2,1)} async-done(((bf16[128,2,3584]{2,1,0:T(2,128)(2,1)}), bf16[128,2,3584]{2,1,0:T(2,128)(2,1)}, u32[]{:S(2)}, u32[]{:S(2)}) %all-to-all-start) | async-done | bytes 1835040 | tf_op jit(solution)/shard_map/all_to_all | solution.py:104
  91.4 5.7 %all-to-all-start.4 = ((bf16[128,2,3584]{2,1,0:T(2,128)(2,1)}), bf16[128,2,3584]{2,1,0:T(2,128)(2,1)}, u32[]{:S(2)}, u32[]{:S(2)}) async-start(bf16[128,2,3584]{2,1,0:T(2,128)(2,1)} %bitcast.22), calls=%async_computation.4 | async-start | bytes 3670016 | tf_op jit(solution)/shard_map/all_to_all | solution.py:105
  102.1 5.3 %reshape.337 = bf16[256,3584]{1,0:T(8,128)(2,1)} reshape(bf16[128,2,3584]{2,1,0:T(2,128)(2,1)} %all-to-all-done) | data formatting | bytes 3670016 | tf_op jit(solution)/shard_map/reshape | solution.py:147
  107.5 4.1 fusion.39
  113.5 10.5 %all-to-all-done.4 = bf16[128,2,3584]{2,1,0:T(2,128)(2,1)} async-done(((bf16[128,2,3584]{2,1,0:T(2,128)(2,1)}), bf16[128,2,3584]{2,1,0:T(2,128)(2,1)}, u32[]{:S(2)}, u32[]{:S(2)}) %all-to-all-start.4) | async-done | bytes 1835040 | tf_op jit(solution)/shard_map/all_to_all | solution.py:105
  126.2 5.2 all-to-all-start.6
  131.8 5.1 reshape.345
  145.6 4.1 fusion.44
  149.7 8.9 %all-to-all-done.6 = bf16[128,2,3584]{2,1,0:T(2,128)(2,1)} async-done(((bf16[128,2,3584]{2,1,0:T(2,128)(2,1)}), bf16[128,2,3584]{2,1,0:T(2,128)(2,1)}, u32[]{:S(2)}, u32[]{:S(2)}) %all-to-all-start.6) | async-done | bytes 1835040 | tf_op jit(solution)/shard_map/all_to_all | solution.py:105
  158.6 5.1 reshape.349
  163.6 4.9 multiply_convert_fusion.2
  169.3 4.1 convolution_add_fusion
  177.1 4.7 convolution_add_fusion.1
  181.9 11.5 %reduce-scatter.4.cloned.1.call-start = ((), (), s32[]{:S(2)}) async-start(), calls=%async_computation.11 | async-start | bytes 11010048 | tf_op jit(solution)/shard_map/reduce_scatter | solution.py:176
  196.2 4.1 convolution_add_fusion.2
  210.4 4.8 convolution_convert_fusion.1
  215.2 4.8 reshape.338
  220.0 21.3 %all-to-all-done.3 = bf16[128,2,3584]{2,1,0:T(2,128)(2,1)S(1)} async-done(((bf16[128,2,3584]{2,1,0:T(2,128)(2,1)}), bf16[128,2,3584]{2,1,0:T(2,128)(2,1)S(1)}, u32[]{:S(2)}, u32[]{:S(2)}) %all-to-all-start.3) | async-done | bytes 1835040 | tf_op jit(solution)/shard_map/all_to_all | solution.py:111
  242.6 5.4 %all-to-all-start.1 = ((bf16[128,2,3584]{2,1,0:T(2,128)(2,1)}), bf16[128,2,3584]{2,1,0:T(2,128)(2,1)}, u32[]{:S(2)}, u32[]{:S(2)}) async-start(bf16[128,2,3584]{2,1,0:T(2,128)(2,1)} %reshape.338), calls=%async_computation.1 | async-start | bytes 3670016 | tf_op jit(solution)/shard_map/all_to_all | solution.py:111
  254.3 24.3 %all-to-all-done.1 = bf16[128,2,3584]{2,1,0:T(2,128)(2,1)} async-done(((bf16[128,2,3584]{2,1,0:T(2,128)(2,1)}), bf16[128,2,3584]{2,1,0:T(2,128)(2,1)}, u32[]{:S(2)}, u32[]{:S(2)}) %all-to-all-start.1) | async-done | bytes 1835040 | tf_op jit(solution)/shard_map/all_to_all | solution.py:111
  278.7 5.4 %all-to-all-start.7 = ((bf16[128,2,3584]{2,1,0:T(2,128)(2,1)}), bf16[128,2,3584]{2,1,0:T(2,128)(2,1)}, u32[]{:S(2)}, u32[]{:S(2)}) async-start(bf16[128,2,3584]{2,1,0:T(2,128)(2,1)} %reshape.350), calls=%async_computation.7 | async-start | bytes 3670016 | tf_op jit(solution)/shard_map/all_to_all | solution.py:112
  290.5 24.2 %all-to-all-done.7 = bf16[128,2,3584]{2,1,0:T(2,128)(2,1)} async-done(((bf16[128,2,3584]{2,1,0:T(2,128)(2,1)}), bf16[128,2,3584]{2,1,0:T(2,128)(2,1)}, u32[]{:S(2)}, u32[]{:S(2)}) %all-to-all-start.7) | async-done | bytes 1835040 | tf_op jit(solution)/shard_map/all_to_all | solution.py:112
  314.7 5.4 %all-to-all-start.5 = ((bf16[128,2,3584]{2,1,0:T(2,128)(2,1)}), bf16[128,2,3584]{2,1,0:T(2,128)(2,1)}, u32[]{:S(2)}, u32[]{:S(2)}) async-start(bf16[128,2,3584]{2,1,0:T(2,128)(2,1)} %reshape.346), calls=%async_computation.5 | async-start | bytes 3670016 | tf_op jit(solution)/shard_map/all_to_all | solution.py:112
  328.1 4.6 convert_reduce_fusion.3
  335.2 4.6 convert_reduce_fusion
  342.3 5.0 all-to-all-done.5
  347.2 4.8 convert_reduce_fusion.1
  361.6 60.4 %reduce-scatter.6.cloned.1.call-done = f32[1792,512]{1,0:T(8,128)} async-done(((f32[3584,512]{1,0:T(8,128)}), f32[1792,512]{1,0:T(8,128)}) %reduce-scatter.6.cloned.1.call-update) | async-done | bytes 3670032 | tf_op jit(solution)/shard_map/reduce_scatter | solution.py:177
  422.0 94.9 %reduce-scatter.4.cloned.1.call-done = f32[1792,512]{1,0:T(8,128)} async-done(((f32[3584,512]{1,0:T(8,128)}), f32[1792,512]{1,0:T(8,128)}) %reduce-scatter.4.cloned.1.call-update) | async-done | bytes 3670032 | tf_op jit(solution)/shard_map/reduce_scatter | solution.py:176
  (144 shorter events, 88.5 us)
Async XLA Ops:
  13.9 12.0 %copy-start.23 = (bf16[2,16,3584]{2,1,0:T(8,128)(2,1)S(1)}, bf16[2,16,3584]{2,1,0:T(8,128)(2,1)}, u32[]{:S(2)}) copy-start(bf16[2,16,3584]{2,1,0:T(8,128)(2,1)} %param.8) | copy-start | bytes 688132
  13.9 38.9 %all-to-all-start.2 = ((bf16[128,2,3584]{2,1,0:T(2,128)(2,1)}), bf16[128,2,3584]{2,1,0:T(2,128)(2,1)S(1)}, u32[]{:S(2)}, u32[]{:S(2)}) async-start(bf16[128,2,3584]{2,1,0:T(2,128)(2,1)} %bitcast.113), calls=%async_computation.2 | async-start | bytes 3670016 | tf_op jit(solution)/shard_map/all_to_all | solution.py:104
  52.8 4.0 copy-start.10
  56.8 5.3 %copy-start.24 = (bf16[2,16,3584]{2,1,0:T(8,128)(2,1)S(1)}, bf16[2,16,3584]{2,1,0:T(8,128)(2,1)}, u32[]{:S(2)}) copy-start(bf16[2,16,3584]{2,1,0:T(8,128)(2,1)} %param.9) | copy-start | bytes 688132
  56.8 5.3 %copy-start.25 = (f32[2,16,4]{1,2,0:T(4,128)S(1)}, f32[2,16,4]{1,2,0:T(4,128)}, u32[]{:S(2)}) copy-start(f32[2,16,4]{1,2,0:T(4,128)} %param.11) | copy-start | bytes 1540
  56.8 32.4 %all-to-all-start = ((bf16[128,2,3584]{2,1,0:T(2,128)(2,1)}), bf16[128,2,3584]{2,1,0:T(2,128)(2,1)}, u32[]{:S(2)}, u32[]{:S(2)}) async-start(bf16[128,2,3584]{2,1,0:T(2,128)(2,1)} %bitcast.112), calls=%async_computation | async-start | bytes 3670016 | tf_op jit(solution)/shard_map/all_to_all | solution.py:104
  91.4 32.7 %all-to-all-start.4 = ((bf16[128,2,3584]{2,1,0:T(2,128)(2,1)}), bf16[128,2,3584]{2,1,0:T(2,128)(2,1)}, u32[]{:S(2)}, u32[]{:S(2)}) async-start(bf16[128,2,3584]{2,1,0:T(2,128)(2,1)} %bitcast.22), calls=%async_computation.4 | async-start | bytes 3670016 | tf_op jit(solution)/shard_map/all_to_all | solution.py:105
  102.1 9.4 %copy-start = (bf16[256,3584]{1,0:T(8,128)(2,1)}, bf16[256,3584]{1,0:T(8,128)(2,1)S(1)}, u32[]{:S(2)}) copy-start(bf16[256,3584]{1,0:T(8,128)(2,1)S(1)} %reshape.341) | copy-start | bytes 5505028
  107.5 4.1 copy-start.6
  126.2 32.4 %all-to-all-start.6 = ((bf16[128,2,3584]{2,1,0:T(2,128)(2,1)}), bf16[128,2,3584]{2,1,0:T(2,128)(2,1)}, u32[]{:S(2)}, u32[]{:S(2)}) async-start(bf16[128,2,3584]{2,1,0:T(2,128)(2,1)} %bitcast.27), calls=%async_computation.6 | async-start | bytes 3670016 | tf_op jit(solution)/shard_map/all_to_all | solution.py:105
  131.5 5.5 %copy-start.2 = (bf16[256,3584]{1,0:T(8,128)(2,1)S(1)}, bf16[256,3584]{1,0:T(8,128)(2,1)}, u32[]{:S(2)}) copy-start(bf16[256,3584]{1,0:T(8,128)(2,1)} %reshape.337) | copy-start | bytes 5505028
  131.5 230.2 %reduce-scatter.8.cloned.1.call-start = ((), (), s32[]{:S(2)}) async-start(), calls=%async_computation.13 | async-start | bytes 11010048 | tf_op jit(solution)/shard_map/reduce_scatter | solution.py:178
  136.9 3.3 copy-start.7
  140.2 2.6 copy-start.9
  158.6 10.7 %slice-start = ((s8[7340032]{0:T(1024)(128)(4,1)}), s8[3145728]{0:T(1024)(128)(4,1)S(1)}, s32[]{:S(2)}) async-start(s8[7340032]{0:T(1024)(128)(4,1)} %bitcast.110), calls=%async_computation.14 | async-start | bytes 6291456
  163.6 5.7 %slice-start.1 = ((s8[7340032]{0:T(1024)(128)(4,1)}), s8[4194304]{0:T(1024)(128)(4,1)S(1)}, s32[]{:S(2)}) async-start(s8[7340032]{0:T(1024)(128)(4,1)} %bitcast.110), calls=%async_computation.15 | async-start | bytes 8388608
  163.6 5.7 %copy-start.8 = (bf16[256,3584]{1,0:T(8,128)(2,1)S(1)}, bf16[256,3584]{1,0:T(8,128)(2,1)}, u32[]{:S(2)}) copy-start(bf16[256,3584]{1,0:T(8,128)(2,1)} %reshape.349) | copy-start | bytes 5505028
  173.4 248.6 %reduce-scatter.6.cloned.1.call-start = ((), (), s32[]{:S(2)}) async-start(), calls=%async_computation.12 | async-start | bytes 11010048 | tf_op jit(solution)/shard_map/reduce_scatter | solution.py:177
  174.4 2.8 copy-start.1
  181.8 11.6 %copy-start.22 = (bf16[256,512]{1,0:T(8,128)(2,1)S(1)}, bf16[256,512]{1,0:T(8,128)(2,1)}, u32[]{:S(2)}) copy-start(bf16[256,512]{1,0:T(8,128)(2,1)} %get-tuple-element.10) | copy-start | bytes 786436
  181.9 335.0 %reduce-scatter.4.cloned.1.call-start = ((), (), s32[]{:S(2)}) async-start(), calls=%async_computation.11 | async-start | bytes 11010048 | tf_op jit(solution)/shard_map/reduce_scatter | solution.py:176
  193.4 2.7 copy-start.21
  206.4 4.0 copy-start.20
  206.4 34.9 %all-to-all-start.3 = ((bf16[128,2,3584]{2,1,0:T(2,128)(2,1)}), bf16[128,2,3584]{2,1,0:T(2,128)(2,1)S(1)}, u32[]{:S(2)}, u32[]{:S(2)}) async-start(bf16[128,2,3584]{2,1,0:T(2,128)(2,1)} %reshape.342), calls=%async_computation.3 | async-start | bytes 3670016 | tf_op jit(solution)/shard_map/all_to_all | solution.py:111
  242.6 36.1 %all-to-all-start.1 = ((bf16[128,2,3584]{2,1,0:T(2,128)(2,1)}), bf16[128,2,3584]{2,1,0:T(2,128)(2,1)}, u32[]{:S(2)}, u32[]{:S(2)}) async-start(bf16[128,2,3584]{2,1,0:T(2,128)(2,1)} %reshape.338), calls=%async_computation.1 | async-start | bytes 3670016 | tf_op jit(solution)/shard_map/all_to_all | solution.py:111
  248.0 3.4 copy-start.3
  278.7 36.0 %all-to-all-start.7 = ((bf16[128,2,3584]{2,1,0:T(2,128)(2,1)}), bf16[128,2,3584]{2,1,0:T(2,128)(2,1)}, u32[]{:S(2)}, u32[]{:S(2)}) async-start(bf16[128,2,3584]{2,1,0:T(2,128)(2,1)} %reshape.350), calls=%async_computation.7 | async-start | bytes 3670016 | tf_op jit(solution)/shard_map/all_to_all | solution.py:112
  284.1 3.4 copy-start.4
  290.5 30.4 %copy-start.12 = (bf16[128,2,3584]{2,1,0:T(2,128)(2,1)S(1)}, bf16[128,2,3584]{2,1,0:T(2,128)(2,1)}, u32[]{:S(2)}) copy-start(bf16[128,2,3584]{2,1,0:T(2,128)(2,1)} %copy-done.11) | copy-start | bytes 5505028
  314.7 32.6 %all-to-all-start.5 = ((bf16[128,2,3584]{2,1,0:T(2,128)(2,1)}), bf16[128,2,3584]{2,1,0:T(2,128)(2,1)}, u32[]{:S(2)}, u32[]{:S(2)}) async-start(bf16[128,2,3584]{2,1,0:T(2,128)(2,1)} %reshape.346), calls=%async_computation.5 | async-start | bytes 3670016 | tf_op jit(solution)/shard_map/all_to_all | solution.py:112
  354.6 2.6 copy-start.13
  354.6 3.6 copy-start.14
  (7 other events, 8.6 us)
Sparse Core Ops, SparseCore 0:
  173.6 146.7 reduce-scatter.7
  323.4 98.6 reduce-scatter.5
  425.0 91.8 reduce-scatter.3
where the time goes:
time: 531 us; the launch traced here: 524 us
  waiting for transfers between devices  300 us (56%)
  matrix products  66 us (12%)
  local copies, waits for them, and re-layouts  62.6 us (12%)
  starting transfers between devices  59.8 us (11%)
  other arithmetic  20.4 us (4%)
  between operations  14.7 us (3%)
    reduce_scatter x1, waiting for transfers between devices, local(): lax.psum_scatter(gate_sum, 'dp', scatter_dimension=0, tiled=True)  94.9 us
    reduce_scatter x1, waiting for transfers between devices, local(): lax.psum_scatter(up_sum, 'dp', scatter_dimension=0, tiled=True)  60.4 us
    all_to_all x2, waiting for transfers between devices, send_out(): lax.all_to_all(moved, ('dp', 'expert'), split_axis=0, concat_axis=0, tile...  50.7 us
    all_to_all x2, waiting for transfers between devices, send_back(): lax.all_to_all(part_out, ('dp', 'expert'), split_axis=0, concat_axis=0, t...  45.6 us
    all_to_all x2, waiting for transfers between devices, send_back(): lax.all_to_all(part_dx, ('dp', 'expert'), split_axis=0, concat_axis=0, ti...  29.2 us
    all_to_all x2, waiting for transfers between devices, send_out(): lax.all_to_all(spread, ('dp', 'expert'), split_axis=0, concat_axis=0, til...  19.4 us
    reduce_sum x4, other arithmetic, fold(): return jnp.sum(shaped, axis=2).reshape(places, width)  17.5 us
    all_to_all x2, starting transfers between devices, send_out(): lax.all_to_all(moved, ('dp', 'expert'), split_axis=0, concat_axis=0, tile...  16.8 us
  transfers between devices with their start and end apart: 11, of which 10 were waited for; matrix products, arithmetic and copies ran while one was open for 22% of the time, Pallas kernels for 0%

commit v1 on v0

v1 whole, which is shorter than its diff:
```python
import jax
import jax.numpy as jnp
from jax import lax
from jax.sharding import PartitionSpec as P

SPLIT = 2
AXES = ("dp", "expert")


def near_groups(n_dp, n_ep):
    groups = []
    for side in range(n_dp):
        for core in range(SPLIT):
            groups.append(
                [((e % n_dp) ^ side) * n_ep + SPLIT * e + core for e in range(n_ep // SPLIT)]
            )
    return groups


def exchange(x, groups):
    return lax.all_to_all(
        x, AXES, split_axis=0, concat_axis=0, tiled=True, axis_index_groups=groups
    )


def slot_tables(expert_ids, route_probs, marks, experts, capacity):
    micros, tok_rows, topk = expert_ids.shape
    slots = 2 * capacity
    labels = jnp.arange(experts, dtype=jnp.int32)
    hit = expert_ids[:, :, :, None] == labels
    member = jnp.any(hit, axis=2)
    prob = jnp.sum(jnp.where(hit, route_probs[:, :, :, None], 0.0), axis=2)
    rows = jnp.arange(tok_rows)
    before = (rows[None, :] < rows[:, None])[None, :, :, None] & member[:, None, :, :]
    ranked = jnp.sum(before.astype(jnp.int32), axis=2)
    limit = jnp.where(marks > 0, 2 * capacity, capacity)
    kept = member & (ranked < limit[:, None, :])
    place = jnp.where(kept, ranked, -1)
    place = place.transpose(2, 0, 1)
    prob = prob.transpose(2, 0, 1)
    rank = jnp.arange(slots, dtype=jnp.int32)
    same = jnp.eye(micros, dtype=bool)
    chosen = (place[:, None, None, :, :] == rank[None, None, :, None, None]) & same[
        None, :, None, :, None
    ]
    mixing = jnp.where(chosen, prob[:, None, None, :, :], 0.0)
    places = experts * micros * slots
    return (
        chosen.reshape(places, micros * tok_rows),
        mixing.reshape(places, micros * tok_rows),
    )


CONTRACT = (((1,), (1,)), ((), ()))
ROWS_FIRST = (((0,), (0,)), ((), ()))


def mm(a, b, dims=(((1,), (0,)), ((), ()))):
    return lax.dot_general(a, b, dims, preferred_element_type=jnp.float32)


def local(tokens, out_grad, expert_ids, route_probs, copy_marks, w_gate, w_up, w_down):
    n_dp = lax.axis_size("dp")
    n_ep = lax.axis_size("expert")
    devices = n_dp * n_ep
    experts = n_ep // SPLIT
    micros, tok_rows, width = tokens.shape
    topk = expert_ids.shape[2]
    capacity = max(1, tok_rows * topk // experts)
    group_rows = micros * 2 * capacity
    half_width = width // n_dp
    half = lax.axis_index("dp")
    groups = near_groups(n_dp, n_ep)
    cores = [(i, i ^ 1) for i in range(devices)]
    pairs = [(i, (i + n_ep) % devices) for i in range(devices)]

    def core_swap(x):
        return lax.ppermute(x, AXES, cores)

    def pair_swap(x):
        return lax.ppermute(x, AXES, pairs)

    def mine(x):
        return lax.dynamic_slice_in_dim(x, half * half_width, half_width, 1)

    def theirs(x):
        return lax.dynamic_slice_in_dim(x, (1 - half) * half_width, half_width, 1)

    chosen, mixing = slot_tables(expert_ids, route_probs, copy_marks, experts, capacity)
    picked = chosen.astype(jnp.bfloat16)
    flat_tokens = tokens.reshape(micros * tok_rows, width)
    flat_cot = out_grad.reshape(micros * tok_rows, width)
    moved = mm(picked, flat_tokens).astype(jnp.bfloat16)
    slot_prob = jnp.sum(mixing, axis=1, keepdims=True)
    spread = (slot_prob * mm(picked, flat_cot)).astype(jnp.bfloat16)

    def dispatch(x):
        return exchange(x.reshape(experts, group_rows, width), groups).reshape(-1, width)

    x_own = dispatch(moved)
    c_own = dispatch(spread)
    x_oth = core_swap(x_own)
    xp_own = pair_swap(theirs(x_own))
    xp_oth = core_swap(xp_own)

    def forward(x):
        gate_pre = mm(x, w_gate)
        up_pre = mm(x, w_up)
        squash = jax.nn.sigmoid(gate_pre)
        active = gate_pre * squash
        hidden = (active * up_pre).astype(jnp.bfloat16)
        part_out = mm(hidden, w_down, CONTRACT).astype(jnp.bfloat16)
        return gate_pre, up_pre, squash, active, hidden, part_out

    def backward(c, kept):
        gate_pre, up_pre, squash, active, hidden, _ = kept
        hidden_grad = mm(c, w_down)
        gate_grad = (hidden_grad * up_pre * squash * (1.0 + gate_pre * (1.0 - squash))).astype(
            jnp.bfloat16
        )
        up_grad = (hidden_grad * active).astype(jnp.bfloat16)
        part_dx = (mm(gate_grad, w_gate, CONTRACT) + mm(up_grad, w_up, CONTRACT)).astype(
            jnp.bfloat16
        )
        return gate_grad, up_grad, part_dx

    def send_back(own, oth):
        other = core_swap(oth)
        total = (own.astype(jnp.float32) + other.astype(jnp.float32)).astype(jnp.bfloat16)
        return exchange(total.reshape(experts, group_rows, width), groups).reshape(-1, width)

    own = forward(x_own)
    oth = forward(x_oth)
    back_out = send_back(own[5], oth[5])

    c_oth = core_swap(c_own)
    cp_own = pair_swap(theirs(c_own))
    cp_oth = core_swap(cp_own)
    gg_own, ug_own, dx_own = backward(c_own, own)
    gg_oth, ug_oth, dx_oth = backward(c_oth, oth)
    back_dx = send_back(dx_own, dx_oth)

    def both(a, b):
        return jnp.concatenate([a, b], axis=0)

    x_cols = jnp.concatenate([mine(x_own), mine(x_oth), xp_own, xp_oth], axis=0)
    c_cols = jnp.concatenate([mine(c_own), mine(c_oth), cp_own, cp_oth], axis=0)

    def whole(a, b):
        here = both(a, b)
        return both(here, pair_swap(here))

    hidden = whole(own[4], oth[4])
    gate_grad = whole(gg_own, gg_oth)
    up_grad = whole(ug_own, ug_oth)
    grad_down = mm(c_cols, hidden, ROWS_FIRST)
    grad_gate = mm(x_cols, gate_grad, ROWS_FIRST)
    grad_up = mm(x_cols, up_grad, ROWS_FIRST)

    def piece(x):
        return lax.reduce_precision(x, exponent_bits=8, mantissa_bits=7)

    high = piece(mixing)
    middle = piece(mixing - high)
    low = mixing - high - middle
    split = jnp.concatenate([high, middle, low], axis=1).astype(jnp.bfloat16)
    sums = mm(split, back_out, ROWS_FIRST).reshape(3, micros, tok_rows, width)
    moe = (sums[0] + (sums[1] + sums[2])).astype(jnp.bfloat16)
    grad_in = mm(picked, back_dx, ROWS_FIRST).reshape(micros, tok_rows, width)
    return (moe, grad_in.astype(jnp.bfloat16), grad_gate, grad_up, grad_down)


def solution(mesh):
    tok = P(None, AXES, None)
    return jax.shard_map(
        local,
        mesh=mesh,
        in_specs=(tok, tok, tok, tok, P(), P(None, "expert"), P(None, "expert"), P(None, "expert")),
        out_specs=(tok, tok, P("dp", "expert"), P("dp", "expert"), P("dp", "expert")),
        check_vma=False,
    )
```

time: 531 us -> 204 us (0.38); the launches traced: 524 us -> 203 us
  waiting for transfers between devices: 300 us -> 95.3 us
  local copies, waits for them, and re-layouts: 62.6 us -> 8.6 us
  starting transfers between devices: 59.8 us -> 40.8 us
  matrix products: 66 us -> 50.5 us
  between operations: 14.7 us -> 0.96 us
  other arithmetic: 20.4 us -> 6.67 us
    reduce_scatter x3 -> x0, waiting for transfers between devices: 155 us -> none  [the longest x1 94.9 us: local(): lax.psum_scatter(gate_sum, 'dp', scatter_dimension=0, tiled=True)]
    all_to_all x8 -> x4, waiting for transfers between devices: 145 us -> 73 us  [exchange(): lax.all_to_all(x, AXES, split_axis=0, concat_axis=0, tiled=True, axis_ind...]
    reshape x12 -> x0, local copies, waits for them, and re-layouts: 40.7 us -> none  [the longest x4 11.2 us: fold(): return jnp.sum(shaped, axis=2).reshape(places, width)]
    ppermute x0 -> x11, waiting for transfers between devices: none -> 22.4 us  [the longest x5 22.3 us: pair_swap(): return lax.ppermute(x, AXES, pairs)]
    reduce_sum x9 -> x3, other arithmetic: 18 us -> 1.76 us  [the longest x1 0.83 us: local(): slot_prob = jnp.sum(mixing, axis=1, keepdims=True)]
    dot_general x28 -> x19, matrix products: 66 us -> 50.5 us  [mm(): return lax.dot_general(a, b, dims, preferred_element_type=jnp.float32)]
    all_to_all x8 -> x4, starting transfers between devices: 47.9 us -> 32.7 us  [exchange(): lax.all_to_all(x, AXES, split_axis=0, concat_axis=0, tiled=True, axis_ind...]
    broadcast_in_dim x8 -> x3, local copies, waits for them, and re-layouts: 12.8 us -> 0.32 us  [slot_tables(): mixing = jnp.where(chosen, prob[:, None, None, :, :], 0.0)]
  transfers between devices with their start and end apart: 11 -> 15, of which waited for: 10 -> 7; matrix products, arithmetic and copies ran while one was open for 22% -> 28% of each run, Pallas kernels for 0% -> 0%
where the time goes in v1:
time: 204 us; the launch traced here: 203 us
  waiting for transfers between devices  95.3 us (47%)
  matrix products  50.5 us (25%)
  starting transfers between devices  40.8 us (20%)
  local copies, waits for them, and re-layouts  8.6 us (4%)
  other arithmetic  6.67 us (3%)
    all_to_all x4, waiting for transfers between devices, exchange(): lax.all_to_all(x, AXES, split_axis=0, concat_axis=0, tiled=True, axis_ind...  73 us
    dot_general x19, matrix products, mm(): return lax.dot_general(a, b, dims, preferred_element_type=jnp.float32)  50.5 us
    all_to_all x4, starting transfers between devices, exchange(): lax.all_to_all(x, AXES, split_axis=0, concat_axis=0, tiled=True, axis_ind...  32.7 us
    ppermute x5, waiting for transfers between devices, pair_swap(): return lax.ppermute(x, AXES, pairs)  22.3 us
    dynamic_slice x4, local copies, waits for them, and re-layouts, mine(): return lax.dynamic_slice_in_dim(x, half * half_width, half_width, 1)  6.72 us
    ppermute x6, starting transfers between devices, core_swap(): return lax.ppermute(x, AXES, cores)  5.23 us
  transfers between devices with their start and end apart: 15, of which 7 were waited for; matrix products, arithmetic and copies ran while one was open for 28% of the time, Pallas kernels for 0%

profile of v1, /device:TPU:1, one launch (start us, length us, event | category | flops | bytes accessed | tf_op | source)
XLA Modules:
  0.0 202.8 jit_solution(6586586607935860439)
XLA Ops:
  4.4 1.8 fusion.5
  6.2 11.1 %all-to-all-start = ((bf16[32,8,3584]{2,1,0:T(8,128)(2,1)}), bf16[32,8,3584]{2,1,0:T(8,128)(2,1)S(1)}, u32[]{:S(2)}, u32[]{:S(2)}) async-start(bf16[32,8,3584]{2,1,0:T(8,128)(2,1)} %fusion.5), calls=%async_computation | async-start | bytes 3670016 | tf_op jit(solution)/shard_map/all_to_all | solution.py:21
  17.5 1.8 fusion.6
  19.4 24.2 %all-to-all-done = bf16[32,8,3584]{2,1,0:T(8,128)(2,1)S(1)} async-done(((bf16[32,8,3584]{2,1,0:T(8,128)(2,1)}), bf16[32,8,3584]{2,1,0:T(8,128)(2,1)S(1)}, u32[]{:S(2)}, u32[]{:S(2)}) %all-to-all-start) | async-done | bytes 1835040 | tf_op jit(solution)/shard_map/all_to_all | solution.py:21
  43.6 7.4 %all-to-all-start.2 = ((bf16[32,8,3584]{2,1,0:T(8,128)(2,1)}), bf16[32,8,3584]{2,1,0:T(8,128)(2,1)}, u32[]{:S(2)}, u32[]{:S(2)}) async-start(bf16[32,8,3584]{2,1,0:T(8,128)(2,1)} %fusion.6), calls=%async_computation.2 | async-start | bytes 3670016 | tf_op jit(solution)/shard_map/all_to_all | solution.py:21
  52.4 24.9 %all-to-all-done.2 = bf16[32,8,3584]{2,1,0:T(8,128)(2,1)} async-done(((bf16[32,8,3584]{2,1,0:T(8,128)(2,1)}), bf16[32,8,3584]{2,1,0:T(8,128)(2,1)}, u32[]{:S(2)}, u32[]{:S(2)}) %all-to-all-start.2) | async-done | bytes 1835040 | tf_op jit(solution)/shard_map/all_to_all | solution.py:21
  77.3 1.5 collective-permute-start.2
  79.9 2.5 %constant_dynamic-slice_fusion.2 = (bf16[256,1792]{1,0:T(8,128)(2,1)}, bf16[256,1792]{1,0:T(8,128)(2,1)S(1)}) fusion(bf16[256,3584]{1,0:T(8,128)(2,1)} %bitcast.14, s32[]{:T(128)S(6)} %select_n.36, s32[]{:T(128)S(6)} %select_n.37), kind=kLoop, calls=%fused_computation.87 | loop fusion | bytes 3670024 | tf_op jit(solution)/shard_map/dynamic_slice | solution.py:84
  82.4 1.5 collective-permute-start.8
  87.0 2.8 %multiply_convert_fusion.2 = (bf16[256,512]{1,0:T(8,128)(2,1)S(1)}, bf16[256,512]{1,0:T(8,128)(2,1)S(1)}, bf16[256,512]{1,0:T(8,128)(2,1)S(1)}) fusion(f32[256,512]{1,0:T(8,128)S(1)} %fusion.58, f32[256,512]{1,0:T(8,128)S(1)} %fusion.56, bf16[3584,512]{1,0:T(8,128)(2,1)S(1)} %copy-done.5, bf16[32,8,3584]{2,1,0:T(8,128)(2,1)} %all-to-all-done.2), kind=kOutput, calls=%fused_computation.52 | convolution fusion | flops 941490176 | bytes 7340032 | tf_op jit(solution)/shard_map/dot_general | solution.py:59
  89.8 2.6 %fusion.60 = f32[256,512]{1,0:T(8,128)S(1)} fusion(bf16[256,3584]{1,0:T(8,128)(2,1)} %collective-permute-done, bf16[3584,512]{1,0:T(8,128)(2,1)S(1)} %copy-done.4), kind=kOutput, calls=%fused_computation.103 | convolution fusion | flops 939524096 | bytes 6029312 | tf_op jit(solution)/shard_map/dot_general | solution.py:59
  92.4 2.6 %fusion.61 = f32[256,512]{1,0:T(8,128)S(1)} fusion(bf16[256,3584]{1,0:T(8,128)(2,1)} %collective-permute-done, bf16[3584,512]{1,0:T(8,128)(2,1)S(1)} %copy-done.2), kind=kOutput, calls=%fused_computation.104 | convolution fusion | flops 939524096 | bytes 6029312 | tf_op jit(solution)/shard_map/dot_general | solution.py:59
  95.0 1.3 multiply_convert_fusion
  96.3 1.2 convolution_convert_fusion
  98.2 3.0 %fusion.62 = f32[256,3584]{1,0:T(8,128)} fusion(bf16[256,512]{1,0:T(8,128)(2,1)S(1)} %get-tuple-element.15, bf16[3584,512]{1,0:T(8,128)(2,1)S(1)} %copy-done.4), kind=kOutput, calls=%fused_computation.105 | convolution fusion | flops 939524096 | bytes 7602176 | tf_op jit(solution)/shard_map/dot_general | solution.py:59
  101.9 1.3 collective-permute-start.5
  103.2 18.3 %collective-permute-done.8 = bf16[256,1792]{1,0:T(8,128)(2,1)} collective-permute-done((bf16[256,1792]{1,0:T(8,128)(2,1)S(1)}, bf16[256,1792]{1,0:T(8,128)(2,1)}, u32[]{:S(2)}, u32[]{:S(2)}) %collective-permute-start.8) | collective-permute-done | bytes 917536 | tf_op jit(solution)/shard_map/ppermute | solution.py:81
  122.4 1.1 fusion.63
  123.6 2.5 %fusion.3 = bf16[256,3584]{1,0:T(8,128)(2,1)} fusion(f32[256,3584]{1,0:T(8,128)S(1)} %fusion.63, bf16[256,512]{1,0:T(8,128)(2,1)S(1)} %get-tuple-element.11, bf16[3584,512]{1,0:T(8,128)(2,1)S(1)} %copy-done.2), kind=kOutput, calls=%fused_computation.6 | convolution fusion | flops 941359104 | bytes 9437184 | tf_op jit(solution)/shard_map/dot_general | solution.py:59
  126.9 2.2 %constant_dynamic-slice_fusion.4 = bf16[256,1792]{1,0:T(8,128)(2,1)} fusion(bf16[256,3584]{1,0:T(8,128)(2,1)} %collective-permute-done, s32[]{:T(128)S(6)} %select_n.36), kind=kLoop, calls=%fused_computation.89 | loop fusion | bytes 1835012 | tf_op jit(solution)/shard_map/dynamic_slice | solution.py:84
  130.9 1.5 collective-permute-start.7
  132.3 2.5 %fusion.15 = bf16[32,8,3584]{2,1,0:T(8,128)(2,1)} fusion(bf16[256,3584]{1,0:T(8,128)(2,1)S(1)} %collective-permute-done.1, bf16[256,512]{1,0:T(8,128)(2,1)S(1)} %get-tuple-element.16, bf16[3584,512]{1,0:T(8,128)(2,1)S(1)} %copy-done.5), kind=kOutput, calls=%fused_computation.25 | convolution fusion | flops 944111616 | bytes 7602176 | tf_op jit(solution)/shard_map/dot_general | solution.py:59
  134.9 6.0 %all-to-all-start.1 = ((bf16[32,8,3584]{2,1,0:T(8,128)(2,1)}), bf16[32,8,3584]{2,1,0:T(8,128)(2,1)S(1)}, u32[]{:S(2)}, u32[]{:S(2)}) async-start(bf16[32,8,3584]{2,1,0:T(8,128)(2,1)} %fusion.15), calls=%async_computation.1 | async-start | bytes 3670016 | tf_op jit(solution)/shard_map/all_to_all | solution.py:21
  141.8 6.3 %fusion.20 = f32[1792,512]{1,0:T(8,128)} fusion(bf16[512,512]{1,0:T(8,128)(2,1)} %collective-permute-done.6, bf16[256,512]{1,0:T(8,128)(2,1)} %copy-done.7, bf16[256,512]{1,0:T(8,128)(2,1)S(1)} %get-tuple-element.15, bf16[256,1792]{1,0:T(8,128)(2,1)} %collective-permute-done.5, bf16[256,1792]{1,0:T(8,128)(2,1)} %collective-permute-done.4, ...), kind=kOutput, calls=%fused_computation.30 | convolution fusion | flops 1896873984 | bytes 8388608 | tf_op jit(solution)/shard_map/dot_general | solution.py:59
  148.1 3.3 %collective-permute-done.7 = bf16[512,512]{1,0:T(8,128)(2,1)} collective-permute-done((bf16[512,512]{1,0:T(8,128)(2,1)}, bf16[512,512]{1,0:T(8,128)(2,1)}, u32[]{:S(2)}, u32[]{:S(2)}) %collective-permute-start.7) | collective-permute-done | bytes 524320 | tf_op jit(solution)/shard_map/ppermute | solution.py:81
  151.4 5.5 %fusion.26 = f32[1792,512]{1,0:T(8,128)} fusion(bf16[512,512]{1,0:T(8,128)(2,1)} %collective-permute-done.7, bf16[256,512]{1,0:T(8,128)(2,1)S(1)} %get-tuple-element.11, bf16[256,512]{1,0:T(8,128)(2,1)S(1)} %get-tuple-element.14, bf16[256,1792]{1,0:T(8,128)(2,1)} %collective-permute-done.5, bf16[256,1792]{1,0:T(8,128)(2,1)} %collective-permute-done.4, ...), kind=kOutput, calls=%fused_computation.36 | convolution fusion | flops 1896873984 | bytes 8388608 | tf_op jit(solution)/shard_map/dot_general | solution.py:59
  157.0 4.0 %fusion.16 = bf16[32,8,3584]{2,1,0:T(8,128)(2,1)} fusion(bf16[256,3584]{1,0:T(8,128)(2,1)} %collective-permute-done.3, f32[256,3584]{1,0:T(8,128)S(1)} %copy-done.6, bf16[256,512]{1,0:T(8,128)(2,1)S(1)} %get-tuple-element.14, bf16[3584,512]{1,0:T(8,128)(2,1)S(1)} %copy-done.3), kind=kOutput, calls=%fused_computation.26 | convolution fusion | flops 945029120 | bytes 11272192 | tf_op jit(solution)/shard_map/dot_general | solution.py:59
  161.0 4.9 %all-to-all-done.1 = bf16[32,8,3584]{2,1,0:T(8,128)(2,1)S(1)} async-done(((bf16[32,8,3584]{2,1,0:T(8,128)(2,1)}), bf16[32,8,3584]{2,1,0:T(8,128)(2,1)S(1)}, u32[]{:S(2)}, u32[]{:S(2)}) %all-to-all-start.1) | async-done | bytes 1835040 | tf_op jit(solution)/shard_map/all_to_all | solution.py:21
  165.9 8.1 %all-to-all-start.3 = ((bf16[32,8,3584]{2,1,0:T(8,128)(2,1)}), bf16[32,8,3584]{2,1,0:T(8,128)(2,1)}, u32[]{:S(2)}, u32[]{:S(2)}) async-start(bf16[32,8,3584]{2,1,0:T(8,128)(2,1)} %fusion.16), calls=%async_computation.3 | async-start | bytes 3670016 | tf_op jit(solution)/shard_map/all_to_all | solution.py:21
  174.0 6.1 %fusion.7 = f32[1792,512]{1,0:T(8,128)} fusion(bf16[256,1792]{1,0:T(8,128)(2,1)} %collective-permute-done.9, bf16[256,1792]{1,0:T(8,128)(2,1)} %collective-permute-done.8, bf16[256,1792]{1,0:T(8,128)(2,1)} %constant_dynamic-slice_fusion.1, bf16[256,1792]{1,0:T(8,128)(2,1)} %get-tuple-element.7, bf16[512,512]{1,0:T(8,128)(2,1)} %collective-permute-done.10, ...), kind=kOutput, calls=%fused_computation.15 | convolution fusion | flops 1896873984 | bytes 8388608 | tf_op jit(solution)/shard_map/dot_general | solution.py:59
  181.3 18.9 %all-to-all-done.3 = bf16[32,8,3584]{2,1,0:T(8,128)(2,1)} async-done(((bf16[32,8,3584]{2,1,0:T(8,128)(2,1)}), bf16[32,8,3584]{2,1,0:T(8,128)(2,1)}, u32[]{:S(2)}, u32[]{:S(2)}) %all-to-all-start.3) | async-done | bytes 1835040 | tf_op jit(solution)/shard_map/all_to_all | solution.py:21
  200.2 2.6 %convolution_convert_fusion.3 = bf16[2,16,3584]{2,1,0:T(8,128)(2,1)} fusion(pred[2,16,256]{2,1,0:T(8,128)(4,1)S(1)} %bitcast.76, bf16[32,8,3584]{2,1,0:T(8,128)(2,1)} %all-to-all-done.3), kind=kOutput, calls=%fused_computation.13 | convolution fusion | flops 58834944 | bytes 2072576 | tf_op jit(solution)/shard_map/dot_general | solution.py:59
  (66 shorter events, 16.3 us)
Async XLA Ops:
  0.6 3.8 %copy-start = (bf16[2,16,3584]{2,1,0:T(8,128)(2,1)S(1)}, bf16[2,16,3584]{2,1,0:T(8,128)(2,1)}, u32[]{:S(2)}) copy-start(bf16[2,16,3584]{2,1,0:T(8,128)(2,1)} %param.8) | copy-start | bytes 688132
  0.6 16.9 %copy-start.10 = (bf16[2,16,3584]{2,1,0:T(8,128)(2,1)S(1)}, bf16[2,16,3584]{2,1,0:T(8,128)(2,1)}, u32[]{:S(2)}) copy-start(bf16[2,16,3584]{2,1,0:T(8,128)(2,1)} %param.9) | copy-start | bytes 688132
  6.2 37.4 %all-to-all-start = ((bf16[32,8,3584]{2,1,0:T(8,128)(2,1)}), bf16[32,8,3584]{2,1,0:T(8,128)(2,1)S(1)}, u32[]{:S(2)}, u32[]{:S(2)}) async-start(bf16[32,8,3584]{2,1,0:T(8,128)(2,1)} %fusion.5), calls=%async_computation | async-start | bytes 3670016 | tf_op jit(solution)/shard_map/all_to_all | solution.py:21
  43.6 33.7 %all-to-all-start.2 = ((bf16[32,8,3584]{2,1,0:T(8,128)(2,1)}), bf16[32,8,3584]{2,1,0:T(8,128)(2,1)}, u32[]{:S(2)}, u32[]{:S(2)}) async-start(bf16[32,8,3584]{2,1,0:T(8,128)(2,1)} %fusion.6), calls=%async_computation.2 | async-start | bytes 3670016 | tf_op jit(solution)/shard_map/all_to_all | solution.py:21
  51.6 38.2 %collective-permute-start = (bf16[256,3584]{1,0:T(8,128)(2,1)S(1)}, bf16[256,3584]{1,0:T(8,128)(2,1)}, u32[]{:S(2)}, u32[]{:S(2)}) collective-permute-start(bf16[256,3584]{1,0:T(8,128)(2,1)S(1)} %bitcast.70), channel_id=1, source_target_pairs={{0,1},{1,0},{2,3},{3,2},{4,5},{5,4},{6,7},{7,6},{8,9},{9,8},{10,11... | collective-permute-start | bytes 5505032 | tf_op jit(solution)/shard_map/ppermute | solution.py:78
  77.3 6.6 %copy-start.4 = (bf16[3584,512]{1,0:T(8,128)(2,1)S(1)}, bf16[3584,512]{1,0:T(8,128)(2,1)}, u32[]{:S(2)}) copy-start(bf16[3584,512]{1,0:T(8,128)(2,1)} %param.13) | copy-start | bytes 11010052
  77.3 17.7 %collective-permute-start.2 = (bf16[256,3584]{1,0:T(8,128)(2,1)}, bf16[256,3584]{1,0:T(8,128)(2,1)S(1)}, u32[]{:S(2)}, u32[]{:S(2)}) collective-permute-start(bf16[256,3584]{1,0:T(8,128)(2,1)} %bitcast.14), channel_id=1, source_target_pairs={{0,1},{1,0},{2,3},{3,2},{4,5},{5,4},{6,7},{7,6},{8,9},{9,8},{10,11... | collective-permute-start | bytes 5505032 | tf_op jit(solution)/shard_map/ppermute | solution.py:78
  79.9 22.0 %collective-permute-start.4 = (bf16[256,1792]{1,0:T(8,128)(2,1)S(1)}, bf16[256,1792]{1,0:T(8,128)(2,1)}, u32[]{:S(2)}, u32[]{:S(2)}) collective-permute-start(bf16[256,1792]{1,0:T(8,128)(2,1)S(1)} %get-tuple-element.10), channel_id=1, source_target_pairs={{0,64},{1,65},{2,66},{3,67},{4,68},{5,69},{6,70},{7,71},{8,72},{9,... | collective-permute-start | bytes 2752520 | tf_op jit(solution)/shard_map/ppermute | solution.py:81
  82.4 2.6 %copy-start.2 = (bf16[3584,512]{1,0:T(8,128)(2,1)S(1)}, bf16[3584,512]{1,0:T(8,128)(2,1)}, u32[]{:S(2)}) copy-start(bf16[3584,512]{1,0:T(8,128)(2,1)} %param.14) | copy-start | bytes 11010052
  82.4 39.1 %collective-permute-start.8 = (bf16[256,1792]{1,0:T(8,128)(2,1)S(1)}, bf16[256,1792]{1,0:T(8,128)(2,1)}, u32[]{:S(2)}, u32[]{:S(2)}) collective-permute-start(bf16[256,1792]{1,0:T(8,128)(2,1)S(1)} %get-tuple-element.8), channel_id=1, source_target_pairs={{0,64},{1,65},{2,66},{3,67},{4,68},{5,69},{6,70},{7,71},{8,72},{9,... | collective-permute-start | bytes 2752520 | tf_op jit(solution)/shard_map/ppermute | solution.py:81
  85.0 2.0 %copy-start.5 = (bf16[3584,512]{1,0:T(8,128)(2,1)S(1)}, bf16[3584,512]{1,0:T(8,128)(2,1)}, u32[]{:S(2)}) copy-start(bf16[3584,512]{1,0:T(8,128)(2,1)} %param.15) | copy-start | bytes 11010052
  96.3 29.8 %copy-start.7 = (bf16[256,512]{1,0:T(8,128)(2,1)}, bf16[256,512]{1,0:T(8,128)(2,1)S(1)}, u32[]{:S(2)}) copy-start(bf16[256,512]{1,0:T(8,128)(2,1)S(1)} %get-tuple-element.12) | copy-start | bytes 786436
  97.5 33.3 %collective-permute-start.1 = (bf16[256,3584]{1,0:T(8,128)(2,1)S(1)}, bf16[256,3584]{1,0:T(8,128)(2,1)S(1)}, u32[]{:S(2)}, u32[]{:S(2)}) collective-permute-start(bf16[256,3584]{1,0:T(8,128)(2,1)S(1)} %convolution_convert_fusion), channel_id=1, source_target_pairs={{0,1},{1,0},{2,3},{3,2},{4,5},{5,4},{6,7},{7,6},{8,9},{9,8},{10,11... | collective-permute-start | bytes 5505032 | tf_op jit(solution)/shard_map/ppermute | solution.py:78
  101.9 39.9 %collective-permute-start.5 = (bf16[256,1792]{1,0:T(8,128)(2,1)}, bf16[256,1792]{1,0:T(8,128)(2,1)}, u32[]{:S(2)}, u32[]{:S(2)}) collective-permute-start(bf16[256,1792]{1,0:T(8,128)(2,1)} %collective-permute-done.4), channel_id=1, source_target_pairs={{0,1},{1,0},{2,3},{3,2},{4,5},{5,4},{6,7},{7,6},{8,9},{9,8},{10,11... | collective-permute-start | bytes 2752520 | tf_op jit(solution)/shard_map/ppermute | solution.py:78
  121.6 52.4 %collective-permute-start.9 = (bf16[256,1792]{1,0:T(8,128)(2,1)}, bf16[256,1792]{1,0:T(8,128)(2,1)}, u32[]{:S(2)}, u32[]{:S(2)}) collective-permute-start(bf16[256,1792]{1,0:T(8,128)(2,1)} %collective-permute-done.8), channel_id=1, source_target_pairs={{0,1},{1,0},{2,3},{3,2},{4,5},{5,4},{6,7},{7,6},{8,9},{9,8},{10,11... | collective-permute-start | bytes 2752520 | tf_op jit(solution)/shard_map/ppermute | solution.py:78
  126.1 30.9 %collective-permute-start.3 = (bf16[256,3584]{1,0:T(8,128)(2,1)}, bf16[256,3584]{1,0:T(8,128)(2,1)}, u32[]{:S(2)}, u32[]{:S(2)}) collective-permute-start(bf16[256,3584]{1,0:T(8,128)(2,1)} %fusion.3), channel_id=1, source_target_pairs={{0,1},{1,0},{2,3},{3,2},{4,5},{5,4},{6,7},{7,6},{8,9},{9,8},{10,11... | collective-permute-start | bytes 5505032 | tf_op jit(solution)/shard_map/ppermute | solution.py:78
  126.9 14.9 %collective-permute-start.6 = (bf16[512,512]{1,0:T(8,128)(2,1)}, bf16[512,512]{1,0:T(8,128)(2,1)}, u32[]{:S(2)}, u32[]{:S(2)}) collective-permute-start(bf16[512,512]{1,0:T(8,128)(2,1)} %pad_maximum_fusion.3), channel_id=1, source_target_pairs={{0,64},{1,65},{2,66},{3,67},{4,68},{5,69},{6,70},{7,71},{8,72},{9,... | collective-permute-start | bytes 1572872 | tf_op jit(solution)/shard_map/ppermute | solution.py:81
  130.9 20.5 %collective-permute-start.7 = (bf16[512,512]{1,0:T(8,128)(2,1)}, bf16[512,512]{1,0:T(8,128)(2,1)}, u32[]{:S(2)}, u32[]{:S(2)}) collective-permute-start(bf16[512,512]{1,0:T(8,128)(2,1)} %pad_maximum_fusion.4), channel_id=1, source_target_pairs={{0,64},{1,65},{2,66},{3,67},{4,68},{5,69},{6,70},{7,71},{8,72},{9,... | collective-permute-start | bytes 1572872 | tf_op jit(solution)/shard_map/ppermute | solution.py:81
  134.9 31.0 %all-to-all-start.1 = ((bf16[32,8,3584]{2,1,0:T(8,128)(2,1)}), bf16[32,8,3584]{2,1,0:T(8,128)(2,1)S(1)}, u32[]{:S(2)}, u32[]{:S(2)}) async-start(bf16[32,8,3584]{2,1,0:T(8,128)(2,1)} %fusion.15), calls=%async_computation.1 | async-start | bytes 3670016 | tf_op jit(solution)/shard_map/all_to_all | solution.py:21
  141.8 32.2 %collective-permute-start.10 = (bf16[512,512]{1,0:T(8,128)(2,1)}, bf16[512,512]{1,0:T(8,128)(2,1)}, u32[]{:S(2)}, u32[]{:S(2)}) collective-permute-start(bf16[512,512]{1,0:T(8,128)(2,1)} %pad_maximum_fusion.5), channel_id=1, source_target_pairs={{0,64},{1,65},{2,66},{3,67},{4,68},{5,69},{6,70},{7,71},{8,72},{9,... | collective-permute-start | bytes 1572872 | tf_op jit(solution)/shard_map/ppermute | solution.py:81
  141.8 9.6 %copy-start.8 = (bf16[256,1792]{1,0:T(8,128)(2,1)S(1)}, bf16[256,1792]{1,0:T(8,128)(2,1)}, u32[]{:S(2)}) copy-start(bf16[256,1792]{1,0:T(8,128)(2,1)} %constant_dynamic-slice_fusion.4) | copy-start | bytes 2752516
  141.8 9.6 %copy-start.9 = (bf16[256,1792]{1,0:T(8,128)(2,1)S(1)}, bf16[256,1792]{1,0:T(8,128)(2,1)}, u32[]{:S(2)}) copy-start(bf16[256,1792]{1,0:T(8,128)(2,1)} %get-tuple-element.9) | copy-start | bytes 2752516
  148.1 8.9 %copy-start.3 = (bf16[3584,512]{1,0:T(8,128)(2,1)S(1)}, bf16[3584,512]{1,0:T(8,128)(2,1)}, u32[]{:S(2)}) copy-start(bf16[3584,512]{1,0:T(8,128)(2,1)} %param.14) | copy-start | bytes 11010052
  148.1 8.9 %copy-start.6 = (f32[256,3584]{1,0:T(8,128)S(1)}, f32[256,3584]{1,0:T(8,128)}, u32[]{:S(2)}) copy-start(f32[256,3584]{1,0:T(8,128)} %fusion.62) | copy-start | bytes 11010052
  165.9 34.3 %all-to-all-start.3 = ((bf16[32,8,3584]{2,1,0:T(8,128)(2,1)}), bf16[32,8,3584]{2,1,0:T(8,128)(2,1)}, u32[]{:S(2)}, u32[]{:S(2)}) async-start(bf16[32,8,3584]{2,1,0:T(8,128)(2,1)} %fusion.16), calls=%async_computation.3 | async-start | bytes 3670016 | tf_op jit(solution)/shard_map/all_to_all | solution.py:21
  174.0 28.8 %copy-start.1 = (bf16[2,16,3584]{2,1,0:T(8,128)(2,1)S(1)}, bf16[2,16,3584]{2,1,0:T(8,128)(2,1)}, u32[]{:S(2)}) copy-start(bf16[2,16,3584]{2,1,0:T(8,128)(2,1)} %param.8) | copy-start | bytes 688132

commit v2 on v1

v2 whole, which is shorter than its diff:
```python
import math

import jax
import jax.numpy as jnp
from jax import lax
from jax.experimental import pallas as pl
from jax.experimental.pallas import tpu as pltpu
from jax.sharding import PartitionSpec as P


SPLIT = 2
AXES = ("dp", "expert")
PLAIN = (((1,), (0,)), ((), ()))
CONTRACT = (((1,), (1,)), ((), ()))
ROWS_FIRST = (((0,), (0,)), ((), ()))
VMEM = pl.BlockSpec(memory_space=pltpu.VMEM)
SMEM = pl.BlockSpec(memory_space=pltpu.SMEM)
HBM = pl.BlockSpec(memory_space=pltpu.HBM)


def near_groups(n_dp, n_ep):
    groups = []
    for side in range(n_dp):
        for core in range(SPLIT):
            groups.append(
                [((e % n_dp) ^ side) * n_ep + SPLIT * e + core for e in range(n_ep // SPLIT)]
            )
    return groups


def exchange(x, groups):
    return lax.all_to_all(
        x, AXES, split_axis=0, concat_axis=0, tiled=True, axis_index_groups=groups
    )


def mm(a, b, dims=PLAIN):
    return lax.dot_general(a, b, dims, preferred_element_type=jnp.float32)


def bf(*shape):
    return jax.ShapeDtypeStruct(shape, jnp.bfloat16)


def in_hbm(x):
    return pltpu.with_memory_space_constraint(x, pltpu.HBM)


def call(kernel, outs, ins, flops, in_specs, out_specs=None, scratch=()):
    size = sum(math.prod(x.shape) * x.dtype.itemsize for x in tuple(ins) + tuple(outs))
    return pl.pallas_call(
        kernel,
        out_shape=outs,
        in_specs=in_specs,
        out_specs=out_specs or [VMEM] * len(outs),
        scratch_shapes=list(scratch),
        compiler_params=pltpu.CompilerParams(vmem_limit_bytes=28 << 20),
        cost_estimate=pl.CostEstimate(flops=flops, bytes_accessed=size, transcendentals=0),
    )(*ins)


def pack_body(slots, capacity, ids_ref, prob_ref, marks_ref, tok_ref, cot_ref,
              sent_ref, pick_ref, split_ref, tok_buf, cot_buf, buf, sems):
    micros, topk, per_micro = ids_ref.shape
    experts = marks_ref.shape[1]
    places, rows = pick_ref.shape
    width = tok_ref.shape[1]
    fetch_tok = pltpu.make_async_copy(tok_ref, tok_buf, sems.at[0])
    fetch_cot = pltpu.make_async_copy(cot_ref, cot_buf, sems.at[1])
    fetch_tok.start()
    fetch_cot.start()
    ids = jnp.concatenate([ids_ref[m] for m in range(micros)], axis=1)
    probs = jnp.concatenate([prob_ref[m] for m in range(micros)], axis=1)
    place = lax.broadcasted_iota(jnp.int32, (places, rows), 0)
    token = lax.broadcasted_iota(jnp.int32, (places, rows), 1)
    expert = place // (micros * slots)
    micro = (place // slots) % micros
    hit = jnp.zeros((places, rows), jnp.float32)
    prob = jnp.zeros((places, rows), jnp.float32)
    for k in range(topk):
        same = ids[k : k + 1, :] == expert
        hit = hit + jnp.where(same, 1.0, 0.0)
        prob = prob + jnp.where(same, probs[k : k + 1, :], 0.0)
    down = lax.broadcasted_iota(jnp.int32, (rows, rows), 0)
    across = lax.broadcasted_iota(jnp.int32, (rows, rows), 1)
    earlier = (down < across) & (across // per_micro == down // per_micro)
    earlier = jnp.where(earlier, 1.0, 0.0).astype(jnp.bfloat16)
    ranked = mm(hit.astype(jnp.bfloat16), earlier)
    label = lax.broadcasted_iota(jnp.int32, (places, experts), 1)
    spot = lax.broadcasted_iota(jnp.int32, (places, experts), 0)
    marks = jnp.zeros((places, experts), jnp.float32)
    for m in range(micros):
        mark = jnp.where(marks_ref[m : m + 1, :] > 0, 1.0, 0.0)
        marks = marks + jnp.where((spot // slots) % micros == m, mark, 0.0)
    marks = jnp.where(label == spot // (micros * slots), marks, 0.0)
    limit = capacity * (1.0 + jnp.sum(marks, axis=1, keepdims=True))
    chosen = (hit > 0.5) & (micro == token // per_micro) & (ranked < limit)
    chosen = chosen & (ranked == (place % slots).astype(jnp.float32))
    picked = jnp.where(chosen, 1.0, 0.0).astype(jnp.bfloat16)
    weight = jnp.where(chosen, prob, 0.0)
    slot_prob = jnp.sum(weight, axis=1, keepdims=True)
    high = weight.astype(jnp.bfloat16)
    rest = weight - high.astype(jnp.float32)
    middle = rest.astype(jnp.bfloat16)
    low = (rest - middle.astype(jnp.float32)).astype(jnp.bfloat16)
    pick_ref[...] = picked
    split_ref[0] = high
    split_ref[1] = middle
    split_ref[2] = low
    fetch_tok.wait()
    buf[:, :width] = mm(picked, tok_buf[...]).astype(jnp.bfloat16)
    first = pltpu.make_async_copy(
        buf.at[:, pl.ds(0, width)], sent_ref.at[:, pl.ds(0, width)], sems.at[2]
    )
    first.start()
    fetch_cot.wait()
    buf[:, width:] = (slot_prob * mm(picked, cot_buf[...])).astype(jnp.bfloat16)
    second = pltpu.make_async_copy(
        buf.at[:, pl.ds(width, width)], sent_ref.at[:, pl.ds(width, width)], sems.at[3]
    )
    second.start()
    first.wait()
    second.wait()


def cut_body(start_ref, rows_ref, out_ref, sems):
    take = out_ref.shape[1] // 2
    width = rows_ref.shape[1] // 2
    start = pl.multiple_of(start_ref[0], 128)
    copies = [
        pltpu.make_async_copy(
            rows_ref.at[:, pl.ds(pl.multiple_of(start + i * width, 128), take)],
            out_ref.at[:, pl.ds(i * take, take)],
            sems.at[i],
        )
        for i in range(2)
    ]
    for copy in copies:
        copy.start()
    for copy in copies:
        copy.wait()


def slopes(gate_pre, up_pre, hidden_grad):
    squash = jax.nn.sigmoid(gate_pre)
    active = gate_pre * squash
    hidden = (active * up_pre).astype(jnp.bfloat16)
    slope = squash * (1.0 + gate_pre * (1.0 - squash))
    gate_grad = (hidden_grad * up_pre * slope).astype(jnp.bfloat16)
    up_grad = (hidden_grad * active).astype(jnp.bfloat16)
    return hidden, gate_grad, up_grad


def own_body(pieces, rows_ref, wg_ref, wu_ref, wd_ref, hid_ref, gg_ref, ug_ref,
             wg_out, wu_out, wd_out, xbuf, cbuf, sems):
    width = wg_ref.shape[0]
    size = width // pieces
    fetches = []
    for i in range(pieces):
        low = i * size
        span = pl.ds(low, size)
        moves = (
            (rows_ref.at[:, span], xbuf.at[:, span]),
            (wg_ref.at[span, :], wg_out.at[span, :]),
            (wu_ref.at[span, :], wu_out.at[span, :]),
            (rows_ref.at[:, pl.ds(width + low, size)], cbuf.at[:, span]),
            (wd_ref.at[span, :], wd_out.at[span, :]),
        )
        fetches.append(
            [pltpu.make_async_copy(a, b, sems.at[i, k]) for k, (a, b) in enumerate(moves)]
        )
    for fetch in fetches:
        for copy in fetch:
            copy.start()
    gate_pre = up_pre = hidden_grad = 0.0
    for i in range(pieces):
        low, high = i * size, (i + 1) * size
        for copy in fetches[i]:
            copy.wait()
        x = xbuf[:, low:high]
        gate_pre = gate_pre + mm(x, wg_out[low:high, :])
        up_pre = up_pre + mm(x, wu_out[low:high, :])
        hidden_grad = hidden_grad + mm(cbuf[:, low:high], wd_out[low:high, :])
    values = slopes(gate_pre, up_pre, hidden_grad)
    for ref, value in zip((hid_ref, gg_ref, ug_ref), values):
        ref[...] = value


def oth_body(rows_ref, wg_ref, wu_ref, wd_ref, h_ref, g_ref, u_ref,
             hid_ref, gg_ref, ug_ref, xbuf, cbuf, sems):
    width = wg_ref.shape[0]
    fetch_x = pltpu.make_async_copy(rows_ref.at[:, pl.ds(0, width)], xbuf, sems.at[0])
    fetch_c = pltpu.make_async_copy(rows_ref.at[:, pl.ds(width, width)], cbuf, sems.at[1])
    fetch_x.start()
    fetch_c.start()
    fetch_x.wait()
    x = xbuf[...]
    gate_pre = mm(x, wg_ref[...])
    up_pre = mm(x, wu_ref[...])
    fetch_c.wait()
    hidden_grad = mm(cbuf[...], wd_ref[...])
    values = slopes(gate_pre, up_pre, hidden_grad)
    rows = h_ref.shape[0]
    for ref, prior, value in zip((hid_ref, gg_ref, ug_ref), (h_ref, g_ref, u_ref), values):
        ref[0:rows, :] = prior[...]
        ref[rows : 2 * rows, :] = value


def out_body(hid_ref, wd_ref, out_ref):
    rows = out_ref.shape[0]
    hidden = hid_ref[rows : 2 * rows, :]
    out_ref[...] = mm(hidden, wd_ref[...], CONTRACT).astype(jnp.bfloat16)


def dx_body(gg_ref, ug_ref, wg_ref, wu_ref, dx_ref):
    rows = dx_ref.shape[0]
    dx = mm(gg_ref[rows : 2 * rows, :], wg_ref[...], CONTRACT)
    dx = dx + mm(ug_ref[rows : 2 * rows, :], wu_ref[...], CONTRACT)
    dx_ref[...] = dx.astype(jnp.bfloat16)


def plus(part, other):
    here = part.astype(jnp.bfloat16).astype(jnp.float32)
    return (here + other.astype(jnp.float32)).astype(jnp.bfloat16)


def out_add_body(hid_ref, wd_ref, other_ref, out_ref):
    rows = out_ref.shape[0]
    out_ref[...] = plus(mm(hid_ref[0:rows, :], wd_ref[...], CONTRACT), other_ref[...])


def dx_add_body(pieces, gg_ref, ug_ref, wg_ref, wu_ref, other_ref, left_ref, out_ref, buf, sems):
    rows, width = left_ref.shape
    copies = [
        pltpu.make_async_copy(left_ref, out_ref.at[:, pl.ds(0, width)], sems.at[pieces])
    ]
    copies[0].start()
    gate_grad = gg_ref[0:rows, :]
    up_grad = ug_ref[0:rows, :]
    size = width // pieces
    for i in range(pieces):
        low, high = i * size, (i + 1) * size
        dx = mm(gate_grad, wg_ref[low:high, :], CONTRACT)
        dx = dx + mm(up_grad, wu_ref[low:high, :], CONTRACT)
        buf[:, low:high] = plus(dx, other_ref[:, low:high])
        copy = pltpu.make_async_copy(
            buf.at[:, pl.ds(low, size)], out_ref.at[:, pl.ds(width + low, size)], sems.at[i]
        )
        copy.start()
        copies.append(copy)
    for copy in copies:
        copy.wait()


def turn_body(half_ref, first_ref, second_ref, out_ref):
    rows = first_ref.shape[0]
    out_ref[:, 0:rows] = first_ref[...].T
    out_ref[:, rows : 2 * rows] = second_ref[...].T


def turn(half, first, second, cut):
    rows, wide = first.shape
    block = 256
    tall = wide if cut else wide // 2
    steps = tall // block
    per = steps // 2
    if cut:
        spec = pl.BlockSpec((rows, block), lambda i, h: (0, i))
    else:
        spec = pl.BlockSpec((rows, block), lambda i, h: (0, h[0] * per + i + i // per * per))
    return pl.pallas_call(
        turn_body,
        out_shape=bf(tall, 2 * rows),
        grid_spec=pltpu.PrefetchScalarGridSpec(
            num_scalar_prefetch=1,
            grid=(steps,),
            in_specs=[spec, spec],
            out_specs=pl.BlockSpec((block, 2 * rows), lambda i, h: (i, 0)),
        ),
        compiler_params=pltpu.CompilerParams(vmem_limit_bytes=28 << 20),
    )(half, first, second)


def grad_body(near_ref, far_ref, here_ref, there_ref, out_ref):
    out_ref[...] = mm(near_ref[...], here_ref[...]) + mm(far_ref[...], there_ref[...])


def weight_grad(near, far, here, there, second):
    wide, rows = near.shape
    part = here.shape[1]
    tall = wide // 2
    block = 256
    steps = tall // block
    start = steps if second else 0
    lhs = pl.BlockSpec((block, rows), lambda i: (start + i, 0))
    whole = pl.BlockSpec((rows, part), lambda i: (0, 0))
    return pl.pallas_call(
        grad_body,
        out_shape=jax.ShapeDtypeStruct((tall, part), jnp.float32),
        grid=(steps,),
        in_specs=[lhs, lhs, whole, whole],
        out_specs=pl.BlockSpec((block, part), lambda i: (i, 0)),
        compiler_params=pltpu.CompilerParams(vmem_limit_bytes=28 << 20),
        cost_estimate=pl.CostEstimate(
            flops=4 * rows * tall * part, bytes_accessed=8 << 20, transcendentals=0
        ),
    )(near, far, here, there)


def combine_body(pieces, back_ref, pick_ref, split_ref, moe_ref, dx_ref, buf, sems):
    width = moe_ref.shape[1]
    size = width // pieces
    copies = []
    for i in range(2 * pieces):
        span = pl.ds(i * size, size)
        copies.append(pltpu.make_async_copy(back_ref.at[:, span], buf.at[:, span], sems.at[i]))
    for copy in copies:
        copy.start()
    for i in range(pieces):
        low, high = i * size, (i + 1) * size
        copies[i].wait()
        rows = buf[:, low:high]
        small = mm(split_ref[1], rows, ROWS_FIRST) + mm(split_ref[2], rows, ROWS_FIRST)
        moe = mm(split_ref[0], rows, ROWS_FIRST) + small
        moe_ref[:, low:high] = moe.astype(jnp.bfloat16)
    for i in range(pieces):
        low, high = i * size, (i + 1) * size
        copies[pieces + i].wait()
        dx = mm(pick_ref[...], buf[:, width + low : width + high], ROWS_FIRST)
        dx_ref[:, low:high] = dx.astype(jnp.bfloat16)


def combine(back, picked, split, pieces):
    places, double = back.shape
    width = double // 2
    rows = picked.shape[1]

    def body(*refs):
        combine_body(pieces, *refs)

    return call(
        body,
        (bf(rows, width), bf(rows, width)),
        (in_hbm(back), picked, split),
        8 * rows * places * width,
        [HBM, VMEM, VMEM],
        scratch=(
            pltpu.VMEM((places, double), jnp.bfloat16),
            pltpu.SemaphoreType.DMA((2 * pieces,)),
        ),
    )


def local(tokens, out_grad, expert_ids, route_probs, copy_marks, w_gate, w_up, w_down):
    n_dp = lax.axis_size("dp")
    n_ep = lax.axis_size("expert")
    devices = n_dp * n_ep
    experts = n_ep // SPLIT
    micros, tok_rows, width = tokens.shape
    topk = expert_ids.shape[2]
    capacity = max(1, tok_rows * topk // experts)
    slots = 2 * capacity
    group_rows = micros * slots
    places = experts * group_rows
    half_width = width // n_dp
    part = w_gate.shape[1]
    flat_rows = micros * tok_rows
    half = lax.axis_index("dp").astype(jnp.int32)
    groups = near_groups(n_dp, n_ep)
    cores = [(i, i ^ 1) for i in range(devices)]
    pairs = [(i, (i + n_ep) % devices) for i in range(devices)]
    unit = 2 * places * part * width

    def core_swap(x):
        return lax.ppermute(x, AXES, cores)

    def pair_swap(x):
        return lax.ppermute(x, AXES, pairs)

    def travel(x):
        return exchange(x.reshape(experts, group_rows, 2 * width), groups).reshape(-1, 2 * width)

    def pack(*refs):
        pack_body(slots, capacity, *refs)

    sent, picked, split = call(
        pack,
        (
            pltpu.HBM((places, 2 * width), jnp.bfloat16),
            bf(places, flat_rows),
            bf(3, places, flat_rows),
        ),
        (
            expert_ids.transpose(0, 2, 1),
            route_probs.transpose(0, 2, 1),
            copy_marks,
            in_hbm(tokens.reshape(flat_rows, width)),
            in_hbm(out_grad.reshape(flat_rows, width)),
        ),
        4 * places * flat_rows * width,
        [VMEM] * 3 + [HBM] * 2,
        [HBM, VMEM, VMEM],
        (
            pltpu.VMEM((flat_rows, width), jnp.bfloat16),
            pltpu.VMEM((flat_rows, width), jnp.bfloat16),
            pltpu.VMEM((places, 2 * width), jnp.bfloat16),
            pltpu.SemaphoreType.DMA((4,)),
        ),
    )
    own = travel(sent)
    oth = core_swap(own)
    (theirs,) = call(
        cut_body,
        (bf(places, width),),
        (((1 - half) * half_width).reshape(1), own),
        0,
        [SMEM, HBM],
        [VMEM],
        (pltpu.SemaphoreType.DMA((2,)),),
    )
    pair_own = pair_swap(theirs)

    pieces = 4

    def begin(*refs):
        own_body(pieces, *refs)

    def finish(*refs):
        dx_add_body(pieces, *refs)

    buffers = (
        pltpu.VMEM((places, width), jnp.bfloat16),
        pltpu.VMEM((places, width), jnp.bfloat16),
    )
    mid = bf(places, part)
    mids = bf(2 * places, part)
    *first, wg, wu, wd = call(
        begin,
        (mid,) * 3 + (bf(width, part),) * 3,
        (own, *map(in_hbm, (w_gate, w_up, w_down))),
        3 * unit,
        [HBM] * 4,
        scratch=buffers + (pltpu.SemaphoreType.DMA((pieces, 5)),),
    )
    hid, gg, ug = call(
        oth_body,
        (mids,) * 3,
        (oth, wg, wu, wd, *first),
        3 * unit,
        [HBM] + [VMEM] * 6,
        scratch=buffers + (pltpu.SemaphoreType.DMA((2,)),),
    )
    row = bf(places, width)
    (out_oth,) = call(out_body, (row,), (hid, wd), unit, [VMEM] * 2)
    (dx_oth,) = call(dx_body, (row,), (gg, ug, wg, wu), 2 * unit, [VMEM] * 4)
    out_other = core_swap(out_oth)
    dx_other = core_swap(dx_oth)
    hid_there = pair_swap(hid)
    gg_there = pair_swap(gg)
    ug_there = pair_swap(ug)

    (left,) = call(out_add_body, (row,), (hid, wd, out_other), unit, [VMEM] * 3)
    (total,) = call(
        finish,
        (pltpu.HBM((places, 2 * width), jnp.bfloat16),),
        (gg, ug, wg, wu, dx_other, left),
        2 * unit,
        [VMEM] * 6,
        [HBM],
        (
            pltpu.VMEM((places, width), jnp.bfloat16),
            pltpu.SemaphoreType.DMA((pieces + 1,)),
        ),
    )
    back = travel(total)
    pair_oth = core_swap(pair_own)
    h = half.reshape(1)
    near = turn(h, own, oth, False)
    far = turn(h, pair_own, pair_oth, True)
    grad_down = weight_grad(near, far, hid, hid_there, True)
    grad_gate = weight_grad(near, far, gg, gg_there, False)
    grad_up = weight_grad(near, far, ug, ug_there, False)
    moe, grad_in = combine(back, picked, split, pieces)
    return (
        moe.reshape(micros, tok_rows, width),
        grad_in.reshape(micros, tok_rows, width),
        grad_gate,
        grad_up,
        grad_down,
    )


def solution(mesh):
    tok = P(None, AXES, None)

    return jax.shard_map(
        local,
        mesh=mesh,
        in_specs=(tok, tok, tok, tok, P(), P(None, "expert"), P(None, "expert"), P(None, "expert")),
        out_specs=(tok, tok, P("dp", "expert"), P("dp", "expert"), P("dp", "expert")),
        check_vma=False,
    )
```

time: 204 us -> 174 us (0.85)
  waiting for transfers between devices: 95.3 us -> 37.8 us
  Pallas kernels: 0 us -> 56.9 us
  blocking collectives: 0 us -> 56.9 us
  matrix products: 50.5 us -> 0 us
  starting transfers between devices: 40.8 us -> 11.1 us
  other arithmetic: 6.67 us -> 0 us
    all_to_all x4 -> x1, waiting for transfers between devices: 73 us -> 0.01 us  [exchange(): lax.all_to_all(x, AXES, split_axis=0, concat_axis=0, tiled=True, axis_ind...]
    all_to_all x0 -> x1, blocking collectives: none -> 56.9 us  [exchange(): lax.all_to_all(x, AXES, split_axis=0, concat_axis=0, tiled=True, axis_ind...]
    pallas_call x0 -> x14, Pallas kernels: none -> 56.9 us  [the longest x9 32 us: call(): pl.pallas_call(kernel, out_shape=outs, in_specs=in_specs, out_specs=out_s...]
    dot_general x19 -> x0, matrix products: 50.5 us -> none  [mm(): return lax.dot_general(a, b, dims, preferred_element_type=jnp.float32)]
    all_to_all x4 -> x1, starting transfers between devices: 32.7 us -> 4.85 us  [exchange(): lax.all_to_all(x, AXES, split_axis=0, concat_axis=0, tiled=True, axis_ind...]
    ppermute x5 -> x4, waiting for transfers between devices: 22.3 us -> 37.8 us  [pair_swap(): return lax.ppermute(x, AXES, pairs)]
    unnamed x22 -> x32, local copies, waits for them, and re-layouts: 0.97 us -> 9.16 us
    dynamic_slice x4 -> x0, local copies, waits for them, and re-layouts: 6.72 us -> none  [mine(): return lax.dynamic_slice_in_dim(x, half * half_width, half_width, 1)]
  transfers between devices with their start and end apart: 15 -> 9, of which waited for: 7 -> 3; matrix products, arithmetic and copies ran while one was open for 28% -> 0% of each run, Pallas kernels for 0% -> 25%
where the time goes in v2:
time: 174 us; the launch traced here: 173 us
  Pallas kernels  56.9 us (33%)
  blocking collectives  56.9 us (33%)
  waiting for transfers between devices  37.8 us (22%)
  starting transfers between devices  11.1 us (6%)
  local copies, waits for them, and re-layouts  9.16 us (5%)
    all_to_all x1, blocking collectives, exchange(): lax.all_to_all(x, AXES, split_axis=0, concat_axis=0, tiled=True, axis_ind...  56.9 us
    ppermute x4, waiting for transfers between devices, pair_swap(): return lax.ppermute(x, AXES, pairs)  37.8 us
    pallas_call x9, Pallas kernels, call(): pl.pallas_call(kernel, out_shape=outs, in_specs=in_specs, out_specs=out_s...  32 us
    pallas_call x3, Pallas kernels, weight_grad(): pl.pallas_call(grad_body, out_shape=jax.ShapeDtypeStruct((tall, part), jn...  14.8 us
    pallas_call x2, Pallas kernels, turn(): pl.pallas_call(turn_body, out_shape=bf(tall, 2 * rows), grid_spec=pltpu.P...  10.1 us
    unnamed x32, local copies, waits for them, and re-layouts  9.16 us
    all_to_all x1, starting transfers between devices, exchange(): lax.all_to_all(x, AXES, split_axis=0, concat_axis=0, tiled=True, axis_ind...  4.85 us
    ppermute x4, starting transfers between devices, core_swap(): return lax.ppermute(x, AXES, cores)  4.49 us
  transfers between devices with their start and end apart: 9, of which 3 were waited for; matrix products, arithmetic and copies ran while one was open for 0% of the time, Pallas kernels for 25%

profile of v2, /device:TPU:1, one launch (start us, length us, event | category | flops | bytes accessed | tf_op | source)
XLA Modules:
  0.0 172.9 jit_solution(18202716772773276610)
XLA Ops:
  0.6 0.7 copy-done.13
  1.3 0.7 copy-done.14
  2.0 0.7 copy-done.15
  2.7 3.7 %shard_map.119 = (bf16[256,7168]{1,0:T(8,128)(2,1)}, bf16[256,32]{1,0:T(8,128)(2,1)S(1)}, bf16[3,256,32]{2,1,0:T(8,128)(2,1)S(1)}) custom-call(s32[2,4,16]{2,1,0:T(4,128)S(1)} %bitcast.16, f32[2,4,16]{2,1,0:T(4,128)S(1)} %bitcast.17, s32[2,32]{1,0:T(2,128)S(1)} %copy-done.15, bf16[32,3584]{1,0:T(8,128)(2,1)} %bitcast.20, bf16[32,3584]{1,0:T(8,128)(2,1)} %bitcast.21), custom_call_target="tpu_custom_call" | custom-call | flops 117440512 | bytes 4195584 | tf_op jit(solution)/shard_map/pallas_call | solution.py:51
  6.4 56.9 %all_to_all.10 = bf16[32,8,7168]{2,1,0:T(8,128)(2,1)S(1)} all-to-all(bf16[32,8,7168]{2,1,0:T(8,128)(2,1)} %bitcast.19), channel_id=1, replica_groups={{0,66,4,70,8,74,12,78,16,82,20,86,24,90,28,94,32,98,36,102,40,106,44,11..., dimensions={0} | all-to-all | bytes 7340032 | tf_op jit(solution)/shard_map/all_to_all | solution.py:32
  63.4 1.8 %collective-permute-start = (bf16[256,7168]{1,0:T(8,128)(2,1)S(1)}, bf16[256,7168]{1,0:T(8,128)(2,1)S(1)}, u32[]{:S(2)}, u32[]{:S(2)}) collective-permute-start(bf16[256,7168]{1,0:T(8,128)(2,1)S(1)} %bitcast.12), channel_id=1, source_target_pairs={{0,1},{1,0},{2,3},{3,2},{4,5},{5,4},{6,7},{7,6},{8,9},{9,8},{10,11... | collective-permute-start | bytes 11010056 | tf_op jit(solution)/shard_map/ppermute | solution.py:375
  65.2 6.4 %shard_map.120 = (bf16[256,512]{1,0:T(8,128)(2,1)S(1)}, bf16[256,512]{1,0:T(8,128)(2,1)S(1)}, bf16[256,512]{1,0:T(8,128)(2,1)S(1)}, bf16[3584,512]{1,0:T(8,128)(...) custom-call(bf16[256,7168]{1,0:T(8,128)(2,1)S(1)} %bitcast.13, bf16[3584,512]{1,0:T(8,128)(2,1)} %refs_1_.1, ...), custom_call_target="tpu_custom_call" | custom-call | flops 2818572288 | bytes 26476544 | tf_op jit(solution)/shard_map/pallas_call | solution.py:51
  71.6 3.6 %shard_map.121 = (bf16[512,512]{1,0:T(8,128)(2,1)S(1)}, bf16[512,512]{1,0:T(8,128)(2,1)S(1)}, bf16[512,512]{1,0:T(8,128)(2,1)S(1)}) custom-call(bf16[256,7168]{1,0:T(8,128)(2,1)S(1)} %collective-permute-done.rows_ref.second_ref, bf16[3584,512]{1,0:T(8,128)(2,1)S(1)} %get-tuple-element.20.wg_ref.refs_2_, ...), custom_call_target="tpu_custom_call" | custom-call | flops 2818572288 | bytes 17039360 | tf_op jit(solution)/shard_map/pallas_call | solution.py:51
  75.3 2.4 %shard_map.123 = bf16[256,3584]{1,0:T(8,128)(2,1)} custom-call(bf16[512,512]{1,0:T(8,128)(2,1)S(1)} %get-tuple-element.28.hid_ref.here_ref, bf16[3584,512]{1,0:T(8,128)(2,1)S(1)} %get-tuple-element.22.wd_ref), custom_call_target="tpu_custom_call" | custom-call | flops 939524096 | bytes 6029312 | tf_op jit(solution)/shard_map/pallas_call | solution.py:51
  77.6 1.3 collective-permute-start.2
  78.9 2.1 %shard_map.122 = bf16[256,3584]{1,0:T(8,128)(2,1)S(1)} custom-call(bf16[512,512]{1,0:T(8,128)(2,1)S(1)} %get-tuple-element.26.gg_ref.refs_0_.here_ref, bf16[512,512]{1,0:T(8,128)(2,1)S(1)} %get-tuple-element.27.ug_ref.refs_1_.here_ref, bf16[3584,512]{1,0:T(8,128)(2,1)S(1)} %get-tuple-element.20.wg_ref.refs_2_, ...), custom_call_target="tpu_custom_call" | custom-call | flops 1879048192 | bytes 10223616 | tf_op jit(solution)/shard_map/pallas_call | solution.py:51
  81.0 0.1 collective-permute-start.1
  81.1 2.0 %copy-done.1 = bf16[32,8,7168]{2,1,0:T(8,128)(2,1)S(1)} copy-done((bf16[32,8,7168]{2,1,0:T(8,128)(2,1)S(1)}, bf16[32,8,7168]{2,1,0:T(8,128)(2,1)}, u32[]{:S(2)}) %copy-start.1) | copy-done | bytes 3670040
  83.2 1.4 shard_map.128
  84.6 0.3 collective-permute-start.3
  84.9 1.0 copy-done.4
  85.9 3.4 %shard_map.124.refs_5_ = bf16[256,3584]{1,0:T(8,128)(2,1)S(1)} custom-call(bf16[512,512]{1,0:T(8,128)(2,1)S(1)} %get-tuple-element.28.hid_ref.here_ref, bf16[3584,512]{1,0:T(8,128)(2,1)S(1)} %copy-done.4, bf16[256,3584]{1,0:T(8,128)(2,1)} %collective-permute-done.2.other_ref), custom_call_target="tpu_custom_call" | custom-call | flops 939524096 | bytes 7864320 | tf_op jit(solution)/shard_map/pallas_call | solution.py:51
  89.3 4.7 %shard_map.125 = bf16[256,7168]{1,0:T(8,128)(2,1)} custom-call(bf16[512,512]{1,0:T(8,128)(2,1)S(1)} %get-tuple-element.26.gg_ref.refs_0_.here_ref, bf16[512,512]{1,0:T(8,128)(2,1)S(1)} %get-tuple-element.27.ug_ref.refs_1_.here_ref, bf16[3584,512]{1,0:T(8,128)(2,1)S(1)} %copy-done.6, bf16[3584,512]{1,0:T(8,128)(2,1)S(1)} %copy-done.8, ...), custom_call_target="tpu_custom_call" | custom-call | flops 1879048192 | bytes 15728640 | tf_op jit(solution)/shard_map/pallas_call | solution.py:51
  94.0 4.8 %all-to-all-start.1 = ((bf16[32,8,7168]{2,1,0:T(8,128)(2,1)}), bf16[32,8,7168]{2,1,0:T(8,128)(2,1)}, u32[]{:S(2)}, u32[]{:S(2)}) async-start(bf16[32,8,7168]{2,1,0:T(8,128)(2,1)} %bitcast.18), calls=%async_computation.1 | async-start | bytes 7340032 | tf_op jit(solution)/shard_map/all_to_all | solution.py:32
  98.9 27.4 %collective-permute-done.3.first_ref = bf16[256,3584]{1,0:T(8,128)(2,1)} collective-permute-done((bf16[256,3584]{1,0:T(8,128)(2,1)}, bf16[256,3584]{1,0:T(8,128)(2,1)}, u32[]{:S(2)}, u32[]{:S(2)}) %collective-permute-start.3) | collective-permute-done | bytes 1835040 | tf_op jit(solution)/shard_map/ppermute | solution.py:378
  126.3 1.3 collective-permute-start.4
  127.6 1.5 collective-permute-start.6
  129.1 2.0 %copy-done.2 = bf16[32,8,7168]{2,1,0:T(8,128)(2,1)S(1)} copy-done((bf16[32,8,7168]{2,1,0:T(8,128)(2,1)S(1)}, bf16[32,8,7168]{2,1,0:T(8,128)(2,1)}, u32[]{:S(2)}) %copy-start.2) | copy-done | bytes 3670040
  131.1 2.0 %copy-done.10 = bf16[256,7168]{1,0:T(8,128)(2,1)S(1)} copy-done((bf16[256,7168]{1,0:T(8,128)(2,1)S(1)}, bf16[256,7168]{1,0:T(8,128)(2,1)}, u32[]{:S(2)}) %copy-start.10) | copy-done | bytes 3670040
  133.2 2.7 %shard_map.127.near_ref = bf16[3584,512]{1,0:T(8,128)(2,1)S(1)} custom-call(s32[1]{0:T(128)} %bitcast.10.half_ref, bf16[256,7168]{1,0:T(8,128)(2,1)S(1)} %bitcast.15, bf16[256,7168]{1,0:T(8,128)(2,1)S(1)} %copy-done.10), custom_call_target="tpu_custom_call" | custom-call | tf_op jit(solution)/shard_map/pallas_call | solution.py:271
  135.9 7.5 %shard_map.129.far_ref = bf16[3584,512]{1,0:T(8,128)(2,1)S(1)} custom-call(s32[1]{0:T(128)} %bitcast.10.half_ref, bf16[256,3584]{1,0:T(8,128)(2,1)} %collective-permute-done.3.first_ref, bf16[256,3584]{1,0:T(8,128)(2,1)S(1)} %collective-permute-done.4.second_ref), custom_call_target="tpu_custom_call" | custom-call | tf_op jit(solution)/shard_map/pallas_call | solution.py:271
  143.3 4.9 %shard_map.130 = f32[1792,512]{1,0:T(8,128)} custom-call(bf16[3584,512]{1,0:T(8,128)(2,1)S(1)} %shard_map.127.near_ref, bf16[3584,512]{1,0:T(8,128)(2,1)S(1)} %shard_map.129.far_ref, bf16[512,512]{1,0:T(8,128)(2,1)S(1)} %get-tuple-element.26.gg_ref.refs_0_.here_ref, bf16[512,512]{1,0:T(8,128)(2,1)S(1)} %collective-permute-done.5.there_ref), custom_call_target="tpu_custom_call" | custom-call | flops 1879048192 | bytes 8388608 | tf_op jit(solution)/shard_map/pallas_call | solution.py:297
  148.3 4.1 %collective-permute-done.6.there_ref = bf16[512,512]{1,0:T(8,128)(2,1)S(1)} collective-permute-done((bf16[512,512]{1,0:T(8,128)(2,1)S(1)}, bf16[512,512]{1,0:T(8,128)(2,1)S(1)}, u32[]{:S(2)}, u32[]{:S(2)}) %collective-permute-start.6) | collective-permute-done | bytes 524320 | tf_op jit(solution)/shard_map/ppermute | solution.py:378
  152.3 4.9 %shard_map.131 = f32[1792,512]{1,0:T(8,128)} custom-call(bf16[3584,512]{1,0:T(8,128)(2,1)S(1)} %shard_map.127.near_ref, bf16[3584,512]{1,0:T(8,128)(2,1)S(1)} %shard_map.129.far_ref, bf16[512,512]{1,0:T(8,128)(2,1)S(1)} %get-tuple-element.27.ug_ref.refs_1_.here_ref, bf16[512,512]{1,0:T(8,128)(2,1)S(1)} %collective-permute-done.6.there_ref), custom_call_target="tpu_custom_call" | custom-call | flops 1879048192 | bytes 8388608 | tf_op jit(solution)/shard_map/pallas_call | solution.py:297
  157.2 6.3 %collective-permute-done.7.there_ref = bf16[512,512]{1,0:T(8,128)(2,1)S(1)} collective-permute-done((bf16[512,512]{1,0:T(8,128)(2,1)S(1)}, bf16[512,512]{1,0:T(8,128)(2,1)S(1)}, u32[]{:S(2)}, u32[]{:S(2)}) %collective-permute-start.7) | collective-permute-done | bytes 524320 | tf_op jit(solution)/shard_map/ppermute | solution.py:378
  163.6 4.9 %shard_map.132 = f32[1792,512]{1,0:T(8,128)} custom-call(bf16[3584,512]{1,0:T(8,128)(2,1)S(1)} %shard_map.127.near_ref, bf16[3584,512]{1,0:T(8,128)(2,1)S(1)} %shard_map.129.far_ref, bf16[512,512]{1,0:T(8,128)(2,1)S(1)} %get-tuple-element.28.hid_ref.here_ref, bf16[512,512]{1,0:T(8,128)(2,1)S(1)} %collective-permute-done.7.there_ref), custom_call_target="tpu_custom_call" | custom-call | flops 1879048192 | bytes 8388608 | tf_op jit(solution)/shard_map/pallas_call | solution.py:297
  168.5 4.3 %shard_map.126 = (bf16[32,3584]{1,0:T(8,128)(2,1)}, bf16[32,3584]{1,0:T(8,128)(2,1)}) custom-call(bf16[256,7168]{1,0:T(8,128)(2,1)} %bitcast.7.refs_0_, bf16[256,32]{1,0:T(8,128)(2,1)S(1)} %get-tuple-element.29.refs_1_, bf16[3,256,32]{2,1,0:T(8,128)(2,1)S(1)} %copy-done.12), custom_call_target="tpu_custom_call" | custom-call | flops 234881024 | bytes 4194304 | tf_op jit(solution)/shard_map/pallas_call | solution.py:51
  (33 shorter events, 0.1 us)
Async XLA Ops:
  0.6 0.7 copy-start.13
  1.3 0.7 copy-start.14
  2.0 0.7 copy-start.15
  6.4 57.0 %copy-start.11 = (bf16[3,256,32]{2,1,0:T(8,128)(2,1)}, bf16[3,256,32]{2,1,0:T(8,128)(2,1)S(1)}, u32[]{:S(2)}) copy-start(bf16[3,256,32]{2,1,0:T(8,128)(2,1)S(1)} %get-tuple-element.30.refs_2_) | copy-start | bytes 147460
  63.4 8.2 %copy-start = (bf16[32,8,7168]{2,1,0:T(8,128)(2,1)}, bf16[32,8,7168]{2,1,0:T(8,128)(2,1)S(1)}, u32[]{:S(2)}) copy-start(bf16[32,8,7168]{2,1,0:T(8,128)(2,1)S(1)} %all_to_all.10) | copy-start | bytes 11010052
  63.4 8.3 %collective-permute-start = (bf16[256,7168]{1,0:T(8,128)(2,1)S(1)}, bf16[256,7168]{1,0:T(8,128)(2,1)S(1)}, u32[]{:S(2)}, u32[]{:S(2)}) collective-permute-start(bf16[256,7168]{1,0:T(8,128)(2,1)S(1)} %bitcast.12), channel_id=1, source_target_pairs={{0,1},{1,0},{2,3},{3,2},{4,5},{5,4},{6,7},{7,6},{8,9},{9,8},{10,11... | collective-permute-start | bytes 11010056 | tf_op jit(solution)/shard_map/ppermute | solution.py:375
  71.6 3.7 %copy-start.3 = (bf16[3584,512]{1,0:T(8,128)(2,1)}, bf16[3584,512]{1,0:T(8,128)(2,1)S(1)}, u32[]{:S(2)}) copy-start(bf16[3584,512]{1,0:T(8,128)(2,1)S(1)} %get-tuple-element.22.wd_ref) | copy-start | bytes 11010052
  71.6 7.3 %copy-start.5 = (bf16[3584,512]{1,0:T(8,128)(2,1)}, bf16[3584,512]{1,0:T(8,128)(2,1)S(1)}, u32[]{:S(2)}) copy-start(bf16[3584,512]{1,0:T(8,128)(2,1)S(1)} %get-tuple-element.20.wg_ref.refs_2_) | copy-start | bytes 11010052
  71.6 7.3 %copy-start.7 = (bf16[3584,512]{1,0:T(8,128)(2,1)}, bf16[3584,512]{1,0:T(8,128)(2,1)S(1)}, u32[]{:S(2)}) copy-start(bf16[3584,512]{1,0:T(8,128)(2,1)S(1)} %get-tuple-element.21.wu_ref.refs_3_) | copy-start | bytes 11010052
  71.6 3.6 %copy-start.9 = (bf16[256,7168]{1,0:T(8,128)(2,1)}, bf16[256,7168]{1,0:T(8,128)(2,1)S(1)}, u32[]{:S(2)}) copy-start(bf16[256,7168]{1,0:T(8,128)(2,1)S(1)} %collective-permute-done.rows_ref.second_ref) | copy-start | bytes 11010052
  77.6 7.3 %collective-permute-start.2 = (bf16[256,3584]{1,0:T(8,128)(2,1)}, bf16[256,3584]{1,0:T(8,128)(2,1)}, u32[]{:S(2)}, u32[]{:S(2)}) collective-permute-start(bf16[256,3584]{1,0:T(8,128)(2,1)} %shard_map.123), channel_id=1, source_target_pairs={{0,1},{1,0},{2,3},{3,2},{4,5},{5,4},{6,7},{7,6},{8,9},{9,8},{10,11... | collective-permute-start | bytes 5505032 | tf_op jit(solution)/shard_map/ppermute | solution.py:375
  81.0 8.3 %collective-permute-start.1 = (bf16[256,3584]{1,0:T(8,128)(2,1)S(1)}, bf16[256,3584]{1,0:T(8,128)(2,1)}, u32[]{:S(2)}, u32[]{:S(2)}) collective-permute-start(bf16[256,3584]{1,0:T(8,128)(2,1)S(1)} %shard_map.122), channel_id=1, source_target_pairs={{0,1},{1,0},{2,3},{3,2},{4,5},{5,4},{6,7},{7,6},{8,9},{9,8},{10,11... | collective-permute-start | bytes 5505032 | tf_op jit(solution)/shard_map/ppermute | solution.py:375
  81.1 2.0 %copy-start.1 = (bf16[32,8,7168]{2,1,0:T(8,128)(2,1)S(1)}, bf16[32,8,7168]{2,1,0:T(8,128)(2,1)}, u32[]{:S(2)}) copy-start(bf16[32,8,7168]{2,1,0:T(8,128)(2,1)} %copy-done) | copy-start | bytes 11010052
  83.2 2.7 %copy-start.4 = (bf16[3584,512]{1,0:T(8,128)(2,1)S(1)}, bf16[3584,512]{1,0:T(8,128)(2,1)}, u32[]{:S(2)}) copy-start(bf16[3584,512]{1,0:T(8,128)(2,1)} %copy-done.3) | copy-start | bytes 11010052
  84.6 4.7 %copy-start.6 = (bf16[3584,512]{1,0:T(8,128)(2,1)S(1)}, bf16[3584,512]{1,0:T(8,128)(2,1)}, u32[]{:S(2)}) copy-start(bf16[3584,512]{1,0:T(8,128)(2,1)} %copy-done.5) | copy-start | bytes 11010052
  84.6 4.7 %copy-start.8 = (bf16[3584,512]{1,0:T(8,128)(2,1)S(1)}, bf16[3584,512]{1,0:T(8,128)(2,1)}, u32[]{:S(2)}) copy-start(bf16[3584,512]{1,0:T(8,128)(2,1)} %copy-done.7) | copy-start | bytes 11010052
  84.6 41.7 %collective-permute-start.3 = (bf16[256,3584]{1,0:T(8,128)(2,1)}, bf16[256,3584]{1,0:T(8,128)(2,1)}, u32[]{:S(2)}, u32[]{:S(2)}) collective-permute-start(bf16[256,3584]{1,0:T(8,128)(2,1)} %shard_map.128), channel_id=1, source_target_pairs={{0,64},{1,65},{2,66},{3,67},{4,68},{5,69},{6,70},{7,71},{8,72},{9,... | collective-permute-start | bytes 5505032 | tf_op jit(solution)/shard_map/ppermute | solution.py:378
  94.0 74.5 %all-to-all-start.1 = ((bf16[32,8,7168]{2,1,0:T(8,128)(2,1)}), bf16[32,8,7168]{2,1,0:T(8,128)(2,1)}, u32[]{:S(2)}, u32[]{:S(2)}) async-start(bf16[32,8,7168]{2,1,0:T(8,128)(2,1)} %bitcast.18), calls=%async_computation.1 | async-start | bytes 7340032 | tf_op jit(solution)/shard_map/all_to_all | solution.py:32
  126.3 9.6 %collective-permute-start.4 = (bf16[256,3584]{1,0:T(8,128)(2,1)}, bf16[256,3584]{1,0:T(8,128)(2,1)S(1)}, u32[]{:S(2)}, u32[]{:S(2)}) collective-permute-start(bf16[256,3584]{1,0:T(8,128)(2,1)} %collective-permute-done.3.first_ref), channel_id=1, source_target_pairs={{0,1},{1,0},{2,3},{3,2},{4,5},{5,4},{6,7},{7,6},{8,9},{9,8},{10,11... | collective-permute-start | bytes 5505032 | tf_op jit(solution)/shard_map/ppermute | solution.py:375
  127.6 15.7 %collective-permute-start.5 = (bf16[512,512]{1,0:T(8,128)(2,1)S(1)}, bf16[512,512]{1,0:T(8,128)(2,1)S(1)}, u32[]{:S(2)}, u32[]{:S(2)}) collective-permute-start(bf16[512,512]{1,0:T(8,128)(2,1)S(1)} %get-tuple-element.26.gg_ref.refs_0_.here_ref), channel_id=1, source_target_pairs={{0,64},{1,65},{2,66},{3,67},{4,68},{5,69},{6,70},{7,71},{8,72},{9,... | collective-permute-start | bytes 1572872 | tf_op jit(solution)/shard_map/ppermute | solution.py:378
  127.6 24.7 %collective-permute-start.6 = (bf16[512,512]{1,0:T(8,128)(2,1)S(1)}, bf16[512,512]{1,0:T(8,128)(2,1)S(1)}, u32[]{:S(2)}, u32[]{:S(2)}) collective-permute-start(bf16[512,512]{1,0:T(8,128)(2,1)S(1)} %get-tuple-element.27.ug_ref.refs_1_.here_ref), channel_id=1, source_target_pairs={{0,64},{1,65},{2,66},{3,67},{4,68},{5,69},{6,70},{7,71},{8,72},{9,... | collective-permute-start | bytes 1572872 | tf_op jit(solution)/shard_map/ppermute | solution.py:378
  129.1 34.5 %collective-permute-start.7 = (bf16[512,512]{1,0:T(8,128)(2,1)S(1)}, bf16[512,512]{1,0:T(8,128)(2,1)S(1)}, u32[]{:S(2)}, u32[]{:S(2)}) collective-permute-start(bf16[512,512]{1,0:T(8,128)(2,1)S(1)} %get-tuple-element.28.hid_ref.here_ref), channel_id=1, source_target_pairs={{0,64},{1,65},{2,66},{3,67},{4,68},{5,69},{6,70},{7,71},{8,72},{9,... | collective-permute-start | bytes 1572872 | tf_op jit(solution)/shard_map/ppermute | solution.py:378
  129.1 2.0 %copy-start.2 = (bf16[32,8,7168]{2,1,0:T(8,128)(2,1)S(1)}, bf16[32,8,7168]{2,1,0:T(8,128)(2,1)}, u32[]{:S(2)}) copy-start(bf16[32,8,7168]{2,1,0:T(8,128)(2,1)} %copy-done) | copy-start | bytes 11010052
  131.1 2.0 %copy-start.10 = (bf16[256,7168]{1,0:T(8,128)(2,1)S(1)}, bf16[256,7168]{1,0:T(8,128)(2,1)}, u32[]{:S(2)}) copy-start(bf16[256,7168]{1,0:T(8,128)(2,1)} %copy-done.9) | copy-start | bytes 11010052
  157.2 11.2 %copy-start.12 = (bf16[3,256,32]{2,1,0:T(8,128)(2,1)S(1)}, bf16[3,256,32]{2,1,0:T(8,128)(2,1)}, u32[]{:S(2)}) copy-start(bf16[3,256,32]{2,1,0:T(8,128)(2,1)} %copy-done.11) | copy-start | bytes 147460

commit v3 on v2

--- a/solution.py
+++ b/solution.py
@@ -40,6 +40,10 @@
 
 def bf(*shape):
     return jax.ShapeDtypeStruct(shape, jnp.bfloat16)
+
+
+def in_vmem(x):
+    return pltpu.with_memory_space_constraint(x, pltpu.VMEM)
 
 
 def in_hbm(x):
@@ -59,8 +63,17 @@
     )(*ins)
 
 
-def pack_body(slots, capacity, ids_ref, prob_ref, marks_ref, tok_ref, cot_ref,
-              sent_ref, pick_ref, split_ref, tok_buf, cot_buf, buf, sems):
+def pack_body(slots, capacity, ids_hbm, prob_hbm, marks_hbm, tok_ref, cot_ref,
+              sent_ref, pick_ref, split_ref, ids_ref, prob_ref, marks_ref,
+              tok_buf, cot_buf, buf, sems):
+    small = [
+        pltpu.make_async_copy(a, b, sems.at[4 + i])
+        for i, (a, b) in enumerate(
+            ((ids_hbm, ids_ref), (prob_hbm, prob_ref), (marks_hbm, marks_ref))
+        )
+    ]
+    for copy in small:
+        copy.start()
     micros, topk, per_micro = ids_ref.shape
     experts = marks_ref.shape[1]
     places, rows = pick_ref.shape
@@ -69,6 +82,8 @@
     fetch_cot = pltpu.make_async_copy(cot_ref, cot_buf, sems.at[1])
     fetch_tok.start()
     fetch_cot.start()
+    for copy in small:
+        copy.wait()
     ids = jnp.concatenate([ids_ref[m] for m in range(micros)], axis=1)
     probs = jnp.concatenate([prob_ref[m] for m in range(micros)], axis=1)
     place = lax.broadcasted_iota(jnp.int32, (places, rows), 0)
@@ -104,9 +119,9 @@
     middle = rest.astype(jnp.bfloat16)
     low = (rest - middle.astype(jnp.float32)).astype(jnp.bfloat16)
     pick_ref[...] = picked
-    split_ref[0] = high
-    split_ref[1] = middle
-    split_ref[2] = low
+    split_ref[:, 0:rows] = high
+    split_ref[:, rows : 2 * rows] = middle
+    split_ref[:, 2 * rows : 3 * rows] = low
     fetch_tok.wait()
     buf[:, :width] = mm(picked, tok_buf[...]).astype(jnp.bfloat16)
     first = pltpu.make_async_copy(
@@ -187,18 +202,12 @@
 
 
 def oth_body(rows_ref, wg_ref, wu_ref, wd_ref, h_ref, g_ref, u_ref,
-             hid_ref, gg_ref, ug_ref, xbuf, cbuf, sems):
+             hid_ref, gg_ref, ug_ref):
     width = wg_ref.shape[0]
-    fetch_x = pltpu.make_async_copy(rows_ref.at[:, pl.ds(0, width)], xbuf, sems.at[0])
-    fetch_c = pltpu.make_async_copy(rows_ref.at[:, pl.ds(width, width)], cbuf, sems.at[1])
-    fetch_x.start()
-    fetch_c.start()
-    fetch_x.wait()
-    x = xbuf[...]
+    x = rows_ref[:, 0:width]
     gate_pre = mm(x, wg_ref[...])
     up_pre = mm(x, wu_ref[...])
-    fetch_c.wait()
-    hidden_grad = mm(cbuf[...], wd_ref[...])
+    hidden_grad = mm(rows_ref[:, width : 2 * width], wd_ref[...])
     values = slopes(gate_pre, up_pre, hidden_grad)
     rows = h_ref.shape[0]
     for ref, prior, value in zip((hid_ref, gg_ref, ug_ref), (h_ref, g_ref, u_ref), values):
@@ -219,35 +228,29 @@
     dx_ref[...] = dx.astype(jnp.bfloat16)
 
 
-def plus(part, other):
-    here = part.astype(jnp.bfloat16).astype(jnp.float32)
-    return (here + other.astype(jnp.float32)).astype(jnp.bfloat16)
-
-
-def out_add_body(hid_ref, wd_ref, other_ref, out_ref):
-    rows = out_ref.shape[0]
-    out_ref[...] = plus(mm(hid_ref[0:rows, :], wd_ref[...], CONTRACT), other_ref[...])
-
-
-def dx_add_body(pieces, gg_ref, ug_ref, wg_ref, wu_ref, other_ref, left_ref, out_ref, buf, sems):
-    rows, width = left_ref.shape
-    copies = [
-        pltpu.make_async_copy(left_ref, out_ref.at[:, pl.ds(0, width)], sems.at[pieces])
-    ]
-    copies[0].start()
-    gate_grad = gg_ref[0:rows, :]
-    up_grad = ug_ref[0:rows, :]
+def own_end_body(hid_ref, gg_ref, ug_ref, wg_ref, wu_ref, wd_ref, out_ref):
+    rows, double = out_ref.shape
+    width = double // 2
+    out = mm(hid_ref[0:rows, :], wd_ref[...], CONTRACT)
+    out_ref[:, 0:width] = out.astype(jnp.bfloat16)
+    dx = mm(gg_ref[0:rows, :], wg_ref[...], CONTRACT)
+    dx = dx + mm(ug_ref[0:rows, :], wu_ref[...], CONTRACT)
+    out_ref[:, width:double] = dx.astype(jnp.bfloat16)
+
+
+def add_body(pieces, part_ref, out_ref, dx_ref, total_ref, buf, sems):
+    width = out_ref.shape[1]
     size = width // pieces
-    for i in range(pieces):
-        low, high = i * size, (i + 1) * size
-        dx = mm(gate_grad, wg_ref[low:high, :], CONTRACT)
-        dx = dx + mm(up_grad, wu_ref[low:high, :], CONTRACT)
-        buf[:, low:high] = plus(dx, other_ref[:, low:high])
-        copy = pltpu.make_async_copy(
-            buf.at[:, pl.ds(low, size)], out_ref.at[:, pl.ds(width + low, size)], sems.at[i]
-        )
-        copy.start()
-        copies.append(copy)
+    copies = []
+    for i in range(2 * pieces):
+        low = i * size
+        source = out_ref if i < pieces else dx_ref
+        there = source[:, low % width : low % width + size].astype(jnp.float32)
+        here = part_ref[:, low : low + size].astype(jnp.float32)
+        buf[:, low : low + size] = (here + there).astype(jnp.bfloat16)
+        span = pl.ds(low, size)
+        copies.append(pltpu.make_async_copy(buf.at[:, span], total_ref.at[:, span], sems.at[i]))
+        copies[i].start()
     for copy in copies:
         copy.wait()
 
@@ -289,7 +292,7 @@
     wide, rows = near.shape
     part = here.shape[1]
     tall = wide // 2
-    block = 256
+    block = 896
     steps = tall // block
     start = steps if second else 0
     lhs = pl.BlockSpec((block, rows), lambda i: (start + i, 0))
@@ -308,7 +311,7 @@
 
 
 def combine_body(pieces, back_ref, pick_ref, split_ref, moe_ref, dx_ref, buf, sems):
-    width = moe_ref.shape[1]
+    count, width = moe_ref.shape
     size = width // pieces
     copies = []
     for i in range(2 * pieces):
@@ -319,9 +322,8 @@
     for i in range(pieces):
         low, high = i * size, (i + 1) * size
         copies[i].wait()
-        rows = buf[:, low:high]
-        small = mm(split_ref[1], rows, ROWS_FIRST) + mm(split_ref[2], rows, ROWS_FIRST)
-        moe = mm(split_ref[0], rows, ROWS_FIRST) + small
+        sums = mm(split_ref[...], buf[:, low:high], ROWS_FIRST)
+        moe = sums[0:count] + (sums[count : 2 * count] + sums[2 * count : 3 * count])
         moe_ref[:, low:high] = moe.astype(jnp.bfloat16)
     for i in range(pieces):
         low, high = i * size, (i + 1) * size
@@ -388,31 +390,36 @@
         (
             pltpu.HBM((places, 2 * width), jnp.bfloat16),
             bf(places, flat_rows),
-            bf(3, places, flat_rows),
+            bf(places, 3 * flat_rows),
         ),
         (
-            expert_ids.transpose(0, 2, 1),
-            route_probs.transpose(0, 2, 1),
-            copy_marks,
+            in_hbm(expert_ids.transpose(0, 2, 1)),
+            in_hbm(route_probs.transpose(0, 2, 1)),
+            in_hbm(copy_marks),
             in_hbm(tokens.reshape(flat_rows, width)),
             in_hbm(out_grad.reshape(flat_rows, width)),
         ),
         4 * places * flat_rows * width,
-        [VMEM] * 3 + [HBM] * 2,
+        [HBM] * 5,
         [HBM, VMEM, VMEM],
         (
+            pltpu.VMEM((micros, topk, tok_rows), jnp.int32),
+            pltpu.VMEM((micros, topk, tok_rows), jnp.float32),
+            pltpu.VMEM((micros, experts), jnp.int32),
             pltpu.VMEM((flat_rows, width), jnp.bfloat16),
             pltpu.VMEM((flat_rows, width), jnp.bfloat16),
             pltpu.VMEM((places, 2 * width), jnp.bfloat16),
-            pltpu.SemaphoreType.DMA((4,)),
-        ),
-    )
+            pltpu.SemaphoreType.DMA((7,)),
+        ),
+    )
+    start = ((1 - half) * half_width).reshape(1)
+    sent, start = lax.optimization_barrier((sent, start))
     own = travel(sent)
-    oth = core_swap(own)
+    oth = in_vmem(core_swap(own))
     (theirs,) = call(
         cut_body,
         (bf(places, width),),
-        (((1 - half) * half_width).reshape(1), own),
+        (start, in_hbm(own)),
         0,
         [SMEM, HBM],
         [VMEM],
@@ -426,29 +433,28 @@
         own_body(pieces, *refs)
 
     def finish(*refs):
-        dx_add_body(pieces, *refs)
-
-    buffers = (
-        pltpu.VMEM((places, width), jnp.bfloat16),
-        pltpu.VMEM((places, width), jnp.bfloat16),
-    )
+        add_body(pieces, *refs)
+
     mid = bf(places, part)
     mids = bf(2 * places, part)
     *first, wg, wu, wd = call(
         begin,
         (mid,) * 3 + (bf(width, part),) * 3,
-        (own, *map(in_hbm, (w_gate, w_up, w_down))),
+        tuple(map(in_hbm, (own, w_gate, w_up, w_down))),
         3 * unit,
         [HBM] * 4,
-        scratch=buffers + (pltpu.SemaphoreType.DMA((pieces, 5)),),
+        scratch=(
+            pltpu.VMEM((places, width), jnp.bfloat16),
+            pltpu.VMEM((places, width), jnp.bfloat16),
+            pltpu.SemaphoreType.DMA((pieces, 5)),
+        ),
     )
     hid, gg, ug = call(
         oth_body,
         (mids,) * 3,
         (oth, wg, wu, wd, *first),
         3 * unit,
-        [HBM] + [VMEM] * 6,
-        scratch=buffers + (pltpu.SemaphoreType.DMA((2,)),),
+        [VMEM] * 7,
     )
     row = bf(places, width)
     (out_oth,) = call(out_body, (row,), (hid, wd), unit, [VMEM] * 2)
@@ -459,17 +465,19 @@
     gg_there = pair_swap(gg)
     ug_there = pair_swap(ug)
 
-    (left,) = call(out_add_body, (row,), (hid, wd, out_other), unit, [VMEM] * 3)
+    (mine,) = call(
+        own_end_body, (bf(places, 2 * width),), (hid, gg, ug, wg, wu, wd), 3 * unit, [VMEM] * 6
+    )
     (total,) = call(
         finish,
         (pltpu.HBM((places, 2 * width), jnp.bfloat16),),
-        (gg, ug, wg, wu, dx_other, left),
-        2 * unit,
-        [VMEM] * 6,
+        (mine, out_other, dx_other),
+        0,
+        [VMEM] * 3,
         [HBM],
         (
-            pltpu.VMEM((places, width), jnp.bfloat16),
-            pltpu.SemaphoreType.DMA((pieces + 1,)),
+            pltpu.VMEM((places, 2 * width), jnp.bfloat16),
+            pltpu.SemaphoreType.DMA((2 * pieces,)),
         ),
     )
     back = travel(total)

time: 174 us -> 166 us (0.954)
  Pallas kernels: 56.9 us -> 47.7 us
  waiting for transfers between devices: 37.8 us -> 44.5 us
  local copies, waits for them, and re-layouts: 9.16 us -> 4.09 us
    ppermute x4, waiting for transfers between devices: 37.8 us -> 44.5 us  [pair_swap(): return lax.ppermute(x, AXES, pairs)]
    unnamed x32 -> x8, local copies, waits for them, and re-layouts: 9.16 us -> 4.09 us
    pallas_call x9, Pallas kernels: 32 us -> 27.2 us  [call(): pl.pallas_call(kernel, out_shape=outs, in_specs=in_specs, out_specs=out_s...]
    pallas_call x3, Pallas kernels: 14.8 us -> 10.4 us  [weight_grad(): pl.pallas_call(grad_body, out_shape=jax.ShapeDtypeStruct((tall, part), jn...]
  transfers between devices with their start and end apart: 9 -> 9, of which waited for: 3 -> 3; matrix products, arithmetic and copies ran while one was open for 0% -> 0% of each run, Pallas kernels for 25% -> 22%
where the time goes in v3:
time: 166 us
  blocking collectives  56.9 us (34%)
  Pallas kernels  47.7 us (29%)
  waiting for transfers between devices  44.5 us (27%)
  starting transfers between devices  11.8 us (7%)
  local copies, waits for them, and re-layouts  4.09 us (2%)
    all_to_all x1, blocking collectives, exchange(): lax.all_to_all(x, AXES, split_axis=0, concat_axis=0, tiled=True, axis_ind...  56.9 us
    ppermute x4, waiting for transfers between devices, pair_swap(): return lax.ppermute(x, AXES, pairs)  44.5 us
    pallas_call x9, Pallas kernels, call(): pl.pallas_call(kernel, out_shape=outs, in_specs=in_specs, out_specs=out_s...  27.2 us
    pallas_call x3, Pallas kernels, weight_grad(): pl.pallas_call(grad_body, out_shape=jax.ShapeDtypeStruct((tall, part), jn...  10.4 us
    pallas_call x2, Pallas kernels, turn(): pl.pallas_call(turn_body, out_shape=bf(tall, 2 * rows), grid_spec=pltpu.P...  10.1 us
    ppermute x4, starting transfers between devices, core_swap(): return lax.ppermute(x, AXES, cores)  5.2 us
    all_to_all x1, starting transfers between devices, exchange(): lax.all_to_all(x, AXES, split_axis=0, concat_axis=0, tiled=True, axis_ind...  4.85 us
    unnamed x8, local copies, waits for them, and re-layouts  4.09 us
  transfers between devices with their start and end apart: 9, of which 3 were waited for; matrix products, arithmetic and copies ran while one was open for 0% of the time, Pallas kernels for 22%

profile of v3, /device:TPU:1, one launch (start us, length us, event | category | flops | bytes accessed | tf_op | source)
XLA Modules:
  0.0 166.0 jit_solution(12527651192766471891)
XLA Ops:
  0.6 3.8 %shard_map.119 = (bf16[256,7168]{1,0:T(8,128)(2,1)}, bf16[256,32]{1,0:T(8,128)(2,1)S(1)}, bf16[256,96]{1,0:T(8,128)(2,1)S(1)}) custom-call(s32[2,4,16]{2,1,0:T(4,128)} %bitcast.20, f32[2,4,16]{2,1,0:T(4,128)} %bitcast.21, s32[2,32]{1,0:T(2,128)} %refs_2_.2, bf16[32,3584]{1,0:T(8,128)(2,1)} %bitcast.18, bf16[32,3584]{1,0:T(8,128)(2,1)} %bitcast.19), custom_call_target="tpu_custom_call" | custom-call | flops 117440512 | bytes 4195584 | tf_op jit(solution)/shard_map/pallas_call | solution.py:55
  4.5 56.9 %all_to_all.10 = bf16[32,8,7168]{2,1,0:T(8,128)(2,1)S(1)} all-to-all(bf16[32,8,7168]{2,1,0:T(8,128)(2,1)} %bitcast.17), channel_id=1, replica_groups={{0,66,4,70,8,74,12,78,16,82,20,86,24,90,28,94,32,98,36,102,40,106,44,11..., dimensions={0} | all-to-all | bytes 7340032 | tf_op jit(solution)/shard_map/all_to_all | solution.py:32
  61.3 1.8 %collective-permute-start = (bf16[256,7168]{1,0:T(8,128)(2,1)S(1)}, bf16[256,7168]{1,0:T(8,128)(2,1)S(1)}, u32[]{:S(2)}, u32[]{:S(2)}) collective-permute-start(bf16[256,7168]{1,0:T(8,128)(2,1)S(1)} %bitcast.12), channel_id=1, source_target_pairs={{0,1},{1,0},{2,3},{3,2},{4,5},{5,4},{6,7},{7,6},{8,9},{9,8},{10,11... | collective-permute-start | bytes 11010056 | tf_op jit(solution)/shard_map/ppermute | solution.py:377
  63.2 6.9 %shard_map.120 = (bf16[256,512]{1,0:T(8,128)(2,1)S(1)}, bf16[256,512]{1,0:T(8,128)(2,1)S(1)}, bf16[256,512]{1,0:T(8,128)(2,1)S(1)}, bf16[3584,512]{1,0:T(8,128)(...) custom-call(bf16[256,7168]{1,0:T(8,128)(2,1)} %bitcast.13, bf16[3584,512]{1,0:T(8,128)(2,1)} %refs_1_.1, ...), custom_call_target="tpu_custom_call" | custom-call | flops 2818572288 | bytes 26476544 | tf_op jit(solution)/shard_map/pallas_call | solution.py:55
  70.1 0.0 collective-permute-done.rows_ref.second_ref
  70.1 0.0 copy-start.2
  70.1 3.1 %shard_map.121 = (bf16[512,512]{1,0:T(8,128)(2,1)S(1)}, bf16[512,512]{1,0:T(8,128)(2,1)S(1)}, bf16[512,512]{1,0:T(8,128)(2,1)S(1)}) custom-call(bf16[256,7168]{1,0:T(8,128)(2,1)S(1)} %collective-permute-done.rows_ref.second_ref, bf16[3584,512]{1,0:T(8,128)(2,1)S(1)} %get-tuple-element.23.wg_ref, bf16[3584,512]{1,0:T(8,128)(2,1)S(1)} %get-tuple-element.24.wu_ref, ...), custom_call_target="tpu_custom_call" | custom-call | flops 2818572288 | bytes 17039360 | tf_op jit(solution)/shard_map/pallas_call | solution.py:55
  73.2 1.1 shard_map.123
  74.4 1.9 %collective-permute-start.1 = (bf16[256,3584]{1,0:T(8,128)(2,1)S(1)}, bf16[256,3584]{1,0:T(8,128)(2,1)S(1)}, u32[]{:S(2)}, u32[]{:S(2)}) collective-permute-start(bf16[256,3584]{1,0:T(8,128)(2,1)S(1)} %shard_map.123), channel_id=1, source_target_pairs={{0,1},{1,0},{2,3},{3,2},{4,5},{5,4},{6,7},{7,6},{8,9},{9,8},{10,11... | collective-permute-start | bytes 5505032 | tf_op jit(solution)/shard_map/ppermute | solution.py:377
  76.3 2.1 %shard_map.124 = bf16[256,3584]{1,0:T(8,128)(2,1)S(1)} custom-call(bf16[512,512]{1,0:T(8,128)(2,1)S(1)} %get-tuple-element.30.gg_ref.here_ref, bf16[512,512]{1,0:T(8,128)(2,1)S(1)} %get-tuple-element.31.ug_ref.here_ref, bf16[3584,512]{1,0:T(8,128)(2,1)S(1)} %get-tuple-element.23.wg_ref, bf16[3584,512]{1,0:T(8,128)(2,1)S(1)} %get-tuple-element.24.wu_ref), custom_call_target="tpu_custom_call" | custom-call | flops 1879048192 | bytes 10223616 | tf_op jit(solution)/shard_map/pallas_call | solution.py:55
  78.4 0.1 collective-permute-start.2
  78.5 1.5 shard_map.128
  80.0 0.3 collective-permute-start.3
  80.2 3.1 %shard_map.122.refs_0_ = bf16[256,7168]{1,0:T(8,128)(2,1)S(1)} custom-call(bf16[512,512]{1,0:T(8,128)(2,1)S(1)} %get-tuple-element.29.hid_ref.here_ref, bf16[512,512]{1,0:T(8,128)(2,1)S(1)} %get-tuple-element.30.gg_ref.here_ref, bf16[512,512]{1,0:T(8,128)(2,1)S(1)} %get-tuple-element.31.ug_ref.here_ref, bf16[3584,512]{1,0:T(8,128)(2,1)S(1)} %get-tuple-element.23.wg_ref, ...), custom_call_target="tpu_custom_call" | custom-call | flops 2818572288 | bytes 16252928 | tf_op jit(solution)/shard_map/pallas_call | solution.py:55
  83.3 0.0 collective-permute-done.1.refs_1_
  83.3 2.0 %shard_map.125 = bf16[256,7168]{1,0:T(8,128)(2,1)} custom-call(bf16[256,7168]{1,0:T(8,128)(2,1)S(1)} %shard_map.122.refs_0_, bf16[256,3584]{1,0:T(8,128)(2,1)S(1)} %collective-permute-done.1.refs_1_, bf16[256,3584]{1,0:T(8,128)(2,1)S(1)} %collective-permute-done.2.refs_2_), custom_call_target="tpu_custom_call" | custom-call | bytes 11010048 | tf_op jit(solution)/shard_map/pallas_call | solution.py:55
  85.3 4.9 %all-to-all-start.1 = ((bf16[32,8,7168]{2,1,0:T(8,128)(2,1)}), bf16[32,8,7168]{2,1,0:T(8,128)(2,1)}, u32[]{:S(2)}, u32[]{:S(2)}) async-start(bf16[32,8,7168]{2,1,0:T(8,128)(2,1)} %bitcast.16), calls=%async_computation.1 | async-start | bytes 7340032 | tf_op jit(solution)/shard_map/all_to_all | solution.py:32
  90.2 31.2 %collective-permute-done.3.first_ref = bf16[256,3584]{1,0:T(8,128)(2,1)} collective-permute-done((bf16[256,3584]{1,0:T(8,128)(2,1)S(1)}, bf16[256,3584]{1,0:T(8,128)(2,1)}, u32[]{:S(2)}, u32[]{:S(2)}) %collective-permute-start.3) | collective-permute-done | bytes 1835040 | tf_op jit(solution)/shard_map/ppermute | solution.py:380
  121.4 1.3 collective-permute-start.4
  122.8 0.0 collective-permute-start.5
  122.8 1.5 collective-permute-start.6
  124.2 0.0 collective-permute-start.7
  124.2 2.0 %copy-done.1 = bf16[32,8,7168]{2,1,0:T(8,128)(2,1)S(1)} copy-done((bf16[32,8,7168]{2,1,0:T(8,128)(2,1)S(1)}, bf16[32,8,7168]{2,1,0:T(8,128)(2,1)}, u32[]{:S(2)}) %copy-start.1) | copy-done | bytes 3670040
  126.3 2.0 %copy-done.3 = bf16[256,7168]{1,0:T(8,128)(2,1)S(1)} copy-done((bf16[256,7168]{1,0:T(8,128)(2,1)S(1)}, bf16[256,7168]{1,0:T(8,128)(2,1)}, u32[]{:S(2)}) %copy-start.3) | copy-done | bytes 3670040
  128.3 2.7 %shard_map.127.near_ref = bf16[3584,512]{1,0:T(8,128)(2,1)S(1)} custom-call(s32[1]{0:T(128)} %bitcast.11.half_ref, bf16[256,7168]{1,0:T(8,128)(2,1)S(1)} %bitcast.15, bf16[256,7168]{1,0:T(8,128)(2,1)S(1)} %copy-done.3), custom_call_target="tpu_custom_call" | custom-call | tf_op jit(solution)/shard_map/pallas_call | solution.py:274
  131.0 7.5 %shard_map.129.far_ref = bf16[3584,512]{1,0:T(8,128)(2,1)S(1)} custom-call(s32[1]{0:T(128)} %bitcast.11.half_ref, bf16[256,3584]{1,0:T(8,128)(2,1)} %collective-permute-done.3.first_ref, bf16[256,3584]{1,0:T(8,128)(2,1)S(1)} %collective-permute-done.4.second_ref), custom_call_target="tpu_custom_call" | custom-call | tf_op jit(solution)/shard_map/pallas_call | solution.py:274
  138.5 3.5 %shard_map.130 = f32[1792,512]{1,0:T(8,128)} custom-call(bf16[3584,512]{1,0:T(8,128)(2,1)S(1)} %shard_map.127.near_ref, bf16[3584,512]{1,0:T(8,128)(2,1)S(1)} %shard_map.129.far_ref, bf16[512,512]{1,0:T(8,128)(2,1)S(1)} %get-tuple-element.30.gg_ref.here_ref, bf16[512,512]{1,0:T(8,128)(2,1)S(1)} %collective-permute-done.5.there_ref), custom_call_target="tpu_custom_call" | custom-call | flops 1879048192 | bytes 8388608 | tf_op jit(solution)/shard_map/pallas_call | solution.py:300
  142.0 5.5 %collective-permute-done.6.there_ref = bf16[512,512]{1,0:T(8,128)(2,1)S(1)} collective-permute-done((bf16[512,512]{1,0:T(8,128)(2,1)S(1)}, bf16[512,512]{1,0:T(8,128)(2,1)S(1)}, u32[]{:S(2)}, u32[]{:S(2)}) %collective-permute-start.6) | collective-permute-done | bytes 524320 | tf_op jit(solution)/shard_map/ppermute | solution.py:380
  147.5 3.5 %shard_map.131 = f32[1792,512]{1,0:T(8,128)} custom-call(bf16[3584,512]{1,0:T(8,128)(2,1)S(1)} %shard_map.127.near_ref, bf16[3584,512]{1,0:T(8,128)(2,1)S(1)} %shard_map.129.far_ref, bf16[512,512]{1,0:T(8,128)(2,1)S(1)} %get-tuple-element.31.ug_ref.here_ref, bf16[512,512]{1,0:T(8,128)(2,1)S(1)} %collective-permute-done.6.there_ref), custom_call_target="tpu_custom_call" | custom-call | flops 1879048192 | bytes 8388608 | tf_op jit(solution)/shard_map/pallas_call | solution.py:300
  150.9 7.8 %collective-permute-done.7.there_ref = bf16[512,512]{1,0:T(8,128)(2,1)S(1)} collective-permute-done((bf16[512,512]{1,0:T(8,128)(2,1)S(1)}, bf16[512,512]{1,0:T(8,128)(2,1)S(1)}, u32[]{:S(2)}, u32[]{:S(2)}) %collective-permute-start.7) | collective-permute-done | bytes 524320 | tf_op jit(solution)/shard_map/ppermute | solution.py:380
  158.7 3.5 %shard_map.132 = f32[1792,512]{1,0:T(8,128)} custom-call(bf16[3584,512]{1,0:T(8,128)(2,1)S(1)} %shard_map.127.near_ref, bf16[3584,512]{1,0:T(8,128)(2,1)S(1)} %shard_map.129.far_ref, bf16[512,512]{1,0:T(8,128)(2,1)S(1)} %get-tuple-element.29.hid_ref.here_ref, bf16[512,512]{1,0:T(8,128)(2,1)S(1)} %collective-permute-done.7.there_ref), custom_call_target="tpu_custom_call" | custom-call | flops 1879048192 | bytes 8388608 | tf_op jit(solution)/shard_map/pallas_call | solution.py:300
  162.2 3.6 %shard_map.126 = (bf16[32,3584]{1,0:T(8,128)(2,1)}, bf16[32,3584]{1,0:T(8,128)(2,1)}) custom-call(bf16[256,7168]{1,0:T(8,128)(2,1)} %bitcast.8.refs_0_, bf16[256,32]{1,0:T(8,128)(2,1)S(1)} %get-tuple-element.32.refs_1_, bf16[256,96]{1,0:T(8,128)(2,1)S(1)} %get-tuple-element.33.refs_2_), custom_call_target="tpu_custom_call" | custom-call | flops 234881024 | bytes 4194304 | tf_op jit(solution)/shard_map/pallas_call | solution.py:55
  (9 shorter events, 0.0 us)
Async XLA Ops:
  61.3 1.9 %copy-start = (bf16[32,8,7168]{2,1,0:T(8,128)(2,1)}, bf16[32,8,7168]{2,1,0:T(8,128)(2,1)S(1)}, u32[]{:S(2)}) copy-start(bf16[32,8,7168]{2,1,0:T(8,128)(2,1)S(1)} %all_to_all.10) | copy-start | bytes 11010052
  61.3 8.8 %collective-permute-start = (bf16[256,7168]{1,0:T(8,128)(2,1)S(1)}, bf16[256,7168]{1,0:T(8,128)(2,1)S(1)}, u32[]{:S(2)}, u32[]{:S(2)}) collective-permute-start(bf16[256,7168]{1,0:T(8,128)(2,1)S(1)} %bitcast.12), channel_id=1, source_target_pairs={{0,1},{1,0},{2,3},{3,2},{4,5},{5,4},{6,7},{7,6},{8,9},{9,8},{10,11... | collective-permute-start | bytes 11010056 | tf_op jit(solution)/shard_map/ppermute | solution.py:377
  70.1 3.1 %copy-start.2 = (bf16[256,7168]{1,0:T(8,128)(2,1)}, bf16[256,7168]{1,0:T(8,128)(2,1)S(1)}, u32[]{:S(2)}) copy-start(bf16[256,7168]{1,0:T(8,128)(2,1)S(1)} %collective-permute-done.rows_ref.second_ref) | copy-start | bytes 11010052
  74.4 8.9 %collective-permute-start.1 = (bf16[256,3584]{1,0:T(8,128)(2,1)S(1)}, bf16[256,3584]{1,0:T(8,128)(2,1)S(1)}, u32[]{:S(2)}, u32[]{:S(2)}) collective-permute-start(bf16[256,3584]{1,0:T(8,128)(2,1)S(1)} %shard_map.123), channel_id=1, source_target_pairs={{0,1},{1,0},{2,3},{3,2},{4,5},{5,4},{6,7},{7,6},{8,9},{9,8},{10,11... | collective-permute-start | bytes 5505032 | tf_op jit(solution)/shard_map/ppermute | solution.py:377
  78.4 4.9 %collective-permute-start.2 = (bf16[256,3584]{1,0:T(8,128)(2,1)S(1)}, bf16[256,3584]{1,0:T(8,128)(2,1)S(1)}, u32[]{:S(2)}, u32[]{:S(2)}) collective-permute-start(bf16[256,3584]{1,0:T(8,128)(2,1)S(1)} %shard_map.124), channel_id=1, source_target_pairs={{0,1},{1,0},{2,3},{3,2},{4,5},{5,4},{6,7},{7,6},{8,9},{9,8},{10,11... | collective-permute-start | bytes 5505032 | tf_op jit(solution)/shard_map/ppermute | solution.py:377
  80.0 41.4 %collective-permute-start.3 = (bf16[256,3584]{1,0:T(8,128)(2,1)S(1)}, bf16[256,3584]{1,0:T(8,128)(2,1)}, u32[]{:S(2)}, u32[]{:S(2)}) collective-permute-start(bf16[256,3584]{1,0:T(8,128)(2,1)S(1)} %shard_map.128), channel_id=1, source_target_pairs={{0,64},{1,65},{2,66},{3,67},{4,68},{5,69},{6,70},{7,71},{8,72},{9,... | collective-permute-start | bytes 5505032 | tf_op jit(solution)/shard_map/ppermute | solution.py:380
  85.3 76.9 %all-to-all-start.1 = ((bf16[32,8,7168]{2,1,0:T(8,128)(2,1)}), bf16[32,8,7168]{2,1,0:T(8,128)(2,1)}, u32[]{:S(2)}, u32[]{:S(2)}) async-start(bf16[32,8,7168]{2,1,0:T(8,128)(2,1)} %bitcast.16), calls=%async_computation.1 | async-start | bytes 7340032 | tf_op jit(solution)/shard_map/all_to_all | solution.py:32
  121.4 9.6 %collective-permute-start.4 = (bf16[256,3584]{1,0:T(8,128)(2,1)}, bf16[256,3584]{1,0:T(8,128)(2,1)S(1)}, u32[]{:S(2)}, u32[]{:S(2)}) collective-permute-start(bf16[256,3584]{1,0:T(8,128)(2,1)} %collective-permute-done.3.first_ref), channel_id=1, source_target_pairs={{0,1},{1,0},{2,3},{3,2},{4,5},{5,4},{6,7},{7,6},{8,9},{9,8},{10,11... | collective-permute-start | bytes 5505032 | tf_op jit(solution)/shard_map/ppermute | solution.py:377
  122.8 15.7 %collective-permute-start.5 = (bf16[512,512]{1,0:T(8,128)(2,1)S(1)}, bf16[512,512]{1,0:T(8,128)(2,1)S(1)}, u32[]{:S(2)}, u32[]{:S(2)}) collective-permute-start(bf16[512,512]{1,0:T(8,128)(2,1)S(1)} %get-tuple-element.30.gg_ref.here_ref), channel_id=1, source_target_pairs={{0,64},{1,65},{2,66},{3,67},{4,68},{5,69},{6,70},{7,71},{8,72},{9,... | collective-permute-start | bytes 1572872 | tf_op jit(solution)/shard_map/ppermute | solution.py:380
  122.8 24.7 %collective-permute-start.6 = (bf16[512,512]{1,0:T(8,128)(2,1)S(1)}, bf16[512,512]{1,0:T(8,128)(2,1)S(1)}, u32[]{:S(2)}, u32[]{:S(2)}) collective-permute-start(bf16[512,512]{1,0:T(8,128)(2,1)S(1)} %get-tuple-element.31.ug_ref.here_ref), channel_id=1, source_target_pairs={{0,64},{1,65},{2,66},{3,67},{4,68},{5,69},{6,70},{7,71},{8,72},{9,... | collective-permute-start | bytes 1572872 | tf_op jit(solution)/shard_map/ppermute | solution.py:380
  124.2 34.5 %collective-permute-start.7 = (bf16[512,512]{1,0:T(8,128)(2,1)S(1)}, bf16[512,512]{1,0:T(8,128)(2,1)S(1)}, u32[]{:S(2)}, u32[]{:S(2)}) collective-permute-start(bf16[512,512]{1,0:T(8,128)(2,1)S(1)} %get-tuple-element.29.hid_ref.here_ref), channel_id=1, source_target_pairs={{0,64},{1,65},{2,66},{3,67},{4,68},{5,69},{6,70},{7,71},{8,72},{9,... | collective-permute-start | bytes 1572872 | tf_op jit(solution)/shard_map/ppermute | solution.py:380
  124.2 2.0 %copy-start.1 = (bf16[32,8,7168]{2,1,0:T(8,128)(2,1)S(1)}, bf16[32,8,7168]{2,1,0:T(8,128)(2,1)}, u32[]{:S(2)}) copy-start(bf16[32,8,7168]{2,1,0:T(8,128)(2,1)} %copy-done) | copy-start | bytes 11010052
  126.3 2.0 %copy-start.3 = (bf16[256,7168]{1,0:T(8,128)(2,1)S(1)}, bf16[256,7168]{1,0:T(8,128)(2,1)}, u32[]{:S(2)}) copy-start(bf16[256,7168]{1,0:T(8,128)(2,1)} %copy-done.2) | copy-start | bytes 11010052

commit v4 on v3

--- a/solution.py
+++ b/solution.py
@@ -12,7 +12,6 @@
 AXES = ("dp", "expert")
 PLAIN = (((1,), (0,)), ((), ()))
 CONTRACT = (((1,), (1,)), ((), ()))
-ROWS_FIRST = (((0,), (0,)), ((), ()))
 VMEM = pl.BlockSpec(memory_space=pltpu.VMEM)
 SMEM = pl.BlockSpec(memory_space=pltpu.SMEM)
 HBM = pl.BlockSpec(memory_space=pltpu.HBM)
@@ -50,7 +49,7 @@
     return pltpu.with_memory_space_constraint(x, pltpu.HBM)
 
 
-def call(kernel, outs, ins, flops, in_specs, out_specs=None, scratch=()):
+def call(kernel, outs, ins, flops, in_specs, out_specs=None, scratch=(), aliases=None):
     size = sum(math.prod(x.shape) * x.dtype.itemsize for x in tuple(ins) + tuple(outs))
     return pl.pallas_call(
         kernel,
@@ -58,13 +57,14 @@
         in_specs=in_specs,
         out_specs=out_specs or [VMEM] * len(outs),
         scratch_shapes=list(scratch),
+        input_output_aliases=aliases or {},
         compiler_params=pltpu.CompilerParams(vmem_limit_bytes=28 << 20),
         cost_estimate=pl.CostEstimate(flops=flops, bytes_accessed=size, transcendentals=0),
     )(*ins)
 
 
-def pack_body(slots, capacity, ids_hbm, prob_hbm, marks_hbm, tok_ref, cot_ref,
-              sent_ref, pick_ref, split_ref, ids_ref, prob_ref, marks_ref,
+def pack_body(slots, capacity, ids_hbm, prob_hbm, marks_hbm, tok_ref, cot_ref, wg_ref,
+              sent_ref, pick_ref, split_ref, wg_out, ids_ref, prob_ref, marks_ref,
               tok_buf, cot_buf, buf, sems):
     small = [
         pltpu.make_async_copy(a, b, sems.at[4 + i])
@@ -82,6 +82,8 @@
     fetch_cot = pltpu.make_async_copy(cot_ref, cot_buf, sems.at[1])
     fetch_tok.start()
     fetch_cot.start()
+    weight = pltpu.make_async_copy(wg_ref, wg_out, sems.at[7])
+    weight.start()
     for copy in small:
         copy.wait()
     ids = jnp.concatenate([ids_ref[m] for m in range(micros)], axis=1)
@@ -112,10 +114,10 @@
     chosen = (hit > 0.5) & (micro == token // per_micro) & (ranked < limit)
     chosen = chosen & (ranked == (place % slots).astype(jnp.float32))
     picked = jnp.where(chosen, 1.0, 0.0).astype(jnp.bfloat16)
-    weight = jnp.where(chosen, prob, 0.0)
-    slot_prob = jnp.sum(weight, axis=1, keepdims=True)
-    high = weight.astype(jnp.bfloat16)
-    rest = weight - high.astype(jnp.float32)
+    mixing = jnp.where(chosen, prob, 0.0)
+    slot_prob = jnp.sum(mixing, axis=1, keepdims=True)
+    high = mixing.astype(jnp.bfloat16)
+    rest = mixing - high.astype(jnp.float32)
     middle = rest.astype(jnp.bfloat16)
     low = (rest - middle.astype(jnp.float32)).astype(jnp.bfloat16)
     pick_ref[...] = picked
@@ -136,6 +138,7 @@
     second.start()
     first.wait()
     second.wait()
+    weight.wait()
 
 
 def cut_body(start_ref, rows_ref, out_ref, sems):
@@ -166,37 +169,32 @@
     return hidden, gate_grad, up_grad
 
 
-def own_body(pieces, rows_ref, wg_ref, wu_ref, wd_ref, hid_ref, gg_ref, ug_ref,
-             wg_out, wu_out, wd_out, xbuf, cbuf, sems):
+def own_body(pieces, rows_ref, wg_ref, wu_ref, wd_ref, hid_ref, gg_ref, ug_ref, wu_out, wd_out,
+             sems):
     width = wg_ref.shape[0]
     size = width // pieces
-    fetches = []
-    for i in range(pieces):
-        low = i * size
-        span = pl.ds(low, size)
-        moves = (
-            (rows_ref.at[:, span], xbuf.at[:, span]),
-            (wg_ref.at[span, :], wg_out.at[span, :]),
-            (wu_ref.at[span, :], wu_out.at[span, :]),
-            (rows_ref.at[:, pl.ds(width + low, size)], cbuf.at[:, span]),
-            (wd_ref.at[span, :], wd_out.at[span, :]),
-        )
-        fetches.append(
-            [pltpu.make_async_copy(a, b, sems.at[i, k]) for k, (a, b) in enumerate(moves)]
-        )
+    fetches = [
+        [
+            pltpu.make_async_copy(
+                w.at[pl.ds(i * size, size), :], out.at[pl.ds(i * size, size), :], sems.at[i, k]
+            )
+            for i in range(pieces)
+        ]
+        for k, (w, out) in enumerate(((wu_ref, wu_out), (wd_ref, wd_out)))
+    ]
     for fetch in fetches:
         for copy in fetch:
             copy.start()
-    gate_pre = up_pre = hidden_grad = 0.0
-    for i in range(pieces):
-        low, high = i * size, (i + 1) * size
-        for copy in fetches[i]:
-            copy.wait()
-        x = xbuf[:, low:high]
-        gate_pre = gate_pre + mm(x, wg_out[low:high, :])
-        up_pre = up_pre + mm(x, wu_out[low:high, :])
-        hidden_grad = hidden_grad + mm(cbuf[:, low:high], wd_out[low:high, :])
-    values = slopes(gate_pre, up_pre, hidden_grad)
+    gate_pre = mm(rows_ref[:, 0:width], wg_ref[...])
+    results = []
+    for k, out in enumerate((wu_out, wd_out)):
+        total = 0.0
+        for i in range(pieces):
+            low, high = i * size, (i + 1) * size
+            fetches[k][i].wait()
+            total = total + mm(rows_ref[:, k * width + low : k * width + high], out[low:high, :])
+        results.append(total)
+    values = slopes(gate_pre, *results)
     for ref, value in zip((hid_ref, gg_ref, ug_ref), values):
         ref[...] = value
 
@@ -228,31 +226,45 @@
     dx_ref[...] = dx.astype(jnp.bfloat16)
 
 
-def own_end_body(hid_ref, gg_ref, ug_ref, wg_ref, wu_ref, wd_ref, out_ref):
-    rows, double = out_ref.shape
-    width = double // 2
-    out = mm(hid_ref[0:rows, :], wd_ref[...], CONTRACT)
-    out_ref[:, 0:width] = out.astype(jnp.bfloat16)
+def own_dx_body(gg_ref, ug_ref, wg_ref, wu_ref, dx_ref):
+    rows = dx_ref.shape[0]
     dx = mm(gg_ref[0:rows, :], wg_ref[...], CONTRACT)
     dx = dx + mm(ug_ref[0:rows, :], wu_ref[...], CONTRACT)
-    out_ref[:, width:double] = dx.astype(jnp.bfloat16)
-
-
-def add_body(pieces, part_ref, out_ref, dx_ref, total_ref, buf, sems):
-    width = out_ref.shape[1]
-    size = width // pieces
+    dx_ref[...] = dx.astype(jnp.bfloat16)
+
+
+def store_sums(pieces, part_of, other_ref, total_ref, start, buf, sems):
+    size = other_ref.shape[1] // pieces
     copies = []
-    for i in range(2 * pieces):
-        low = i * size
-        source = out_ref if i < pieces else dx_ref
-        there = source[:, low % width : low % width + size].astype(jnp.float32)
-        here = part_ref[:, low : low + size].astype(jnp.float32)
-        buf[:, low : low + size] = (here + there).astype(jnp.bfloat16)
-        span = pl.ds(low, size)
-        copies.append(pltpu.make_async_copy(buf.at[:, span], total_ref.at[:, span], sems.at[i]))
+    for i in range(pieces):
+        low, high = i * size, (i + 1) * size
+        here = part_of(low, high).astype(jnp.bfloat16).astype(jnp.float32)
+        there = other_ref[:, low:high].astype(jnp.float32)
+        buf[:, low:high] = (here + there).astype(jnp.bfloat16)
+        copies.append(
+            pltpu.make_async_copy(
+                buf.at[:, pl.ds(low, size)], total_ref.at[:, pl.ds(start + low, size)], sems.at[i]
+            )
+        )
         copies[i].start()
     for copy in copies:
         copy.wait()
+
+
+def own_out_body(pieces, hid_ref, wd_ref, other_ref, total_ref, buf, sems):
+    hidden = hid_ref[0 : other_ref.shape[0], :]
+
+    def part_of(low, high):
+        return mm(hidden, wd_ref[low:high, :], CONTRACT)
+
+    store_sums(pieces, part_of, other_ref, total_ref, 0, buf, sems)
+
+
+def add_body(pieces, half_ref, dx_ref, other_ref, total_ref, buf, sems):
+    def part_of(low, high):
+        return dx_ref[:, low:high]
+
+    store_sums(pieces, part_of, other_ref, total_ref, other_ref.shape[1], buf, sems)
 
 
 def turn_body(half_ref, first_ref, second_ref, out_ref):
@@ -310,6 +322,23 @@
     )(near, far, here, there)
 
 
+def near_body(near_ref, here_ref, sum_ref):
+    sum_ref[...] = mm(near_ref[0 : sum_ref.shape[0], :], here_ref[...])
+
+
+def far_body(pieces, sum_ref, far_ref, there_ref, out_ref, buf, sems):
+    size = sum_ref.shape[0] // pieces
+    copies = []
+    for i in range(pieces):
+        low, high = i * size, (i + 1) * size
+        buf[low:high, :] = sum_ref[low:high, :] + mm(far_ref[low:high, :], there_ref[...])
+        span = pl.ds(low, size)
+        copies.append(pltpu.make_async_copy(buf.at[span, :], out_ref.at[span, :], sems.at[i]))
+        copies[i].start()
+    for copy in copies:
+        copy.wait()
+
+
 def combine_body(pieces, back_ref, pick_ref, split_ref, moe_ref, dx_ref, buf, sems):
     count, width = moe_ref.shape
     size = width // pieces
@@ -319,16 +348,18 @@
         copies.append(pltpu.make_async_copy(back_ref.at[:, span], buf.at[:, span], sems.at[i]))
     for copy in copies:
         copy.start()
+    split = split_ref[...].T
+    picked = pick_ref[...].T
     for i in range(pieces):
         low, high = i * size, (i + 1) * size
         copies[i].wait()
-        sums = mm(split_ref[...], buf[:, low:high], ROWS_FIRST)
+        sums = mm(split, buf[:, low:high])
         moe = sums[0:count] + (sums[count : 2 * count] + sums[2 * count : 3 * count])
         moe_ref[:, low:high] = moe.astype(jnp.bfloat16)
     for i in range(pieces):
         low, high = i * size, (i + 1) * size
         copies[pieces + i].wait()
-        dx = mm(pick_ref[...], buf[:, width + low : width + high], ROWS_FIRST)
+        dx = mm(picked, buf[:, width + low : width + high])
         dx_ref[:, low:high] = dx.astype(jnp.bfloat16)
 
 
@@ -385,12 +416,13 @@
     def pack(*refs):
         pack_body(slots, capacity, *refs)
 
-    sent, picked, split = call(
+    sent, picked, split, wg = call(
         pack,
         (
             pltpu.HBM((places, 2 * width), jnp.bfloat16),
             bf(places, flat_rows),
             bf(places, 3 * flat_rows),
+            pltpu.VMEM((width, part), jnp.bfloat16),
         ),
         (
             in_hbm(expert_ids.transpose(0, 2, 1)),
@@ -398,10 +430,11 @@
             in_hbm(copy_marks),
             in_hbm(tokens.reshape(flat_rows, width)),
             in_hbm(out_grad.reshape(flat_rows, width)),
+            in_hbm(w_gate),
         ),
         4 * places * flat_rows * width,
-        [HBM] * 5,
-        [HBM, VMEM, VMEM],
+        [HBM] * 6,
+        [HBM] + [VMEM] * 3,
         (
             pltpu.VMEM((micros, topk, tok_rows), jnp.int32),
             pltpu.VMEM((micros, topk, tok_rows), jnp.float32),
@@ -409,13 +442,15 @@
             pltpu.VMEM((flat_rows, width), jnp.bfloat16),
             pltpu.VMEM((flat_rows, width), jnp.bfloat16),
             pltpu.VMEM((places, 2 * width), jnp.bfloat16),
-            pltpu.SemaphoreType.DMA((7,)),
+            pltpu.SemaphoreType.DMA((8,)),
         ),
     )
     start = ((1 - half) * half_width).reshape(1)
     sent, start = lax.optimization_barrier((sent, start))
+    wg = in_vmem(wg)
     own = travel(sent)
-    oth = in_vmem(core_swap(own))
+    own_near = in_vmem(own)
+    oth = in_vmem(core_swap(own_near))
     (theirs,) = call(
         cut_body,
         (bf(places, width),),
@@ -432,22 +467,21 @@
     def begin(*refs):
         own_body(pieces, *refs)
 
-    def finish(*refs):
+    def finish_out(*refs):
+        own_out_body(pieces, *refs)
+
+    def finish_dx(*refs):
         add_body(pieces, *refs)
 
     mid = bf(places, part)
     mids = bf(2 * places, part)
-    *first, wg, wu, wd = call(
+    *first, wu, wd = call(
         begin,
-        (mid,) * 3 + (bf(width, part),) * 3,
-        tuple(map(in_hbm, (own, w_gate, w_up, w_down))),
+        (mid,) * 3 + (bf(width, part),) * 2,
+        (own_near, wg, in_hbm(w_up), in_hbm(w_down)),
         3 * unit,
-        [HBM] * 4,
-        scratch=(
-            pltpu.VMEM((places, width), jnp.bfloat16),
-            pltpu.VMEM((places, width), jnp.bfloat16),
-            pltpu.SemaphoreType.DMA((pieces, 5)),
-        ),
+        [VMEM, VMEM, HBM, HBM],
+        scratch=(pltpu.SemaphoreType.DMA((pieces, 2)),),
     )
     hid, gg, ug = call(
         oth_body,
@@ -465,20 +499,24 @@
     gg_there = pair_swap(gg)
     ug_there = pair_swap(ug)
 
-    (mine,) = call(
-        own_end_body, (bf(places, 2 * width),), (hid, gg, ug, wg, wu, wd), 3 * unit, [VMEM] * 6
-    )
+    room = (
+        pltpu.VMEM((places, width), jnp.bfloat16),
+        pltpu.SemaphoreType.DMA((pieces,)),
+    )
+    joined = (pltpu.HBM((places, 2 * width), jnp.bfloat16),)
+    (dx_own,) = call(own_dx_body, (row,), (gg, ug, wg, wu), 2 * unit, [VMEM] * 4)
     (total,) = call(
-        finish,
-        (pltpu.HBM((places, 2 * width), jnp.bfloat16),),
-        (mine, out_other, dx_other),
+        finish_out, joined, (hid, wd, out_other), unit, [VMEM] * 3, [HBM], room
+    )
+    (total,) = call(
+        finish_dx,
+        joined,
+        (total, dx_own, dx_other),
         0,
-        [VMEM] * 3,
+        [HBM, VMEM, VMEM],
         [HBM],
-        (
-            pltpu.VMEM((places, 2 * width), jnp.bfloat16),
-            pltpu.SemaphoreType.DMA((2 * pieces,)),
-        ),
+        room,
+        aliases={0: 0},
     )
     back = travel(total)
     pair_oth = core_swap(pair_own)
@@ -487,7 +525,29 @@
     far = turn(h, pair_own, pair_oth, True)
     grad_down = weight_grad(near, far, hid, hid_there, True)
     grad_gate = weight_grad(near, far, gg, gg_there, False)
-    grad_up = weight_grad(near, far, ug, ug_there, False)
+    (up_near,) = call(
+        near_body,
+        (pltpu.VMEM((half_width, part), jnp.float32),),
+        (near, ug),
+        2 * unit // n_dp,
+        [VMEM] * 2,
+    )
+
+    def up_far(*refs):
+        far_body(pieces, *refs)
+
+    (grad_up,) = call(
+        up_far,
+        (pltpu.HBM((half_width, part), jnp.float32),),
+        (in_vmem(up_near), far, ug_there),
+        2 * unit // n_dp,
+        [VMEM] * 3,
+        [HBM],
+        (
+            pltpu.VMEM((half_width, part), jnp.float32),
+            pltpu.SemaphoreType.DMA((pieces,)),
+        ),
+    )
     moe, grad_in = combine(back, picked, split, pieces)
     return (
         moe.reshape(micros, tok_rows, width),

time: 166 us -> 164 us (0.988)
  Pallas kernels: 47.7 us -> 45.7 us
    pallas_call x3 -> x2, Pallas kernels: 10.4 us -> 6.92 us  [weight_grad(): pl.pallas_call(grad_body, out_shape=jax.ShapeDtypeStruct((tall, part), jn...]
    pallas_call x9 -> x12, Pallas kernels: 27.2 us -> 28.7 us  [call(): pl.pallas_call(kernel, out_shape=outs, in_specs=in_specs, out_specs=out_s...]
  transfers between devices with their start and end apart: 9 -> 9, of which waited for: 3 -> 4; matrix products, arithmetic and copies ran while one was open for 0% -> 0% of each run, Pallas kernels for 22% -> 21%
where the time goes in v4:
time: 164 us
  blocking collectives  56.9 us (35%)
  Pallas kernels  45.7 us (28%)
  waiting for transfers between devices  45.6 us (28%)
  starting transfers between devices  10.3 us (6%)
  local copies, waits for them, and re-layouts  4.08 us (2%)
    all_to_all x1, blocking collectives, exchange(): lax.all_to_all(x, AXES, split_axis=0, concat_axis=0, tiled=True, axis_ind...  56.9 us
    ppermute x4, waiting for transfers between devices, pair_swap(): return lax.ppermute(x, AXES, pairs)  44 us
    pallas_call x12, Pallas kernels, call(): pl.pallas_call(kernel, out_shape=outs, in_specs=in_specs, out_specs=out_s...  28.7 us
    pallas_call x2, Pallas kernels, turn(): pl.pallas_call(turn_body, out_shape=bf(tall, 2 * rows), grid_spec=pltpu.P...  10.1 us
    pallas_call x2, Pallas kernels, weight_grad(): pl.pallas_call(grad_body, out_shape=jax.ShapeDtypeStruct((tall, part), jn...  6.92 us
    all_to_all x1, starting transfers between devices, exchange(): lax.all_to_all(x, AXES, split_axis=0, concat_axis=0, tiled=True, axis_ind...  4.85 us
    unnamed x8, local copies, waits for them, and re-layouts  4.08 us
    ppermute x4, starting transfers between devices, core_swap(): return lax.ppermute(x, AXES, cores)  3.7 us
  transfers between devices with their start and end apart: 9, of which 4 were waited for; matrix products, arithmetic and copies ran while one was open for 0% of the time, Pallas kernels for 21%

profile of v4, /device:TPU:1, one launch (start us, length us, event | category | flops | bytes accessed | tf_op | source)
XLA Modules:
  0.0 163.6 jit_solution(585122998755970805)
XLA Ops:
  0.6 3.8 %shard_map.119 = (bf16[256,7168]{1,0:T(8,128)(2,1)}, bf16[256,32]{1,0:T(8,128)(2,1)S(1)}, bf16[256,96]{1,0:T(8,128)(2,1)S(1)}, bf16[3584,512]{1,0:T(8,128)(2,1)S(1)}) custom-call(s32[2,4,16]{2,1,0:T(4,128)} %bitcast.20, f32[2,4,16]{2,1,0:T(4,128)} %bitcast.21, s32[2,32]{1,0:T(2,128)} %refs_2_.2, bf16[32,3584]{1,0:T(8,128)(2,1)} %bitcast.18, ...), custom_call_target="tpu_custom_call" | custom-call | flops 117440512 | bytes 11535616 | tf_op jit(solution)/shard_map/pallas_call | solution.py:54
  4.5 56.9 %all_to_all.10 = bf16[32,8,7168]{2,1,0:T(8,128)(2,1)S(1)} all-to-all(bf16[32,8,7168]{2,1,0:T(8,128)(2,1)} %bitcast.17), channel_id=1, replica_groups={{0,66,4,70,8,74,12,78,16,82,20,86,24,90,28,94,32,98,36,102,40,106,44,11..., dimensions={0} | all-to-all | bytes 7340032 | tf_op jit(solution)/shard_map/all_to_all | solution.py:31
  61.4 1.8 %collective-permute-start = (bf16[256,7168]{1,0:T(8,128)(2,1)S(1)}, bf16[256,7168]{1,0:T(8,128)(2,1)S(1)}, u32[]{:S(2)}, u32[]{:S(2)}) collective-permute-start(bf16[256,7168]{1,0:T(8,128)(2,1)S(1)} %bitcast.12), channel_id=1, source_target_pairs={{0,1},{1,0},{2,3},{3,2},{4,5},{5,4},{6,7},{7,6},{8,9},{9,8},{10,11... | collective-permute-start | bytes 11010056 | tf_op jit(solution)/shard_map/ppermute | solution.py:408
  63.2 4.4 %shard_map.120 = (bf16[256,512]{1,0:T(8,128)(2,1)S(1)}, bf16[256,512]{1,0:T(8,128)(2,1)S(1)}, bf16[256,512]{1,0:T(8,128)(2,1)S(1)}, bf16[3584,512]{1,0:T(8,128)(2,1)S(1)}, bf16[3584,512]{1,0:T(8,128)(2,1)S(1)}) custom-call(bf16[256,7168]{1,0:T(8,128)(2,1)S(1)} %bitcast.13, bf16[3584,512]{1,0:T(8,128)(2,1)S(1)} %get-tuple-element.23.refs_1_.wg_ref, ...), custom_call_target="tpu_custom_call" | custom-call | flops 2818572288 | bytes 22806528 | tf_op jit(solution)/shard_map/pallas_call | solution.py:54
  67.7 1.6 collective-permute-done.rows_ref.second_ref
  69.2 3.1 %shard_map.121 = (bf16[512,512]{1,0:T(8,128)(2,1)S(1)}, bf16[512,512]{1,0:T(8,128)(2,1)S(1)}, bf16[512,512]{1,0:T(8,128)(2,1)S(1)}) custom-call(bf16[256,7168]{1,0:T(8,128)(2,1)S(1)} %collective-permute-done.rows_ref.second_ref, bf16[3584,512]{1,0:T(8,128)(2,1)S(1)} %get-tuple-element.23.refs_1_.wg_ref, bf16[3584,512]{1,0:T(8,128)(2,1)S(1)} %get-tuple-element.24.wu_ref, ...), custom_call_target="tpu_custom_call" | custom-call | flops 2818572288 | bytes 17039360 | tf_op jit(solution)/shard_map/pallas_call | solution.py:54
  72.3 1.2 shard_map.122
  73.5 0.5 collective-permute-start.1
  74.0 2.1 %shard_map.125 = bf16[256,3584]{1,0:T(8,128)(2,1)S(1)} custom-call(bf16[512,512]{1,0:T(8,128)(2,1)S(1)} %get-tuple-element.30.gg_ref.here_ref, bf16[512,512]{1,0:T(8,128)(2,1)S(1)} %get-tuple-element.31.ug_ref.here_ref, bf16[3584,512]{1,0:T(8,128)(2,1)S(1)} %get-tuple-element.23.refs_1_.wg_ref, bf16[3584,512]{1,0:T(8,128)(2,1)S(1)} %get-tuple-element.24.wu_ref), custom_call_target="tpu_custom_call" | custom-call | flops 1879048192 | bytes 10223616 | tf_op jit(solution)/shard_map/pallas_call | solution.py:54
  76.1 0.2 collective-permute-start.2
  76.3 1.5 shard_map.129
  77.8 0.3 collective-permute-start.3
  78.0 2.1 %shard_map.124.refs_1_ = bf16[256,3584]{1,0:T(8,128)(2,1)S(1)} custom-call(bf16[512,512]{1,0:T(8,128)(2,1)S(1)} %get-tuple-element.30.gg_ref.here_ref, bf16[512,512]{1,0:T(8,128)(2,1)S(1)} %get-tuple-element.31.ug_ref.here_ref, bf16[3584,512]{1,0:T(8,128)(2,1)S(1)} %get-tuple-element.23.refs_1_.wg_ref, bf16[3584,512]{1,0:T(8,128)(2,1)S(1)} %get-tuple-element.24.wu_ref), custom_call_target="tpu_custom_call" | custom-call | flops 1879048192 | bytes 10223616 | tf_op jit(solution)/shard_map/pallas_call | solution.py:54
  80.2 2.2 %shard_map.123.refs_0_ = bf16[256,7168]{1,0:T(8,128)(2,1)} custom-call(bf16[512,512]{1,0:T(8,128)(2,1)S(1)} %get-tuple-element.29.hid_ref.refs_0_.here_ref, bf16[3584,512]{1,0:T(8,128)(2,1)S(1)} %get-tuple-element.25.wd_ref.refs_1_, bf16[256,3584]{1,0:T(8,128)(2,1)S(1)} %collective-permute-done.1.refs_2_), custom_call_target="tpu_custom_call" | custom-call | flops 939524096 | bytes 9699328 | tf_op jit(solution)/shard_map/pallas_call | solution.py:54
  82.4 1.4 shard_map.126
  83.8 4.9 %all-to-all-start.1 = ((bf16[32,8,7168]{2,1,0:T(8,128)(2,1)}), bf16[32,8,7168]{2,1,0:T(8,128)(2,1)}, u32[]{:S(2)}, u32[]{:S(2)}) async-start(bf16[32,8,7168]{2,1,0:T(8,128)(2,1)} %bitcast.16), calls=%async_computation.1 | async-start | bytes 7340032 | tf_op jit(solution)/shard_map/all_to_all | solution.py:31
  88.6 30.7 %collective-permute-done.3.first_ref = bf16[256,3584]{1,0:T(8,128)(2,1)} collective-permute-done((bf16[256,3584]{1,0:T(8,128)(2,1)S(1)}, bf16[256,3584]{1,0:T(8,128)(2,1)}, u32[]{:S(2)}, u32[]{:S(2)}) %collective-permute-start.3) | collective-permute-done | bytes 1835040 | tf_op jit(solution)/shard_map/ppermute | solution.py:411
  119.3 1.2 collective-permute-start.4
  120.6 0.0 collective-permute-start.6
  120.6 1.5 collective-permute-start.5
  122.0 0.0 collective-permute-start.7
  122.0 2.0 %copy-done.1 = bf16[32,8,7168]{2,1,0:T(8,128)(2,1)S(1)} copy-done((bf16[32,8,7168]{2,1,0:T(8,128)(2,1)S(1)}, bf16[32,8,7168]{2,1,0:T(8,128)(2,1)}, u32[]{:S(2)}) %copy-start.1) | copy-done | bytes 3670040
  124.1 2.0 %copy-done.3 = bf16[256,7168]{1,0:T(8,128)(2,1)S(1)} copy-done((bf16[256,7168]{1,0:T(8,128)(2,1)S(1)}, bf16[256,7168]{1,0:T(8,128)(2,1)}, u32[]{:S(2)}) %copy-start.3) | copy-done | bytes 3670040
  126.1 2.7 %shard_map.128.near_ref = bf16[3584,512]{1,0:T(8,128)(2,1)S(1)} custom-call(s32[1]{0:T(128)} %bitcast.11.half_ref, bf16[256,7168]{1,0:T(8,128)(2,1)S(1)} %bitcast.15, bf16[256,7168]{1,0:T(8,128)(2,1)S(1)} %copy-done.3), custom_call_target="tpu_custom_call" | custom-call | tf_op jit(solution)/shard_map/pallas_call | solution.py:286
  128.8 7.5 %shard_map.130.far_ref.refs_1_ = bf16[3584,512]{1,0:T(8,128)(2,1)S(1)} custom-call(s32[1]{0:T(128)} %bitcast.11.half_ref, bf16[256,3584]{1,0:T(8,128)(2,1)} %collective-permute-done.3.first_ref, bf16[256,3584]{1,0:T(8,128)(2,1)S(1)} %collective-permute-done.4.second_ref), custom_call_target="tpu_custom_call" | custom-call | tf_op jit(solution)/shard_map/pallas_call | solution.py:286
  136.3 1.1 shard_map.132.refs_0_
  137.4 2.3 %shard_map.133 = f32[1792,512]{1,0:T(8,128)} custom-call(f32[1792,512]{1,0:T(8,128)S(1)} %shard_map.132.refs_0_, bf16[3584,512]{1,0:T(8,128)(2,1)S(1)} %shard_map.130.far_ref.refs_1_, bf16[512,512]{1,0:T(8,128)(2,1)S(1)} %collective-permute-done.6.refs_2_), custom_call_target="tpu_custom_call" | custom-call | flops 939524096 | bytes 11534336 | tf_op jit(solution)/shard_map/pallas_call | solution.py:54
  139.7 5.6 %collective-permute-done.5.there_ref = bf16[512,512]{1,0:T(8,128)(2,1)S(1)} collective-permute-done((bf16[512,512]{1,0:T(8,128)(2,1)S(1)}, bf16[512,512]{1,0:T(8,128)(2,1)S(1)}, u32[]{:S(2)}, u32[]{:S(2)}) %collective-permute-start.5) | collective-permute-done | bytes 524320 | tf_op jit(solution)/shard_map/ppermute | solution.py:411
  145.3 3.5 %shard_map.131 = f32[1792,512]{1,0:T(8,128)} custom-call(bf16[3584,512]{1,0:T(8,128)(2,1)S(1)} %shard_map.128.near_ref, bf16[3584,512]{1,0:T(8,128)(2,1)S(1)} %shard_map.130.far_ref.refs_1_, bf16[512,512]{1,0:T(8,128)(2,1)S(1)} %get-tuple-element.30.gg_ref.here_ref, bf16[512,512]{1,0:T(8,128)(2,1)S(1)} %collective-permute-done.5.there_ref), custom_call_target="tpu_custom_call" | custom-call | flops 1879048192 | bytes 8388608 | tf_op jit(solution)/shard_map/pallas_call | solution.py:312
  148.7 7.8 %collective-permute-done.7.there_ref = bf16[512,512]{1,0:T(8,128)(2,1)S(1)} collective-permute-done((bf16[512,512]{1,0:T(8,128)(2,1)S(1)}, bf16[512,512]{1,0:T(8,128)(2,1)S(1)}, u32[]{:S(2)}, u32[]{:S(2)}) %collective-permute-start.7) | collective-permute-done | bytes 524320 | tf_op jit(solution)/shard_map/ppermute | solution.py:411
  156.5 3.5 %shard_map.134 = f32[1792,512]{1,0:T(8,128)} custom-call(bf16[3584,512]{1,0:T(8,128)(2,1)S(1)} %shard_map.128.near_ref, bf16[3584,512]{1,0:T(8,128)(2,1)S(1)} %shard_map.130.far_ref.refs_1_, bf16[512,512]{1,0:T(8,128)(2,1)S(1)} %get-tuple-element.29.hid_ref.refs_0_.here_ref, bf16[512,512]{1,0:T(8,128)(2,1)S(1)} %collective-permute-done.7.there_ref), custom_call_target="tpu_custom_call" | custom-call | flops 1879048192 | bytes 8388608 | tf_op jit(solution)/shard_map/pallas_call | solution.py:312
  160.0 3.5 %shard_map.127 = (bf16[32,3584]{1,0:T(8,128)(2,1)}, bf16[32,3584]{1,0:T(8,128)(2,1)}) custom-call(bf16[256,7168]{1,0:T(8,128)(2,1)} %bitcast.8.refs_0_, bf16[256,32]{1,0:T(8,128)(2,1)S(1)} %get-tuple-element.32.refs_1_, bf16[256,96]{1,0:T(8,128)(2,1)S(1)} %get-tuple-element.33.refs_2_), custom_call_target="tpu_custom_call" | custom-call | flops 234881024 | bytes 4194304 | tf_op jit(solution)/shard_map/pallas_call | solution.py:54
  (11 shorter events, 0.0 us)
Async XLA Ops:
  61.4 6.3 %copy-start = (bf16[32,8,7168]{2,1,0:T(8,128)(2,1)}, bf16[32,8,7168]{2,1,0:T(8,128)(2,1)S(1)}, u32[]{:S(2)}) copy-start(bf16[32,8,7168]{2,1,0:T(8,128)(2,1)S(1)} %all_to_all.10) | copy-start | bytes 11010052
  61.4 7.8 %collective-permute-start = (bf16[256,7168]{1,0:T(8,128)(2,1)S(1)}, bf16[256,7168]{1,0:T(8,128)(2,1)S(1)}, u32[]{:S(2)}, u32[]{:S(2)}) collective-permute-start(bf16[256,7168]{1,0:T(8,128)(2,1)S(1)} %bitcast.12), channel_id=1, source_target_pairs={{0,1},{1,0},{2,3},{3,2},{4,5},{5,4},{6,7},{7,6},{8,9},{9,8},{10,11... | collective-permute-start | bytes 11010056 | tf_op jit(solution)/shard_map/ppermute | solution.py:408
  69.2 3.1 %copy-start.2 = (bf16[256,7168]{1,0:T(8,128)(2,1)}, bf16[256,7168]{1,0:T(8,128)(2,1)S(1)}, u32[]{:S(2)}) copy-start(bf16[256,7168]{1,0:T(8,128)(2,1)S(1)} %collective-permute-done.rows_ref.second_ref) | copy-start | bytes 11010052
  73.5 6.6 %collective-permute-start.1 = (bf16[256,3584]{1,0:T(8,128)(2,1)S(1)}, bf16[256,3584]{1,0:T(8,128)(2,1)S(1)}, u32[]{:S(2)}, u32[]{:S(2)}) collective-permute-start(bf16[256,3584]{1,0:T(8,128)(2,1)S(1)} %shard_map.122), channel_id=1, source_target_pairs={{0,1},{1,0},{2,3},{3,2},{4,5},{5,4},{6,7},{7,6},{8,9},{9,8},{10,11... | collective-permute-start | bytes 5505032 | tf_op jit(solution)/shard_map/ppermute | solution.py:408
  76.1 6.3 %collective-permute-start.2 = (bf16[256,3584]{1,0:T(8,128)(2,1)S(1)}, bf16[256,3584]{1,0:T(8,128)(2,1)S(1)}, u32[]{:S(2)}, u32[]{:S(2)}) collective-permute-start(bf16[256,3584]{1,0:T(8,128)(2,1)S(1)} %shard_map.125), channel_id=1, source_target_pairs={{0,1},{1,0},{2,3},{3,2},{4,5},{5,4},{6,7},{7,6},{8,9},{9,8},{10,11... | collective-permute-start | bytes 5505032 | tf_op jit(solution)/shard_map/ppermute | solution.py:408
  77.8 41.6 %collective-permute-start.3 = (bf16[256,3584]{1,0:T(8,128)(2,1)S(1)}, bf16[256,3584]{1,0:T(8,128)(2,1)}, u32[]{:S(2)}, u32[]{:S(2)}) collective-permute-start(bf16[256,3584]{1,0:T(8,128)(2,1)S(1)} %shard_map.129), channel_id=1, source_target_pairs={{0,64},{1,65},{2,66},{3,67},{4,68},{5,69},{6,70},{7,71},{8,72},{9,... | collective-permute-start | bytes 5505032 | tf_op jit(solution)/shard_map/ppermute | solution.py:411
  83.8 76.2 %all-to-all-start.1 = ((bf16[32,8,7168]{2,1,0:T(8,128)(2,1)}), bf16[32,8,7168]{2,1,0:T(8,128)(2,1)}, u32[]{:S(2)}, u32[]{:S(2)}) async-start(bf16[32,8,7168]{2,1,0:T(8,128)(2,1)} %bitcast.16), calls=%async_computation.1 | async-start | bytes 7340032 | tf_op jit(solution)/shard_map/all_to_all | solution.py:31
  119.3 9.5 %collective-permute-start.4 = (bf16[256,3584]{1,0:T(8,128)(2,1)}, bf16[256,3584]{1,0:T(8,128)(2,1)S(1)}, u32[]{:S(2)}, u32[]{:S(2)}) collective-permute-start(bf16[256,3584]{1,0:T(8,128)(2,1)} %collective-permute-done.3.first_ref), channel_id=1, source_target_pairs={{0,1},{1,0},{2,3},{3,2},{4,5},{5,4},{6,7},{7,6},{8,9},{9,8},{10,11... | collective-permute-start | bytes 5505032 | tf_op jit(solution)/shard_map/ppermute | solution.py:408
  120.6 16.8 %collective-permute-start.6 = (bf16[512,512]{1,0:T(8,128)(2,1)S(1)}, bf16[512,512]{1,0:T(8,128)(2,1)S(1)}, u32[]{:S(2)}, u32[]{:S(2)}) collective-permute-start(bf16[512,512]{1,0:T(8,128)(2,1)S(1)} %get-tuple-element.31.ug_ref.here_ref), channel_id=1, source_target_pairs={{0,64},{1,65},{2,66},{3,67},{4,68},{5,69},{6,70},{7,71},{8,72},{9,... | collective-permute-start | bytes 1572872 | tf_op jit(solution)/shard_map/ppermute | solution.py:411
  120.6 24.7 %collective-permute-start.5 = (bf16[512,512]{1,0:T(8,128)(2,1)S(1)}, bf16[512,512]{1,0:T(8,128)(2,1)S(1)}, u32[]{:S(2)}, u32[]{:S(2)}) collective-permute-start(bf16[512,512]{1,0:T(8,128)(2,1)S(1)} %get-tuple-element.30.gg_ref.here_ref), channel_id=1, source_target_pairs={{0,64},{1,65},{2,66},{3,67},{4,68},{5,69},{6,70},{7,71},{8,72},{9,... | collective-permute-start | bytes 1572872 | tf_op jit(solution)/shard_map/ppermute | solution.py:411
  122.0 34.5 %collective-permute-start.7 = (bf16[512,512]{1,0:T(8,128)(2,1)S(1)}, bf16[512,512]{1,0:T(8,128)(2,1)S(1)}, u32[]{:S(2)}, u32[]{:S(2)}) collective-permute-start(bf16[512,512]{1,0:T(8,128)(2,1)S(1)} %get-tuple-element.29.hid_ref.refs_0_.here_ref), channel_id=1, source_target_pairs={{0,64},{1,65},{2,66},{3,67},{4,68},{5,69},{6,70},{7,71},{8,72},{9,... | collective-permute-start | bytes 1572872 | tf_op jit(solution)/shard_map/ppermute | solution.py:411
  122.0 2.0 %copy-start.1 = (bf16[32,8,7168]{2,1,0:T(8,128)(2,1)S(1)}, bf16[32,8,7168]{2,1,0:T(8,128)(2,1)}, u32[]{:S(2)}) copy-start(bf16[32,8,7168]{2,1,0:T(8,128)(2,1)} %copy-done) | copy-start | bytes 11010052
  124.1 2.0 %copy-start.3 = (bf16[256,7168]{1,0:T(8,128)(2,1)S(1)}, bf16[256,7168]{1,0:T(8,128)(2,1)}, u32[]{:S(2)}) copy-start(bf16[256,7168]{1,0:T(8,128)(2,1)} %copy-done.2) | copy-start | bytes 11010052

commit v5 on v4

--- a/solution.py
+++ b/solution.py
@@ -124,20 +124,26 @@
     split_ref[:, 0:rows] = high
     split_ref[:, rows : 2 * rows] = middle
     split_ref[:, 2 * rows : 3 * rows] = low
-    fetch_tok.wait()
-    buf[:, :width] = mm(picked, tok_buf[...]).astype(jnp.bfloat16)
-    first = pltpu.make_async_copy(
-        buf.at[:, pl.ds(0, width)], sent_ref.at[:, pl.ds(0, width)], sems.at[2]
-    )
-    first.start()
-    fetch_cot.wait()
-    buf[:, width:] = (slot_prob * mm(picked, cot_buf[...])).astype(jnp.bfloat16)
-    second = pltpu.make_async_copy(
-        buf.at[:, pl.ds(width, width)], sent_ref.at[:, pl.ds(width, width)], sems.at[3]
-    )
-    second.start()
-    first.wait()
-    second.wait()
+    copies = []
+    part = width // 2
+    for i in range(4):
+        if i == 0:
+            fetch_tok.wait()
+        if i == 2:
+            fetch_cot.wait()
+        low = i % 2 * part
+        source = tok_buf if i < 2 else cot_buf
+        rows_now = mm(picked, source[:, low : low + part])
+        if i >= 2:
+            rows_now = slot_prob * rows_now
+        buf[:, i * part : (i + 1) * part] = rows_now.astype(jnp.bfloat16)
+        span = pl.ds(i * part, part)
+        copies.append(
+            pltpu.make_async_copy(buf.at[:, span], sent_ref.at[:, span], sems.at[8 + i])
+        )
+        copies[i].start()
+    for copy in copies:
+        copy.wait()
     weight.wait()
 
 
@@ -182,16 +188,20 @@
         ]
         for k, (w, out) in enumerate(((wu_ref, wu_out), (wd_ref, wd_out)))
     ]
-    for fetch in fetches:
-        for copy in fetch:
-            copy.start()
+    for copy in fetches[0]:
+        copy.start()
     gate_pre = mm(rows_ref[:, 0:width], wg_ref[...])
     results = []
     for k, out in enumerate((wu_out, wd_out)):
         total = 0.0
+        if k == 0:
+            fetches[0][0].wait()
+            for copy in fetches[1]:
+                copy.start()
         for i in range(pieces):
             low, high = i * size, (i + 1) * size
-            fetches[k][i].wait()
+            if k + i > 0:
+                fetches[k][i].wait()
             total = total + mm(rows_ref[:, k * width + low : k * width + high], out[low:high, :])
         results.append(total)
     values = slopes(gate_pre, *results)
@@ -442,7 +452,7 @@
             pltpu.VMEM((flat_rows, width), jnp.bfloat16),
             pltpu.VMEM((flat_rows, width), jnp.bfloat16),
             pltpu.VMEM((places, 2 * width), jnp.bfloat16),
-            pltpu.SemaphoreType.DMA((8,)),
+            pltpu.SemaphoreType.DMA((12,)),
         ),
     )
     start = ((1 - half) * half_width).reshape(1)
@@ -483,6 +493,7 @@
         [VMEM, VMEM, HBM, HBM],
         scratch=(pltpu.SemaphoreType.DMA((pieces, 2)),),
     )
+    row = bf(places, width)
     hid, gg, ug = call(
         oth_body,
         (mids,) * 3,
@@ -490,7 +501,6 @@
         3 * unit,
         [VMEM] * 7,
     )
-    row = bf(places, width)
     (out_oth,) = call(out_body, (row,), (hid, wd), unit, [VMEM] * 2)
     (dx_oth,) = call(dx_body, (row,), (gg, ug, wg, wu), 2 * unit, [VMEM] * 4)
     out_other = core_swap(out_oth)
@@ -548,7 +558,7 @@
             pltpu.SemaphoreType.DMA((pieces,)),
         ),
     )
-    moe, grad_in = combine(back, picked, split, pieces)
+    moe, grad_in = combine(back, picked, split, 2)
     return (
         moe.reshape(micros, tok_rows, width),
         grad_in.reshape(micros, tok_rows, width),

time: 164 us -> 164 us (level)
  no operation moved by 1% of the time
where the time goes in v5:
time: 164 us; the launch traced here: 163 us
  blocking collectives  56.9 us (35%)
  waiting for transfers between devices  45.6 us (28%)
  Pallas kernels  45.2 us (28%)
  starting transfers between devices  10.3 us (6%)
  local copies, waits for them, and re-layouts  4.08 us (2%)
    all_to_all x1, blocking collectives, exchange(): lax.all_to_all(x, AXES, split_axis=0, concat_axis=0, tiled=True, axis_ind...  56.9 us
    ppermute x4, waiting for transfers between devices, pair_swap(): return lax.ppermute(x, AXES, pairs)  44 us
    pallas_call x12, Pallas kernels, call(): pl.pallas_call(kernel, out_shape=outs, in_specs=in_specs, out_specs=out_s...  28.1 us
    pallas_call x2, Pallas kernels, turn(): pl.pallas_call(turn_body, out_shape=bf(tall, 2 * rows), grid_spec=pltpu.P...  10.1 us
    pallas_call x2, Pallas kernels, weight_grad(): pl.pallas_call(grad_body, out_shape=jax.ShapeDtypeStruct((tall, part), jn...  6.92 us
    all_to_all x1, starting transfers between devices, exchange(): lax.all_to_all(x, AXES, split_axis=0, concat_axis=0, tiled=True, axis_ind...  4.85 us
    unnamed x8, local copies, waits for them, and re-layouts  4.08 us
    ppermute x4, starting transfers between devices, core_swap(): return lax.ppermute(x, AXES, cores)  3.7 us
  transfers between devices with their start and end apart: 9, of which 4 were waited for; matrix products, arithmetic and copies ran while one was open for 0% of the time, Pallas kernels for 21%

profile of v5, /device:TPU:1, one launch (start us, length us, event | category | flops | bytes accessed | tf_op | source)
XLA Modules:
  0.0 163.1 jit_solution(13759179409069226786)
XLA Ops:
  0.6 3.6 %shard_map.119 = (bf16[256,7168]{1,0:T(8,128)(2,1)}, bf16[256,32]{1,0:T(8,128)(2,1)S(1)}, bf16[256,96]{1,0:T(8,128)(2,1)S(1)}, bf16[3584,512]{1,0:T(8,128)(2,1)S(1)}) custom-call(s32[2,4,16]{2,1,0:T(4,128)} %bitcast.20, f32[2,4,16]{2,1,0:T(4,128)} %bitcast.21, s32[2,32]{1,0:T(2,128)} %refs_2_.2, bf16[32,3584]{1,0:T(8,128)(2,1)} %bitcast.18, ...), custom_call_target="tpu_custom_call" | custom-call | flops 117440512 | bytes 11535616 | tf_op jit(solution)/shard_map/pallas_call | solution.py:54
  4.3 56.9 %all_to_all.10 = bf16[32,8,7168]{2,1,0:T(8,128)(2,1)S(1)} all-to-all(bf16[32,8,7168]{2,1,0:T(8,128)(2,1)} %bitcast.17), channel_id=1, replica_groups={{0,66,4,70,8,74,12,78,16,82,20,86,24,90,28,94,32,98,36,102,40,106,44,11..., dimensions={0} | all-to-all | bytes 7340032 | tf_op jit(solution)/shard_map/all_to_all | solution.py:31
  61.2 1.8 %collective-permute-start = (bf16[256,7168]{1,0:T(8,128)(2,1)S(1)}, bf16[256,7168]{1,0:T(8,128)(2,1)S(1)}, u32[]{:S(2)}, u32[]{:S(2)}) collective-permute-start(bf16[256,7168]{1,0:T(8,128)(2,1)S(1)} %bitcast.12), channel_id=1, source_target_pairs={{0,1},{1,0},{2,3},{3,2},{4,5},{5,4},{6,7},{7,6},{8,9},{9,8},{10,11... | collective-permute-start | bytes 11010056 | tf_op jit(solution)/shard_map/ppermute | solution.py:418
  63.0 4.4 %shard_map.120 = (bf16[256,512]{1,0:T(8,128)(2,1)S(1)}, bf16[256,512]{1,0:T(8,128)(2,1)S(1)}, bf16[256,512]{1,0:T(8,128)(2,1)S(1)}, bf16[3584,512]{1,0:T(8,128)(2,1)S(1)}, bf16[3584,512]{1,0:T(8,128)(2,1)S(1)}) custom-call(bf16[256,7168]{1,0:T(8,128)(2,1)S(1)} %bitcast.13, bf16[3584,512]{1,0:T(8,128)(2,1)S(1)} %get-tuple-element.23.refs_1_.wg_ref, ...), custom_call_target="tpu_custom_call" | custom-call | flops 2818572288 | bytes 22806528 | tf_op jit(solution)/shard_map/pallas_call | solution.py:54
  67.5 1.6 collective-permute-done.rows_ref.second_ref
  69.1 3.1 %shard_map.121 = (bf16[512,512]{1,0:T(8,128)(2,1)S(1)}, bf16[512,512]{1,0:T(8,128)(2,1)S(1)}, bf16[512,512]{1,0:T(8,128)(2,1)S(1)}) custom-call(bf16[256,7168]{1,0:T(8,128)(2,1)S(1)} %collective-permute-done.rows_ref.second_ref, bf16[3584,512]{1,0:T(8,128)(2,1)S(1)} %get-tuple-element.23.refs_1_.wg_ref, bf16[3584,512]{1,0:T(8,128)(2,1)S(1)} %get-tuple-element.24.wu_ref, ...), custom_call_target="tpu_custom_call" | custom-call | flops 2818572288 | bytes 17039360 | tf_op jit(solution)/shard_map/pallas_call | solution.py:54
  72.2 1.1 shard_map.122
  73.3 0.5 collective-permute-start.1
  73.8 2.1 %shard_map.125 = bf16[256,3584]{1,0:T(8,128)(2,1)S(1)} custom-call(bf16[512,512]{1,0:T(8,128)(2,1)S(1)} %get-tuple-element.30.gg_ref.here_ref, bf16[512,512]{1,0:T(8,128)(2,1)S(1)} %get-tuple-element.31.ug_ref.here_ref, bf16[3584,512]{1,0:T(8,128)(2,1)S(1)} %get-tuple-element.23.refs_1_.wg_ref, bf16[3584,512]{1,0:T(8,128)(2,1)S(1)} %get-tuple-element.24.wu_ref), custom_call_target="tpu_custom_call" | custom-call | flops 1879048192 | bytes 10223616 | tf_op jit(solution)/shard_map/pallas_call | solution.py:54
  75.9 0.2 collective-permute-start.2
  76.1 1.5 shard_map.129
  77.6 0.3 collective-permute-start.3
  77.9 2.1 %shard_map.124.refs_1_ = bf16[256,3584]{1,0:T(8,128)(2,1)S(1)} custom-call(bf16[512,512]{1,0:T(8,128)(2,1)S(1)} %get-tuple-element.30.gg_ref.here_ref, bf16[512,512]{1,0:T(8,128)(2,1)S(1)} %get-tuple-element.31.ug_ref.here_ref, bf16[3584,512]{1,0:T(8,128)(2,1)S(1)} %get-tuple-element.23.refs_1_.wg_ref, bf16[3584,512]{1,0:T(8,128)(2,1)S(1)} %get-tuple-element.24.wu_ref), custom_call_target="tpu_custom_call" | custom-call | flops 1879048192 | bytes 10223616 | tf_op jit(solution)/shard_map/pallas_call | solution.py:54
  80.0 2.2 %shard_map.123.refs_0_ = bf16[256,7168]{1,0:T(8,128)(2,1)} custom-call(bf16[512,512]{1,0:T(8,128)(2,1)S(1)} %get-tuple-element.29.hid_ref.refs_0_.here_ref, bf16[3584,512]{1,0:T(8,128)(2,1)S(1)} %get-tuple-element.25.wd_ref.refs_1_, bf16[256,3584]{1,0:T(8,128)(2,1)S(1)} %collective-permute-done.1.refs_2_), custom_call_target="tpu_custom_call" | custom-call | flops 939524096 | bytes 9699328 | tf_op jit(solution)/shard_map/pallas_call | solution.py:54
  82.2 1.4 shard_map.126
  83.6 4.9 %all-to-all-start.1 = ((bf16[32,8,7168]{2,1,0:T(8,128)(2,1)}), bf16[32,8,7168]{2,1,0:T(8,128)(2,1)}, u32[]{:S(2)}, u32[]{:S(2)}) async-start(bf16[32,8,7168]{2,1,0:T(8,128)(2,1)} %bitcast.16), calls=%async_computation.1 | async-start | bytes 7340032 | tf_op jit(solution)/shard_map/all_to_all | solution.py:31
  88.5 30.7 %collective-permute-done.3.first_ref = bf16[256,3584]{1,0:T(8,128)(2,1)} collective-permute-done((bf16[256,3584]{1,0:T(8,128)(2,1)S(1)}, bf16[256,3584]{1,0:T(8,128)(2,1)}, u32[]{:S(2)}, u32[]{:S(2)}) %collective-permute-start.3) | collective-permute-done | bytes 1835040 | tf_op jit(solution)/shard_map/ppermute | solution.py:421
  119.1 1.2 collective-permute-start.4
  120.4 0.0 collective-permute-start.6
  120.4 1.5 collective-permute-start.5
  121.9 0.0 collective-permute-start.7
  121.9 2.0 %copy-done.1 = bf16[32,8,7168]{2,1,0:T(8,128)(2,1)S(1)} copy-done((bf16[32,8,7168]{2,1,0:T(8,128)(2,1)S(1)}, bf16[32,8,7168]{2,1,0:T(8,128)(2,1)}, u32[]{:S(2)}) %copy-start.1) | copy-done | bytes 3670040
  123.9 2.0 %copy-done.3 = bf16[256,7168]{1,0:T(8,128)(2,1)S(1)} copy-done((bf16[256,7168]{1,0:T(8,128)(2,1)S(1)}, bf16[256,7168]{1,0:T(8,128)(2,1)}, u32[]{:S(2)}) %copy-start.3) | copy-done | bytes 3670040
  126.0 2.7 %shard_map.128.near_ref = bf16[3584,512]{1,0:T(8,128)(2,1)S(1)} custom-call(s32[1]{0:T(128)} %bitcast.11.half_ref, bf16[256,7168]{1,0:T(8,128)(2,1)S(1)} %bitcast.15, bf16[256,7168]{1,0:T(8,128)(2,1)S(1)} %copy-done.3), custom_call_target="tpu_custom_call" | custom-call | tf_op jit(solution)/shard_map/pallas_call | solution.py:296
  128.6 7.5 %shard_map.130.far_ref.refs_1_ = bf16[3584,512]{1,0:T(8,128)(2,1)S(1)} custom-call(s32[1]{0:T(128)} %bitcast.11.half_ref, bf16[256,3584]{1,0:T(8,128)(2,1)} %collective-permute-done.3.first_ref, bf16[256,3584]{1,0:T(8,128)(2,1)S(1)} %collective-permute-done.4.second_ref), custom_call_target="tpu_custom_call" | custom-call | tf_op jit(solution)/shard_map/pallas_call | solution.py:296
  136.1 1.1 shard_map.132.refs_0_
  137.2 2.3 %shard_map.133 = f32[1792,512]{1,0:T(8,128)} custom-call(f32[1792,512]{1,0:T(8,128)S(1)} %shard_map.132.refs_0_, bf16[3584,512]{1,0:T(8,128)(2,1)S(1)} %shard_map.130.far_ref.refs_1_, bf16[512,512]{1,0:T(8,128)(2,1)S(1)} %collective-permute-done.6.refs_2_), custom_call_target="tpu_custom_call" | custom-call | flops 939524096 | bytes 11534336 | tf_op jit(solution)/shard_map/pallas_call | solution.py:54
  139.5 5.6 %collective-permute-done.5.there_ref = bf16[512,512]{1,0:T(8,128)(2,1)S(1)} collective-permute-done((bf16[512,512]{1,0:T(8,128)(2,1)S(1)}, bf16[512,512]{1,0:T(8,128)(2,1)S(1)}, u32[]{:S(2)}, u32[]{:S(2)}) %collective-permute-start.5) | collective-permute-done | bytes 524320 | tf_op jit(solution)/shard_map/ppermute | solution.py:421
  145.1 3.5 %shard_map.131 = f32[1792,512]{1,0:T(8,128)} custom-call(bf16[3584,512]{1,0:T(8,128)(2,1)S(1)} %shard_map.128.near_ref, bf16[3584,512]{1,0:T(8,128)(2,1)S(1)} %shard_map.130.far_ref.refs_1_, bf16[512,512]{1,0:T(8,128)(2,1)S(1)} %get-tuple-element.30.gg_ref.here_ref, bf16[512,512]{1,0:T(8,128)(2,1)S(1)} %collective-permute-done.5.there_ref), custom_call_target="tpu_custom_call" | custom-call | flops 1879048192 | bytes 8388608 | tf_op jit(solution)/shard_map/pallas_call | solution.py:322
  148.6 7.8 %collective-permute-done.7.there_ref = bf16[512,512]{1,0:T(8,128)(2,1)S(1)} collective-permute-done((bf16[512,512]{1,0:T(8,128)(2,1)S(1)}, bf16[512,512]{1,0:T(8,128)(2,1)S(1)}, u32[]{:S(2)}, u32[]{:S(2)}) %collective-permute-start.7) | collective-permute-done | bytes 524320 | tf_op jit(solution)/shard_map/ppermute | solution.py:421
  156.3 3.5 %shard_map.134 = f32[1792,512]{1,0:T(8,128)} custom-call(bf16[3584,512]{1,0:T(8,128)(2,1)S(1)} %shard_map.128.near_ref, bf16[3584,512]{1,0:T(8,128)(2,1)S(1)} %shard_map.130.far_ref.refs_1_, bf16[512,512]{1,0:T(8,128)(2,1)S(1)} %get-tuple-element.29.hid_ref.refs_0_.here_ref, bf16[512,512]{1,0:T(8,128)(2,1)S(1)} %collective-permute-done.7.there_ref), custom_call_target="tpu_custom_call" | custom-call | flops 1879048192 | bytes 8388608 | tf_op jit(solution)/shard_map/pallas_call | solution.py:322
  159.8 3.1 %shard_map.127 = (bf16[32,3584]{1,0:T(8,128)(2,1)}, bf16[32,3584]{1,0:T(8,128)(2,1)}) custom-call(bf16[256,7168]{1,0:T(8,128)(2,1)} %bitcast.8.refs_0_, bf16[256,32]{1,0:T(8,128)(2,1)S(1)} %get-tuple-element.32.refs_1_, bf16[256,96]{1,0:T(8,128)(2,1)S(1)} %get-tuple-element.33.refs_2_), custom_call_target="tpu_custom_call" | custom-call | flops 234881024 | bytes 4194304 | tf_op jit(solution)/shard_map/pallas_call | solution.py:54
  (11 shorter events, 0.0 us)
Async XLA Ops:
  61.2 6.3 %copy-start = (bf16[32,8,7168]{2,1,0:T(8,128)(2,1)}, bf16[32,8,7168]{2,1,0:T(8,128)(2,1)S(1)}, u32[]{:S(2)}) copy-start(bf16[32,8,7168]{2,1,0:T(8,128)(2,1)S(1)} %all_to_all.10) | copy-start | bytes 11010052
  61.2 7.8 %collective-permute-start = (bf16[256,7168]{1,0:T(8,128)(2,1)S(1)}, bf16[256,7168]{1,0:T(8,128)(2,1)S(1)}, u32[]{:S(2)}, u32[]{:S(2)}) collective-permute-start(bf16[256,7168]{1,0:T(8,128)(2,1)S(1)} %bitcast.12), channel_id=1, source_target_pairs={{0,1},{1,0},{2,3},{3,2},{4,5},{5,4},{6,7},{7,6},{8,9},{9,8},{10,11... | collective-permute-start | bytes 11010056 | tf_op jit(solution)/shard_map/ppermute | solution.py:418
  69.1 3.1 %copy-start.2 = (bf16[256,7168]{1,0:T(8,128)(2,1)}, bf16[256,7168]{1,0:T(8,128)(2,1)S(1)}, u32[]{:S(2)}) copy-start(bf16[256,7168]{1,0:T(8,128)(2,1)S(1)} %collective-permute-done.rows_ref.second_ref) | copy-start | bytes 11010052
  73.3 6.6 %collective-permute-start.1 = (bf16[256,3584]{1,0:T(8,128)(2,1)S(1)}, bf16[256,3584]{1,0:T(8,128)(2,1)S(1)}, u32[]{:S(2)}, u32[]{:S(2)}) collective-permute-start(bf16[256,3584]{1,0:T(8,128)(2,1)S(1)} %shard_map.122), channel_id=1, source_target_pairs={{0,1},{1,0},{2,3},{3,2},{4,5},{5,4},{6,7},{7,6},{8,9},{9,8},{10,11... | collective-permute-start | bytes 5505032 | tf_op jit(solution)/shard_map/ppermute | solution.py:418
  75.9 6.3 %collective-permute-start.2 = (bf16[256,3584]{1,0:T(8,128)(2,1)S(1)}, bf16[256,3584]{1,0:T(8,128)(2,1)S(1)}, u32[]{:S(2)}, u32[]{:S(2)}) collective-permute-start(bf16[256,3584]{1,0:T(8,128)(2,1)S(1)} %shard_map.125), channel_id=1, source_target_pairs={{0,1},{1,0},{2,3},{3,2},{4,5},{5,4},{6,7},{7,6},{8,9},{9,8},{10,11... | collective-permute-start | bytes 5505032 | tf_op jit(solution)/shard_map/ppermute | solution.py:418
  77.6 41.6 %collective-permute-start.3 = (bf16[256,3584]{1,0:T(8,128)(2,1)S(1)}, bf16[256,3584]{1,0:T(8,128)(2,1)}, u32[]{:S(2)}, u32[]{:S(2)}) collective-permute-start(bf16[256,3584]{1,0:T(8,128)(2,1)S(1)} %shard_map.129), channel_id=1, source_target_pairs={{0,64},{1,65},{2,66},{3,67},{4,68},{5,69},{6,70},{7,71},{8,72},{9,... | collective-permute-start | bytes 5505032 | tf_op jit(solution)/shard_map/ppermute | solution.py:421
  83.6 76.2 %all-to-all-start.1 = ((bf16[32,8,7168]{2,1,0:T(8,128)(2,1)}), bf16[32,8,7168]{2,1,0:T(8,128)(2,1)}, u32[]{:S(2)}, u32[]{:S(2)}) async-start(bf16[32,8,7168]{2,1,0:T(8,128)(2,1)} %bitcast.16), calls=%async_computation.1 | async-start | bytes 7340032 | tf_op jit(solution)/shard_map/all_to_all | solution.py:31
  119.1 9.5 %collective-permute-start.4 = (bf16[256,3584]{1,0:T(8,128)(2,1)}, bf16[256,3584]{1,0:T(8,128)(2,1)S(1)}, u32[]{:S(2)}, u32[]{:S(2)}) collective-permute-start(bf16[256,3584]{1,0:T(8,128)(2,1)} %collective-permute-done.3.first_ref), channel_id=1, source_target_pairs={{0,1},{1,0},{2,3},{3,2},{4,5},{5,4},{6,7},{7,6},{8,9},{9,8},{10,11... | collective-permute-start | bytes 5505032 | tf_op jit(solution)/shard_map/ppermute | solution.py:418
  120.4 16.8 %collective-permute-start.6 = (bf16[512,512]{1,0:T(8,128)(2,1)S(1)}, bf16[512,512]{1,0:T(8,128)(2,1)S(1)}, u32[]{:S(2)}, u32[]{:S(2)}) collective-permute-start(bf16[512,512]{1,0:T(8,128)(2,1)S(1)} %get-tuple-element.31.ug_ref.here_ref), channel_id=1, source_target_pairs={{0,64},{1,65},{2,66},{3,67},{4,68},{5,69},{6,70},{7,71},{8,72},{9,... | collective-permute-start | bytes 1572872 | tf_op jit(solution)/shard_map/ppermute | solution.py:421
  120.4 24.7 %collective-permute-start.5 = (bf16[512,512]{1,0:T(8,128)(2,1)S(1)}, bf16[512,512]{1,0:T(8,128)(2,1)S(1)}, u32[]{:S(2)}, u32[]{:S(2)}) collective-permute-start(bf16[512,512]{1,0:T(8,128)(2,1)S(1)} %get-tuple-element.30.gg_ref.here_ref), channel_id=1, source_target_pairs={{0,64},{1,65},{2,66},{3,67},{4,68},{5,69},{6,70},{7,71},{8,72},{9,... | collective-permute-start | bytes 1572872 | tf_op jit(solution)/shard_map/ppermute | solution.py:421
  121.9 34.5 %collective-permute-start.7 = (bf16[512,512]{1,0:T(8,128)(2,1)S(1)}, bf16[512,512]{1,0:T(8,128)(2,1)S(1)}, u32[]{:S(2)}, u32[]{:S(2)}) collective-permute-start(bf16[512,512]{1,0:T(8,128)(2,1)S(1)} %get-tuple-element.29.hid_ref.refs_0_.here_ref), channel_id=1, source_target_pairs={{0,64},{1,65},{2,66},{3,67},{4,68},{5,69},{6,70},{7,71},{8,72},{9,... | collective-permute-start | bytes 1572872 | tf_op jit(solution)/shard_map/ppermute | solution.py:421
  121.9 2.0 %copy-start.1 = (bf16[32,8,7168]{2,1,0:T(8,128)(2,1)S(1)}, bf16[32,8,7168]{2,1,0:T(8,128)(2,1)}, u32[]{:S(2)}) copy-start(bf16[32,8,7168]{2,1,0:T(8,128)(2,1)} %copy-done) | copy-start | bytes 11010052
  123.9 2.0 %copy-start.3 = (bf16[256,7168]{1,0:T(8,128)(2,1)S(1)}, bf16[256,7168]{1,0:T(8,128)(2,1)}, u32[]{:S(2)}) copy-start(bf16[256,7168]{1,0:T(8,128)(2,1)} %copy-done.2) | copy-start | bytes 11010052

commit v6 on v5

--- a/solution.py
+++ b/solution.py
@@ -349,7 +349,7 @@
         copy.wait()
 
 
-def combine_body(pieces, back_ref, pick_ref, split_ref, moe_ref, dx_ref, buf, sems):
+def combine_body(pieces, back_ref, pick_ref, split_ref, moe_hbm, dx_hbm, buf, moe_ref, dx_ref, sems):
     count, width = moe_ref.shape
     size = width // pieces
     copies = []
@@ -366,11 +366,22 @@
         sums = mm(split, buf[:, low:high])
         moe = sums[0:count] + (sums[count : 2 * count] + sums[2 * count : 3 * count])
         moe_ref[:, low:high] = moe.astype(jnp.bfloat16)
+    stores = [pltpu.make_async_copy(moe_ref, moe_hbm, sems.at[2 * pieces])]
+    stores[0].start()
     for i in range(pieces):
         low, high = i * size, (i + 1) * size
         copies[pieces + i].wait()
         dx = mm(picked, buf[:, width + low : width + high])
         dx_ref[:, low:high] = dx.astype(jnp.bfloat16)
+        span = pl.ds(low, size)
+        stores.append(
+            pltpu.make_async_copy(
+                dx_ref.at[:, span], dx_hbm.at[:, span], sems.at[2 * pieces + 1 + i]
+            )
+        )
+        stores[i + 1].start()
+    for store in stores:
+        store.wait()
 
 
 def combine(back, picked, split, pieces):
@@ -383,13 +394,16 @@
 
     return call(
         body,
-        (bf(rows, width), bf(rows, width)),
+        (pltpu.HBM((rows, width), jnp.bfloat16),) * 2,
         (in_hbm(back), picked, split),
         8 * rows * places * width,
         [HBM, VMEM, VMEM],
+        [HBM] * 2,
         scratch=(
             pltpu.VMEM((places, double), jnp.bfloat16),
-            pltpu.SemaphoreType.DMA((2 * pieces,)),
+            pltpu.VMEM((rows, width), jnp.bfloat16),
+            pltpu.VMEM((rows, width), jnp.bfloat16),
+            pltpu.SemaphoreType.DMA((3 * pieces + 1,)),
         ),
     )
 

time: 164 us -> 164 us (level)
  no operation moved by 1% of the time
where the time goes in v6:
time: 164 us; the launch traced here: 163 us
  blocking collectives  56.9 us (35%)
  waiting for transfers between devices  45.6 us (28%)
  Pallas kernels  45.1 us (28%)
  starting transfers between devices  10.3 us (6%)
  local copies, waits for them, and re-layouts  4.08 us (2%)
    all_to_all x1, blocking collectives, exchange(): lax.all_to_all(x, AXES, split_axis=0, concat_axis=0, tiled=True, axis_ind...  56.9 us
    ppermute x4, waiting for transfers between devices, pair_swap(): return lax.ppermute(x, AXES, pairs)  44 us
    pallas_call x12, Pallas kernels, call(): pl.pallas_call(kernel, out_shape=outs, in_specs=in_specs, out_specs=out_s...  28.1 us
    pallas_call x2, Pallas kernels, turn(): pl.pallas_call(turn_body, out_shape=bf(tall, 2 * rows), grid_spec=pltpu.P...  10.1 us
    pallas_call x2, Pallas kernels, weight_grad(): pl.pallas_call(grad_body, out_shape=jax.ShapeDtypeStruct((tall, part), jn...  6.92 us
    all_to_all x1, starting transfers between devices, exchange(): lax.all_to_all(x, AXES, split_axis=0, concat_axis=0, tiled=True, axis_ind...  4.85 us
    unnamed x8, local copies, waits for them, and re-layouts  4.08 us
    ppermute x4, starting transfers between devices, core_swap(): return lax.ppermute(x, AXES, cores)  3.7 us
  transfers between devices with their start and end apart: 9, of which 4 were waited for; matrix products, arithmetic and copies ran while one was open for 0% of the time, Pallas kernels for 21%

profile of v6, /device:TPU:1, one launch (start us, length us, event | category | flops | bytes accessed | tf_op | source)
XLA Modules:
  0.0 163.0 jit_solution(9138705394407799723)
XLA Ops:
  0.6 3.6 %shard_map.119 = (bf16[256,7168]{1,0:T(8,128)(2,1)}, bf16[256,32]{1,0:T(8,128)(2,1)S(1)}, bf16[256,96]{1,0:T(8,128)(2,1)S(1)}, bf16[3584,512]{1,0:T(8,128)(2,1)S(1)}) custom-call(s32[2,4,16]{2,1,0:T(4,128)} %bitcast.20, f32[2,4,16]{2,1,0:T(4,128)} %bitcast.21, s32[2,32]{1,0:T(2,128)} %refs_2_.2, bf16[32,3584]{1,0:T(8,128)(2,1)} %bitcast.18, ...), custom_call_target="tpu_custom_call" | custom-call | flops 117440512 | bytes 11535616 | tf_op jit(solution)/shard_map/pallas_call | solution.py:54
  4.3 56.9 %all_to_all.10 = bf16[32,8,7168]{2,1,0:T(8,128)(2,1)S(1)} all-to-all(bf16[32,8,7168]{2,1,0:T(8,128)(2,1)} %bitcast.17), channel_id=1, replica_groups={{0,66,4,70,8,74,12,78,16,82,20,86,24,90,28,94,32,98,36,102,40,106,44,11..., dimensions={0} | all-to-all | bytes 7340032 | tf_op jit(solution)/shard_map/all_to_all | solution.py:31
  61.2 1.8 %collective-permute-start = (bf16[256,7168]{1,0:T(8,128)(2,1)S(1)}, bf16[256,7168]{1,0:T(8,128)(2,1)S(1)}, u32[]{:S(2)}, u32[]{:S(2)}) collective-permute-start(bf16[256,7168]{1,0:T(8,128)(2,1)S(1)} %bitcast.12), channel_id=1, source_target_pairs={{0,1},{1,0},{2,3},{3,2},{4,5},{5,4},{6,7},{7,6},{8,9},{9,8},{10,11... | collective-permute-start | bytes 11010056 | tf_op jit(solution)/shard_map/ppermute | solution.py:432
  63.0 4.4 %shard_map.120 = (bf16[256,512]{1,0:T(8,128)(2,1)S(1)}, bf16[256,512]{1,0:T(8,128)(2,1)S(1)}, bf16[256,512]{1,0:T(8,128)(2,1)S(1)}, bf16[3584,512]{1,0:T(8,128)(2,1)S(1)}, bf16[3584,512]{1,0:T(8,128)(2,1)S(1)}) custom-call(bf16[256,7168]{1,0:T(8,128)(2,1)S(1)} %bitcast.13, bf16[3584,512]{1,0:T(8,128)(2,1)S(1)} %get-tuple-element.23.refs_1_.wg_ref, ...), custom_call_target="tpu_custom_call" | custom-call | flops 2818572288 | bytes 22806528 | tf_op jit(solution)/shard_map/pallas_call | solution.py:54
  67.5 1.6 collective-permute-done.rows_ref.second_ref
  69.1 3.1 %shard_map.121 = (bf16[512,512]{1,0:T(8,128)(2,1)S(1)}, bf16[512,512]{1,0:T(8,128)(2,1)S(1)}, bf16[512,512]{1,0:T(8,128)(2,1)S(1)}) custom-call(bf16[256,7168]{1,0:T(8,128)(2,1)S(1)} %collective-permute-done.rows_ref.second_ref, bf16[3584,512]{1,0:T(8,128)(2,1)S(1)} %get-tuple-element.23.refs_1_.wg_ref, bf16[3584,512]{1,0:T(8,128)(2,1)S(1)} %get-tuple-element.24.wu_ref, ...), custom_call_target="tpu_custom_call" | custom-call | flops 2818572288 | bytes 17039360 | tf_op jit(solution)/shard_map/pallas_call | solution.py:54
  72.2 1.1 shard_map.122
  73.3 0.5 collective-permute-start.1
  73.8 2.1 %shard_map.125 = bf16[256,3584]{1,0:T(8,128)(2,1)S(1)} custom-call(bf16[512,512]{1,0:T(8,128)(2,1)S(1)} %get-tuple-element.30.gg_ref.here_ref, bf16[512,512]{1,0:T(8,128)(2,1)S(1)} %get-tuple-element.31.ug_ref.here_ref, bf16[3584,512]{1,0:T(8,128)(2,1)S(1)} %get-tuple-element.23.refs_1_.wg_ref, bf16[3584,512]{1,0:T(8,128)(2,1)S(1)} %get-tuple-element.24.wu_ref), custom_call_target="tpu_custom_call" | custom-call | flops 1879048192 | bytes 10223616 | tf_op jit(solution)/shard_map/pallas_call | solution.py:54
  75.9 0.2 collective-permute-start.2
  76.1 1.5 shard_map.129
  77.6 0.3 collective-permute-start.3
  77.9 2.1 %shard_map.124.refs_1_ = bf16[256,3584]{1,0:T(8,128)(2,1)S(1)} custom-call(bf16[512,512]{1,0:T(8,128)(2,1)S(1)} %get-tuple-element.30.gg_ref.here_ref, bf16[512,512]{1,0:T(8,128)(2,1)S(1)} %get-tuple-element.31.ug_ref.here_ref, bf16[3584,512]{1,0:T(8,128)(2,1)S(1)} %get-tuple-element.23.refs_1_.wg_ref, bf16[3584,512]{1,0:T(8,128)(2,1)S(1)} %get-tuple-element.24.wu_ref), custom_call_target="tpu_custom_call" | custom-call | flops 1879048192 | bytes 10223616 | tf_op jit(solution)/shard_map/pallas_call | solution.py:54
  80.0 2.2 %shard_map.123.refs_0_ = bf16[256,7168]{1,0:T(8,128)(2,1)} custom-call(bf16[512,512]{1,0:T(8,128)(2,1)S(1)} %get-tuple-element.29.hid_ref.refs_0_.here_ref, bf16[3584,512]{1,0:T(8,128)(2,1)S(1)} %get-tuple-element.25.wd_ref.refs_1_, bf16[256,3584]{1,0:T(8,128)(2,1)S(1)} %collective-permute-done.1.refs_2_), custom_call_target="tpu_custom_call" | custom-call | flops 939524096 | bytes 9699328 | tf_op jit(solution)/shard_map/pallas_call | solution.py:54
  82.2 1.4 shard_map.126
  83.6 4.9 %all-to-all-start.1 = ((bf16[32,8,7168]{2,1,0:T(8,128)(2,1)}), bf16[32,8,7168]{2,1,0:T(8,128)(2,1)}, u32[]{:S(2)}, u32[]{:S(2)}) async-start(bf16[32,8,7168]{2,1,0:T(8,128)(2,1)} %bitcast.16), calls=%async_computation.1 | async-start | bytes 7340032 | tf_op jit(solution)/shard_map/all_to_all | solution.py:31
  88.5 30.7 %collective-permute-done.3.first_ref = bf16[256,3584]{1,0:T(8,128)(2,1)} collective-permute-done((bf16[256,3584]{1,0:T(8,128)(2,1)S(1)}, bf16[256,3584]{1,0:T(8,128)(2,1)}, u32[]{:S(2)}, u32[]{:S(2)}) %collective-permute-start.3) | collective-permute-done | bytes 1835040 | tf_op jit(solution)/shard_map/ppermute | solution.py:435
  119.1 1.2 collective-permute-start.4
  120.4 0.0 collective-permute-start.6
  120.4 1.5 collective-permute-start.5
  121.9 0.0 collective-permute-start.7
  121.9 2.0 %copy-done.1 = bf16[32,8,7168]{2,1,0:T(8,128)(2,1)S(1)} copy-done((bf16[32,8,7168]{2,1,0:T(8,128)(2,1)S(1)}, bf16[32,8,7168]{2,1,0:T(8,128)(2,1)}, u32[]{:S(2)}) %copy-start.1) | copy-done | bytes 3670040
  123.9 2.0 %copy-done.3 = bf16[256,7168]{1,0:T(8,128)(2,1)S(1)} copy-done((bf16[256,7168]{1,0:T(8,128)(2,1)S(1)}, bf16[256,7168]{1,0:T(8,128)(2,1)}, u32[]{:S(2)}) %copy-start.3) | copy-done | bytes 3670040
  126.0 2.7 %shard_map.128.near_ref = bf16[3584,512]{1,0:T(8,128)(2,1)S(1)} custom-call(s32[1]{0:T(128)} %bitcast.11.half_ref, bf16[256,7168]{1,0:T(8,128)(2,1)S(1)} %bitcast.15, bf16[256,7168]{1,0:T(8,128)(2,1)S(1)} %copy-done.3), custom_call_target="tpu_custom_call" | custom-call | tf_op jit(solution)/shard_map/pallas_call | solution.py:296
  128.6 7.5 %shard_map.130.far_ref.refs_1_ = bf16[3584,512]{1,0:T(8,128)(2,1)S(1)} custom-call(s32[1]{0:T(128)} %bitcast.11.half_ref, bf16[256,3584]{1,0:T(8,128)(2,1)} %collective-permute-done.3.first_ref, bf16[256,3584]{1,0:T(8,128)(2,1)S(1)} %collective-permute-done.4.second_ref), custom_call_target="tpu_custom_call" | custom-call | tf_op jit(solution)/shard_map/pallas_call | solution.py:296
  136.1 1.1 shard_map.132.refs_0_
  137.2 2.3 %shard_map.133 = f32[1792,512]{1,0:T(8,128)} custom-call(f32[1792,512]{1,0:T(8,128)S(1)} %shard_map.132.refs_0_, bf16[3584,512]{1,0:T(8,128)(2,1)S(1)} %shard_map.130.far_ref.refs_1_, bf16[512,512]{1,0:T(8,128)(2,1)S(1)} %collective-permute-done.6.refs_2_), custom_call_target="tpu_custom_call" | custom-call | flops 939524096 | bytes 11534336 | tf_op jit(solution)/shard_map/pallas_call | solution.py:54
  139.5 5.6 %collective-permute-done.5.there_ref = bf16[512,512]{1,0:T(8,128)(2,1)S(1)} collective-permute-done((bf16[512,512]{1,0:T(8,128)(2,1)S(1)}, bf16[512,512]{1,0:T(8,128)(2,1)S(1)}, u32[]{:S(2)}, u32[]{:S(2)}) %collective-permute-start.5) | collective-permute-done | bytes 524320 | tf_op jit(solution)/shard_map/ppermute | solution.py:435
  145.1 3.5 %shard_map.131 = f32[1792,512]{1,0:T(8,128)} custom-call(bf16[3584,512]{1,0:T(8,128)(2,1)S(1)} %shard_map.128.near_ref, bf16[3584,512]{1,0:T(8,128)(2,1)S(1)} %shard_map.130.far_ref.refs_1_, bf16[512,512]{1,0:T(8,128)(2,1)S(1)} %get-tuple-element.30.gg_ref.here_ref, bf16[512,512]{1,0:T(8,128)(2,1)S(1)} %collective-permute-done.5.there_ref), custom_call_target="tpu_custom_call" | custom-call | flops 1879048192 | bytes 8388608 | tf_op jit(solution)/shard_map/pallas_call | solution.py:322
  148.6 7.8 %collective-permute-done.7.there_ref = bf16[512,512]{1,0:T(8,128)(2,1)S(1)} collective-permute-done((bf16[512,512]{1,0:T(8,128)(2,1)S(1)}, bf16[512,512]{1,0:T(8,128)(2,1)S(1)}, u32[]{:S(2)}, u32[]{:S(2)}) %collective-permute-start.7) | collective-permute-done | bytes 524320 | tf_op jit(solution)/shard_map/ppermute | solution.py:435
  156.3 3.5 %shard_map.134 = f32[1792,512]{1,0:T(8,128)} custom-call(bf16[3584,512]{1,0:T(8,128)(2,1)S(1)} %shard_map.128.near_ref, bf16[3584,512]{1,0:T(8,128)(2,1)S(1)} %shard_map.130.far_ref.refs_1_, bf16[512,512]{1,0:T(8,128)(2,1)S(1)} %get-tuple-element.29.hid_ref.refs_0_.here_ref, bf16[512,512]{1,0:T(8,128)(2,1)S(1)} %collective-permute-done.7.there_ref), custom_call_target="tpu_custom_call" | custom-call | flops 1879048192 | bytes 8388608 | tf_op jit(solution)/shard_map/pallas_call | solution.py:322
  159.8 3.1 %shard_map.127 = (bf16[32,3584]{1,0:T(8,128)(2,1)}, bf16[32,3584]{1,0:T(8,128)(2,1)}) custom-call(bf16[256,7168]{1,0:T(8,128)(2,1)} %bitcast.8.refs_0_, bf16[256,32]{1,0:T(8,128)(2,1)S(1)} %get-tuple-element.32.refs_1_, bf16[256,96]{1,0:T(8,128)(2,1)S(1)} %get-tuple-element.33.refs_2_), custom_call_target="tpu_custom_call" | custom-call | flops 234881024 | bytes 4194304 | tf_op jit(solution)/shard_map/pallas_call | solution.py:54
  (11 shorter events, 0.0 us)
Async XLA Ops:
  61.2 6.3 %copy-start = (bf16[32,8,7168]{2,1,0:T(8,128)(2,1)}, bf16[32,8,7168]{2,1,0:T(8,128)(2,1)S(1)}, u32[]{:S(2)}) copy-start(bf16[32,8,7168]{2,1,0:T(8,128)(2,1)S(1)} %all_to_all.10) | copy-start | bytes 11010052
  61.2 7.8 %collective-permute-start = (bf16[256,7168]{1,0:T(8,128)(2,1)S(1)}, bf16[256,7168]{1,0:T(8,128)(2,1)S(1)}, u32[]{:S(2)}, u32[]{:S(2)}) collective-permute-start(bf16[256,7168]{1,0:T(8,128)(2,1)S(1)} %bitcast.12), channel_id=1, source_target_pairs={{0,1},{1,0},{2,3},{3,2},{4,5},{5,4},{6,7},{7,6},{8,9},{9,8},{10,11... | collective-permute-start | bytes 11010056 | tf_op jit(solution)/shard_map/ppermute | solution.py:432
  69.1 3.1 %copy-start.2 = (bf16[256,7168]{1,0:T(8,128)(2,1)}, bf16[256,7168]{1,0:T(8,128)(2,1)S(1)}, u32[]{:S(2)}) copy-start(bf16[256,7168]{1,0:T(8,128)(2,1)S(1)} %collective-permute-done.rows_ref.second_ref) | copy-start | bytes 11010052
  73.3 6.6 %collective-permute-start.1 = (bf16[256,3584]{1,0:T(8,128)(2,1)S(1)}, bf16[256,3584]{1,0:T(8,128)(2,1)S(1)}, u32[]{:S(2)}, u32[]{:S(2)}) collective-permute-start(bf16[256,3584]{1,0:T(8,128)(2,1)S(1)} %shard_map.122), channel_id=1, source_target_pairs={{0,1},{1,0},{2,3},{3,2},{4,5},{5,4},{6,7},{7,6},{8,9},{9,8},{10,11... | collective-permute-start | bytes 5505032 | tf_op jit(solution)/shard_map/ppermute | solution.py:432
  75.9 6.3 %collective-permute-start.2 = (bf16[256,3584]{1,0:T(8,128)(2,1)S(1)}, bf16[256,3584]{1,0:T(8,128)(2,1)S(1)}, u32[]{:S(2)}, u32[]{:S(2)}) collective-permute-start(bf16[256,3584]{1,0:T(8,128)(2,1)S(1)} %shard_map.125), channel_id=1, source_target_pairs={{0,1},{1,0},{2,3},{3,2},{4,5},{5,4},{6,7},{7,6},{8,9},{9,8},{10,11... | collective-permute-start | bytes 5505032 | tf_op jit(solution)/shard_map/ppermute | solution.py:432
  77.6 41.6 %collective-permute-start.3 = (bf16[256,3584]{1,0:T(8,128)(2,1)S(1)}, bf16[256,3584]{1,0:T(8,128)(2,1)}, u32[]{:S(2)}, u32[]{:S(2)}) collective-permute-start(bf16[256,3584]{1,0:T(8,128)(2,1)S(1)} %shard_map.129), channel_id=1, source_target_pairs={{0,64},{1,65},{2,66},{3,67},{4,68},{5,69},{6,70},{7,71},{8,72},{9,... | collective-permute-start | bytes 5505032 | tf_op jit(solution)/shard_map/ppermute | solution.py:435
  83.6 76.2 %all-to-all-start.1 = ((bf16[32,8,7168]{2,1,0:T(8,128)(2,1)}), bf16[32,8,7168]{2,1,0:T(8,128)(2,1)}, u32[]{:S(2)}, u32[]{:S(2)}) async-start(bf16[32,8,7168]{2,1,0:T(8,128)(2,1)} %bitcast.16), calls=%async_computation.1 | async-start | bytes 7340032 | tf_op jit(solution)/shard_map/all_to_all | solution.py:31
  119.1 9.5 %collective-permute-start.4 = (bf16[256,3584]{1,0:T(8,128)(2,1)}, bf16[256,3584]{1,0:T(8,128)(2,1)S(1)}, u32[]{:S(2)}, u32[]{:S(2)}) collective-permute-start(bf16[256,3584]{1,0:T(8,128)(2,1)} %collective-permute-done.3.first_ref), channel_id=1, source_target_pairs={{0,1},{1,0},{2,3},{3,2},{4,5},{5,4},{6,7},{7,6},{8,9},{9,8},{10,11... | collective-permute-start | bytes 5505032 | tf_op jit(solution)/shard_map/ppermute | solution.py:432
  120.4 16.8 %collective-permute-start.6 = (bf16[512,512]{1,0:T(8,128)(2,1)S(1)}, bf16[512,512]{1,0:T(8,128)(2,1)S(1)}, u32[]{:S(2)}, u32[]{:S(2)}) collective-permute-start(bf16[512,512]{1,0:T(8,128)(2,1)S(1)} %get-tuple-element.31.ug_ref.here_ref), channel_id=1, source_target_pairs={{0,64},{1,65},{2,66},{3,67},{4,68},{5,69},{6,70},{7,71},{8,72},{9,... | collective-permute-start | bytes 1572872 | tf_op jit(solution)/shard_map/ppermute | solution.py:435
  120.4 24.7 %collective-permute-start.5 = (bf16[512,512]{1,0:T(8,128)(2,1)S(1)}, bf16[512,512]{1,0:T(8,128)(2,1)S(1)}, u32[]{:S(2)}, u32[]{:S(2)}) collective-permute-start(bf16[512,512]{1,0:T(8,128)(2,1)S(1)} %get-tuple-element.30.gg_ref.here_ref), channel_id=1, source_target_pairs={{0,64},{1,65},{2,66},{3,67},{4,68},{5,69},{6,70},{7,71},{8,72},{9,... | collective-permute-start | bytes 1572872 | tf_op jit(solution)/shard_map/ppermute | solution.py:435
  121.9 34.5 %collective-permute-start.7 = (bf16[512,512]{1,0:T(8,128)(2,1)S(1)}, bf16[512,512]{1,0:T(8,128)(2,1)S(1)}, u32[]{:S(2)}, u32[]{:S(2)}) collective-permute-start(bf16[512,512]{1,0:T(8,128)(2,1)S(1)} %get-tuple-element.29.hid_ref.refs_0_.here_ref), channel_id=1, source_target_pairs={{0,64},{1,65},{2,66},{3,67},{4,68},{5,69},{6,70},{7,71},{8,72},{9,... | collective-permute-start | bytes 1572872 | tf_op jit(solution)/shard_map/ppermute | solution.py:435
  121.9 2.0 %copy-start.1 = (bf16[32,8,7168]{2,1,0:T(8,128)(2,1)S(1)}, bf16[32,8,7168]{2,1,0:T(8,128)(2,1)}, u32[]{:S(2)}) copy-start(bf16[32,8,7168]{2,1,0:T(8,128)(2,1)} %copy-done) | copy-start | bytes 11010052
  123.9 2.0 %copy-start.3 = (bf16[256,7168]{1,0:T(8,128)(2,1)S(1)}, bf16[256,7168]{1,0:T(8,128)(2,1)}, u32[]{:S(2)}) copy-start(bf16[256,7168]{1,0:T(8,128)(2,1)} %copy-done.2) | copy-start | bytes 11010052
